TPU v7x, 256 devices: a whole 4x4x8 slice. The times are simulated.
256 devices in a mesh: head: 8 (over x_hi, y), key: 8 (over z), hid: 4 (over x_lo, core).
Axes of the slice: x: 4 (x_hi: 2, x_lo: 2; x = x_hi * 2 + x_lo), y: 4, z: 8, core: 2. Of those that a mesh axis runs over, the one named last changes fastest.
Arguments:
- tokens: bfloat16 [2048, 8192], P('key', 'hid'), may hold values from -6 to 6
- query_weight: bfloat16 [8192, 8192], P('hid', 'head'), may hold values from -0.0625 to 0.0625
- key_weight: bfloat16 [8192, 1024], P('hid', 'head'), may hold values from -0.0625 to 0.0625
- value_weight: bfloat16 [8192, 1024], P('hid', 'head'), may hold values from -0.0625 to 0.0625
- output_weight: bfloat16 [8192, 8192], P(('head', 'hid')), may hold values from -0.125 to 0.125
- key_cache: bfloat16 [16384, 8, 128], P('key', 'head'), may hold values from -2000 to 2000
- value_cache: bfloat16 [16384, 8, 128], P('key', 'head'), may hold values from -6 to 6
- cache_places: int32 [64], P('key'), may hold values from 1 to 510, as said below
- slab_places: int32 [8], replicated, may hold values from 0 to 511, as said below
Outputs:
- attended: bfloat16 [2048, 8192], P('key', ('head', 'hid'))
Inputs may be any that keep to these rules, and one draw needn't show every extreme that they name: The 64 entries of cache_places and the 8 entries of slab_places are all different from one another. `slab_places`: see cache_places: no slab shares a block number with another slab or with a resident block.
All inputs are finite; a program needn't handle non-finite values.
Results may differ from a plain program's by a relative error of at most 0.039.
Values may be sent and summed in bfloat16 or wider, within the bound.
No kernel may reach another device: no remote copies, remote signals or barrier semaphores. Data moves between devices by JAX's collectives and lax.ppermute only.
A program may use at most 128 MiB of HBM per device.

v0:
```python
import math

import jax
import jax.numpy as jnp
from jax import lax
from jax.sharding import Mesh
from jax.sharding import PartitionSpec as P

H = 64
KVH = 8
HID = ("hid_0", "hid_1")
HEAD = ("head_0", "head_1")
HEAD_HID = ("head_0", "head_1", "hid_0", "hid_1")


THETA = 500000.0
NEGATIVE = -1e30


def in_blocks(shard, dim, length):
    before, after = (shard.shape[:dim], shard.shape[dim + 1 :])
    return jnp.moveaxis(shard.reshape(*before, length, -1, *after), dim, 0)


def summed_on_arrival(shard, axis, dim):
    parts = in_blocks(shard, dim, lax.axis_size(axis))
    arrived = lax.all_to_all(parts, axis, split_axis=0, concat_axis=0, tiled=True)
    return arrived.sum(axis=0)


def sent_to_all(shard, axis):
    copies = jnp.broadcast_to(shard, (lax.axis_size(axis), *shard.shape))
    return lax.all_to_all(copies, axis, split_axis=0, concat_axis=0, tiled=True)


def of_everyone(shard, axis):
    everything = sent_to_all(shard, axis)
    return jnp.sum(everything, axis=0)


def together(arrays, axis):
    ends = [0]
    for a in arrays:
        ends.append(ends[-1] + a.size)
    so_far = of_everyone(jnp.concatenate([a.ravel() for a in arrays]), axis)
    return tuple((so_far[b:e].reshape(a.shape) for a, b, e in zip(arrays, ends, ends[1:])))


def laid_out(parts, dim):
    parts = jnp.moveaxis(parts, 0, dim)
    lengths = parts.shape
    return parts.reshape(*lengths[:dim], lengths[dim] * lengths[dim + 1], *lengths[dim + 2 :])


def gathered_copies(shard, axis, dim):
    parts = sent_to_all(shard, axis)
    return laid_out(parts, dim)


def summed_rows(shard, axes, dim):
    far, near = axes
    own = summed_on_arrival(in_blocks(shard, dim, lax.axis_size(far)), near, dim + 1)
    return jnp.sum(lax.all_to_all(own, far, 0, 0, tiled=True), axis=0)


def rotate(vectors, spots):
    middle = vectors.shape[-1] // 2
    freq_index = jnp.arange(middle, dtype=jnp.float32)
    frequency = jnp.exp(freq_index * (-2.0 * math.log(THETA) / vectors.shape[-1]))
    angles = spots.astype(jnp.float32)[:, None] * frequency[None, :]
    cosine_part = jnp.cos(angles)[:, None, :]
    sine_part = jnp.sin(angles)[:, None, :]
    leading = vectors[..., :middle]
    trailing = vectors[..., middle:]
    return jnp.concatenate(
        [
            leading * cosine_part - trailing * sine_part,
            trailing * cosine_part + leading * sine_part,
        ],
        axis=-1,
    )


def body(
    tokens,
    query_weight,
    key_weight,
    value_weight,
    output_weight,
    key_cache,
    value_cache,
    cache_places,
    slab_places,
):
    slab_rows = tokens.shape[0]
    head_width = key_cache.shape[2]
    local_groups = key_cache.shape[1]
    key_devices = lax.axis_size("key")
    slab_index = lax.axis_index("key")
    offsets = jnp.arange(slab_rows, dtype=jnp.int32)
    slab_table = jnp.arange(key_devices, dtype=jnp.int32)
    own_first = jnp.sum(jnp.where(slab_table == slab_index, slab_places, 0)) * slab_rows
    own_spots = own_first + offsets
    cache_spots = (cache_places[:, None] * slab_rows + offsets[None, :]).reshape(-1)
    query_part = jnp.dot(tokens, query_weight, preferred_element_type=jnp.float32)
    query_slab = summed_on_arrival(query_part, HID, 1)
    key_part = jnp.dot(tokens, key_weight, preferred_element_type=jnp.float32)
    value_part = jnp.dot(tokens, value_weight, preferred_element_type=jnp.float32)
    key_fresh, value_fresh = together((key_part, value_part), HID)
    local_heads = query_slab.shape[1] // head_width
    queries = rotate(query_slab.reshape(slab_rows, local_heads, head_width), own_spots).astype(
        jnp.bfloat16
    )
    queries = queries.reshape(slab_rows, local_heads * head_width)
    keys_new = rotate(key_fresh.reshape(slab_rows, local_groups, head_width), own_spots).astype(
        jnp.bfloat16
    )
    values_new = value_fresh.reshape(slab_rows, local_groups, head_width).astype(jnp.bfloat16)
    group_heads = H // KVH
    used_groups = max(1, local_heads // group_heads)
    per_group = local_heads // used_groups
    key_rows = jnp.concatenate([key_cache, keys_new], axis=0)
    value_rows = jnp.concatenate([value_cache, values_new], axis=0)
    key_spots = jnp.concatenate([cache_spots, own_spots], axis=0)
    score_scale = 1.0 / math.sqrt(head_width)
    query_piece = gathered_copies(queries, "key", 0)
    height = query_piece.shape[0]
    global_rows = jnp.arange(height, dtype=jnp.int32)
    owners = global_rows // slab_rows
    slab_starts = jnp.sum(
        jnp.where(owners[:, None] == slab_table[None, :], slab_places[None, :], 0), axis=1
    )
    query_spots = slab_starts * slab_rows + global_rows % slab_rows
    grouped = query_piece.reshape(height, used_groups, per_group, head_width)
    scores = (
        jnp.einsum("rkgd,ckd->rkgc", grouped, key_rows, preferred_element_type=jnp.float32)
        * score_scale
    )
    visible = key_spots[None, None, None, :] <= query_spots[:, None, None, None]
    peaks = jnp.max(jnp.where(visible, scores, NEGATIVE), axis=-1)
    weights = jnp.where(visible, jnp.exp(scores - peaks[..., None]), 0.0)
    totals = jnp.sum(weights, axis=-1)
    summed = jnp.einsum(
        "rkgc,ckd->rkgd",
        weights.astype(jnp.bfloat16),
        value_rows,
        preferred_element_type=jnp.float32,
    )
    partial_value, maxima, totals = (summed, peaks, totals)
    partial_value, maxima, totals = (
        lax.all_to_all(partial_value, "key", split_axis=0, concat_axis=0, tiled=True),
        lax.all_to_all(maxima, "key", split_axis=0, concat_axis=0, tiled=True),
        lax.all_to_all(totals, "key", split_axis=0, concat_axis=0, tiled=True),
    )
    partial_value = partial_value.reshape(
        key_devices, slab_rows, used_groups, per_group, head_width
    )
    maxima = maxima.reshape(key_devices, slab_rows, used_groups, per_group)
    totals = totals.reshape(key_devices, slab_rows, used_groups, per_group)
    highest = jnp.max(maxima, axis=0)
    factor = jnp.exp(maxima - highest[None])
    partial_value = jnp.sum(partial_value * factor[..., None], axis=0)
    totals = jnp.sum(totals * factor, axis=0)
    heads_out = (
        (partial_value / totals[..., None])
        .astype(jnp.bfloat16)
        .reshape(slab_rows, local_heads * head_width)
    )
    partial_out = jnp.dot(heads_out, output_weight, preferred_element_type=jnp.float32)
    attended = summed_rows(partial_out, (("head_0", "head_1", "hid_0"), "hid_1"), 1)
    return attended.astype(jnp.bfloat16)


def solution(mesh):
    finer = Mesh(
        mesh.devices.reshape(2, 4, mesh.shape["key"], 2, 2),
        ("head_0", "head_1", "key", "hid_0", "hid_1"),
    )
    return jax.shard_map(
        body,
        mesh=finer,
        in_specs=(
            P("key", HID),
            P(HID, HEAD),
            P(HID, HEAD),
            P(HID, HEAD),
            P(HEAD_HID, None),
            P("key", HEAD, None),
            P("key", HEAD, None),
            P("key"),
            P(),
        ),
        out_specs=P("key", HEAD_HID),
        check_vma=False,
    )
```

profile of v0, /device:TPU:1, one launch (start us, length us, event | category | flops | bytes accessed | tf_op | source)
XLA Modules:
  0.0 298.5 jit_solution(6182558006311619307)
XLA Ops:
  0.0 1.2 copy-done
  1.2 3.4 %fusion.42 = f32[256,1024]{1,0:T(8,128)S(1)} fusion(bf16[256,2048]{1,0:T(8,128)(2,1)S(1)} %copy-done, bf16[2048,1024]{1,0:T(8,128)(2,1)} %param.10), kind=kOutput, calls=%fused_computation.76 | convolution fusion | flops 1073741824 | bytes 6291456 | tf_op jit(solution)/shard_map/dot_general | solution.py:105
  4.7 1.1 copy.154
  5.7 6.7 %all-to-all-start.1 = ((f32[4,256,256]{2,1,0:T(8,128)}), f32[4,256,256]{2,1,0:T(8,128)S(1)}, u32[]{:S(2)}, u32[]{:S(2)}) async-start(f32[4,256,256]{2,1,0:T(8,128)} %bitcast.91), calls=%async_computation.1 | async-start | bytes 2097152 | tf_op jit(solution)/shard_map/all_to_all | solution.py:27
  12.5 0.6 fusion.35
  14.8 2.1 copy.116
  16.9 9.1 %all-to-all-done.1 = f32[4,256,256]{2,1,0:T(8,128)S(1)} async-done(((f32[4,256,256]{2,1,0:T(8,128)}), f32[4,256,256]{2,1,0:T(8,128)S(1)}, u32[]{:S(2)}, u32[]{:S(2)}) %all-to-all-start.1) | async-done | bytes 1048608 | tf_op jit(solution)/shard_map/all_to_all | solution.py:27
  26.1 1.5 broadcast_in_dim.38
  27.6 4.4 %all-to-all-start = ((f32[4,1,65536]{2,1,0:T(1,128)}), f32[4,1,65536]{2,1,0:T(1,128)S(1)}, u32[]{:S(2)}, u32[]{:S(2)}) async-start(f32[4,1,65536]{2,1,0:T(1,128)} %broadcast_in_dim.38), calls=%async_computation | async-start | bytes 2097152 | tf_op jit(solution)/shard_map/all_to_all | solution.py:33
  31.9 0.5 multiply_cosine_fusion
  32.7 0.5 subtract_convert_fusion
  33.7 11.9 %all-to-all-done = f32[4,1,65536]{2,1,0:T(1,128)S(1)} async-done(((f32[4,1,65536]{2,1,0:T(1,128)}), f32[4,1,65536]{2,1,0:T(1,128)S(1)}, u32[]{:S(2)}, u32[]{:S(2)}) %all-to-all-start) | async-done | bytes 1048608 | tf_op jit(solution)/shard_map/all_to_all | solution.py:33
  45.5 1.1 broadcast_in_dim.64
  46.6 6.4 %all-to-all-start.2 = ((bf16[8,256,256]{1,2,0:T(8,128)(2,1)}), bf16[8,256,256]{1,2,0:T(8,128)(2,1)S(1)}, u32[]{:S(2)}, u32[]{:S(2)}) async-start(bf16[8,256,256]{1,2,0:T(8,128)(2,1)} %broadcast_in_dim.64), calls=%async_computation.2 | async-start | bytes 2097152 | tf_op jit(solution)/shard_map/all_to_all | solution.py:33
  53.0 4.9 %broadcast_compare_fusion = pred[2048,2304]{0,1:T(8,128)(4,1)} fusion(s32[2048]{0:T(1024)S(1)} %fusion.33, s32[2304]{0:T(1024)S(1)} %pad_add_fusion), kind=kLoop, calls=%fused_computation.10 | loop fusion | flops 4718592 | bytes 4736000 | tf_op jit(solution)/shard_map/le | solution.py:139
  57.9 1.0 reduce_sum.83
  59.6 22.6 %all-to-all-done.2 = bf16[8,256,256]{1,2,0:T(8,128)(2,1)S(1)} async-done(((bf16[8,256,256]{1,2,0:T(8,128)(2,1)}), bf16[8,256,256]{1,2,0:T(8,128)(2,1)S(1)}, u32[]{:S(2)}, u32[]{:S(2)}) %all-to-all-start.2) | async-done | bytes 1048608 | tf_op jit(solution)/shard_map/all_to_all | solution.py:33
  82.2 0.6 copy.124
  82.8 0.5 reshape.365
  83.4 17.8 %fusion = (f32[2048,2]{0,1:T(2,128)S(1)}, f32[2304,2048,2]{1,0,2:T(8,128)}) fusion(pred[2048,2304]{0,1:T(8,128)(4,1)} %broadcast_compare_fusion, bf16[2048,2,128]{0,2,1:T(8,128)(2,1)S(1)} %reshape.365, bf16[256,1,128]{2,0,1:T(8,128)(2,1)S(1)} %copy.120, bf16[2048,1,128]{2,0,1:T(8,128)(2,1)} %param.14), kind=kOutput, calls=%fused_computation.2 | convolution fusion | flops 2445406208 | bytes 44122112 | tf_op jit(solution)/shard_map/rkgd,ckd->rkgc/dot_general | solution.py:136
  101.2 16.8 %fusion.3 = f32[2048,2]{0,1:T(2,128)S(1)} fusion(f32[2304,2048,2]{1,0,2:T(8,128)} %get-tuple-element.14, f32[2048,2]{0,1:T(2,128)S(1)} %get-tuple-element.13, pred[2048,2304]{0,1:T(8,128)(4,1)} %broadcast_compare_fusion), kind=kLoop, calls=%fused_computation.5 | loop fusion | flops 37744640 | bytes 42500096 | tf_op jit(solution)/shard_map/reduce_sum | solution.py:142
  118.0 0.6 broadcast.215
  118.6 0.7 reduce.8
  119.7 1.2 reshape.377
  120.9 3.5 %all-to-all-start.5 = ((f32[8,1,512]{2,1,0:T(1,128)}), f32[8,1,512]{2,1,0:T(1,128)S(1)}, u32[]{:S(2)}, u32[]{:S(2)}) async-start(f32[8,1,512]{2,1,0:T(1,128)} %reshape.377), calls=%async_computation.5 | async-start | bytes 32768 | tf_op jit(solution)/shard_map/all_to_all | solution.py:153
  124.6 0.7 reduce.6
  125.7 1.2 reshape.375
  126.9 4.0 %all-to-all-done.5 = f32[8,1,512]{2,1,0:T(1,128)S(1)} async-done(((f32[8,1,512]{2,1,0:T(1,128)}), f32[8,1,512]{2,1,0:T(1,128)S(1)}, u32[]{:S(2)}, u32[]{:S(2)}) %all-to-all-start.5) | async-done | bytes 16416 | tf_op jit(solution)/shard_map/all_to_all | solution.py:153
  130.9 3.3 %all-to-all-start.4 = ((f32[8,1,512]{2,1,0:T(1,128)}), f32[8,1,512]{2,1,0:T(1,128)S(1)}, u32[]{:S(2)}, u32[]{:S(2)}) async-start(f32[8,1,512]{2,1,0:T(1,128)} %reshape.375), calls=%async_computation.4 | async-start | bytes 32768 | tf_op jit(solution)/shard_map/all_to_all | solution.py:152
  134.2 16.5 %fusion.9 = f32[2048,1,2,128]{0,3,2,1:T(8,128)S(1)} fusion(f32[2304,2048,2]{1,0,2:T(8,128)} %get-tuple-element.14, f32[2048,2]{0,1:T(2,128)S(1)} %get-tuple-element.13, pred[2048,2304]{0,1:T(8,128)(4,1)} %broadcast_compare_fusion, bf16[256,1,128]{0,2,1:T(8,128)(2,1)S(1)} %copy.117, bf16[2048,1,128]{0,2,1:T(8,128)(2,1)} %copy.116), kind=kOutput, calls=%fused_computation.14 | convolution fusion | flops 2454847488 | bytes 45170688 | tf_op jit(solution)/shard_map/rkgc,ckd->rkgd/dot_general | solution.py:143
  150.7 2.4 copy.127
  153.1 6.5 %all-to-all-start.3 = ((f32[2048,1,2,128]{3,2,1,0:T(2,128)}), f32[2048,1,2,128]{3,2,1,0:T(2,128)S(1)}, u32[]{:S(2)}, u32[]{:S(2)}) async-start(f32[2048,1,2,128]{3,2,1,0:T(2,128)} %copy.127), calls=%async_computation.3 | async-start | bytes 4194304 | tf_op jit(solution)/shard_map/all_to_all | solution.py:151
  159.6 6.4 %copy.143 = bf16[8192,256]{1,0:T(8,128)(2,1)} copy(bf16[8192,256]{0,1:T(8,128)(2,1)} %bitcast.101) | data formatting | bytes 8388608 | tf_op jit(solution)/shard_map/dot_general | solution.py:169
  166.0 0.7 reduce.9
  166.7 1.7 reshape.378
  168.8 0.7 reduce.7
  169.5 1.7 reshape.376
  171.7 1.2 fusion.12
  172.9 1.5 copy.129
  174.5 36.8 %all-to-all-done.3 = f32[2048,1,2,128]{3,2,1,0:T(2,128)S(1)} async-done(((f32[2048,1,2,128]{3,2,1,0:T(2,128)}), f32[2048,1,2,128]{3,2,1,0:T(2,128)S(1)}, u32[]{:S(2)}, u32[]{:S(2)}) %all-to-all-start.3) | async-done | bytes 2097184 | tf_op jit(solution)/shard_map/all_to_all | solution.py:151
  211.3 1.9 copy.130
  213.1 2.2 multiply_reduce_fusion
  215.4 3.5 %fusion.43 = f32[256,16,512]{2,0,1:T(8,128)S(1)} fusion(bf16[256,256,1]{0,1,2:T(8,128)(2,1)S(1)} %bitcast.104, bf16[16,512,256]{2,1,0:T(8,128)(2,1)} %bitcast.96), kind=kOutput, calls=%fused_computation.77 | convolution fusion | flops 1073741824 | bytes 12713984 | tf_op jit(solution)/shard_map/dot_general | solution.py:169
  218.9 1.2 copy.153
  220.1 11.9 %all_to_all.41 = f32[2,16,256,256]{3,2,1,0:T(8,128)} all-to-all(f32[2,16,256,256]{3,2,1,0:T(8,128)S(1)} %bitcast.95), channel_id=1, replica_groups=mesh['head_0'=2,'head_1'=4,'key'=8,'hid_0'=2,'hid_1'=2] {'hid_1'}, dimensions={0} | all-to-all | bytes 16777216 | tf_op jit(solution)/shard_map/all_to_all | solution.py:27
  232.0 6.5 %reduce_sum.91 = f32[16,256,256]{2,1,0:T(8,128)} reduce(f32[2,16,256,256]{3,2,1,0:T(8,128)} %all_to_all.41, f32[]{:T(128)} %constant.37.clone.1), dimensions={0}, to_apply=%region_9.10 | reduce | flops 1048576 | bytes 12582916 | tf_op jit(solution)/shard_map/reduce_sum | solution.py:28
  238.5 56.9 %all_to_all.42 = f32[16,256,256]{2,1,0:T(8,128)} all-to-all(f32[16,256,256]{2,1,0:T(8,128)} %reduce_sum.91), channel_id=1, replica_groups=mesh['head_0'=2,'head_1'=4,'key'=8,'hid_0'=2,'hid_1'=2] {'head_0','head_..., dimensions={0} | all-to-all | bytes 8388608 | tf_op jit(solution)/shard_map/all_to_all | solution.py:63
  295.4 3.1 %reduce_sum.92 = bf16[256,256]{1,0:T(8,128)(2,1)} reduce(f32[16,256,256]{2,1,0:T(8,128)} %all_to_all.42, f32[]{:T(128)} %constant.37.clone.1), dimensions={0}, to_apply=%region_10.11 | reduce | flops 983040 | bytes 4325380 | tf_op jit(solution)/shard_map/reduce_sum | solution.py:63
  (45 shorter events, 4.2 us)
Async XLA Ops:
  0.0 1.2 copy-start
  0.0 12.5 %copy-start.4 = (s32[8]{0:T(128)S(1)}, s32[8]{0:T(128)}, u32[]{:S(2)}) copy-start(s32[8]{0:T(128)} %param.17) | copy-start | bytes 100
  0.0 13.8 %copy-start.2 = (bf16[2048,128]{1,0:T(8,128)(2,1)S(1)}, bf16[2048,128]{1,0:T(8,128)(2,1)}, u32[]{:S(2)}) copy-start(bf16[2048,128]{1,0:T(8,128)(2,1)} %param.12) | copy-start | bytes 1572868
  0.0 14.2 %copy-start.3 = (bf16[2048,128]{1,0:T(8,128)(2,1)S(1)}, bf16[2048,128]{1,0:T(8,128)(2,1)}, u32[]{:S(2)}) copy-start(bf16[2048,128]{1,0:T(8,128)(2,1)} %param.11) | copy-start | bytes 1572868
  0.0 14.6 %copy-start.5 = (s32[8]{0:T(128)S(1)}, s32[8]{0:T(128)}, u32[]{:S(2)}) copy-start(s32[8]{0:T(128)} %param.16) | copy-start | bytes 100
  5.7 20.3 %all-to-all-start.1 = ((f32[4,256,256]{2,1,0:T(8,128)}), f32[4,256,256]{2,1,0:T(8,128)S(1)}, u32[]{:S(2)}, u32[]{:S(2)}) async-start(f32[4,256,256]{2,1,0:T(8,128)} %bitcast.91), calls=%async_computation.1 | async-start | bytes 2097152 | tf_op jit(solution)/shard_map/all_to_all | solution.py:27
  27.6 18.0 %all-to-all-start = ((f32[4,1,65536]{2,1,0:T(1,128)}), f32[4,1,65536]{2,1,0:T(1,128)S(1)}, u32[]{:S(2)}, u32[]{:S(2)}) async-start(f32[4,1,65536]{2,1,0:T(1,128)} %broadcast_in_dim.38), calls=%async_computation | async-start | bytes 2097152 | tf_op jit(solution)/shard_map/all_to_all | solution.py:33
  46.6 35.6 %all-to-all-start.2 = ((bf16[8,256,256]{1,2,0:T(8,128)(2,1)}), bf16[8,256,256]{1,2,0:T(8,128)(2,1)S(1)}, u32[]{:S(2)}, u32[]{:S(2)}) async-start(bf16[8,256,256]{1,2,0:T(8,128)(2,1)} %broadcast_in_dim.64), calls=%async_computation.2 | async-start | bytes 2097152 | tf_op jit(solution)/shard_map/all_to_all | solution.py:33
  120.9 10.0 %all-to-all-start.5 = ((f32[8,1,512]{2,1,0:T(1,128)}), f32[8,1,512]{2,1,0:T(1,128)S(1)}, u32[]{:S(2)}, u32[]{:S(2)}) async-start(f32[8,1,512]{2,1,0:T(1,128)} %reshape.377), calls=%async_computation.5 | async-start | bytes 32768 | tf_op jit(solution)/shard_map/all_to_all | solution.py:153
  130.9 22.2 %all-to-all-start.4 = ((f32[8,1,512]{2,1,0:T(1,128)}), f32[8,1,512]{2,1,0:T(1,128)S(1)}, u32[]{:S(2)}, u32[]{:S(2)}) async-start(f32[8,1,512]{2,1,0:T(1,128)} %reshape.375), calls=%async_computation.4 | async-start | bytes 32768 | tf_op jit(solution)/shard_map/all_to_all | solution.py:152
  153.1 58.2 %all-to-all-start.3 = ((f32[2048,1,2,128]{3,2,1,0:T(2,128)}), f32[2048,1,2,128]{3,2,1,0:T(2,128)S(1)}, u32[]{:S(2)}, u32[]{:S(2)}) async-start(f32[2048,1,2,128]{3,2,1,0:T(2,128)} %copy.127), calls=%async_computation.3 | async-start | bytes 4194304 | tf_op jit(solution)/shard_map/all_to_all | solution.py:151
  232.0 66.6 %copy-start.1 = (bf16[256,2048]{1,0:T(8,128)(2,1)S(1)}, bf16[256,2048]{1,0:T(8,128)(2,1)}, u32[]{:S(2)}) copy-start(bf16[256,2048]{1,0:T(8,128)(2,1)} %param.9) | copy-start | bytes 3145732
where the time goes:
time: 300 us; the launch traced here: 299 us
  waiting for transfers between devices  84.4 us (28%)
  blocking collectives  68.8 us (23%)
  matrix products  42 us (14%)
  other arithmetic  41.3 us (14%)
  starting transfers between devices  31 us (10%)
  local copies, waits for them, and re-layouts  30.1 us (10%)
    all_to_all x1, blocking collectives, summed_rows(): return jnp.sum(lax.all_to_all(own, far, 0, 0, tiled=True), axis=0)  56.9 us
    all_to_all x1, waiting for transfers between devices, body(): lax.all_to_all(partial_value, 'key', split_axis=0, concat_axis=0, tiled=T...  36.8 us
    all_to_all x2, waiting for transfers between devices, sent_to_all(): return lax.all_to_all(copies, axis, split_axis=0, concat_axis=0, tiled=True)  34.5 us
    dot_general x1, matrix products, body(): jnp.einsum('rkgd,ckd->rkgc', grouped, key_rows, preferred_element_type=jn...  17.8 us
    reduce_sum x2, other arithmetic, body(): totals = jnp.sum(weights, axis=-1)  17.5 us
    dot_general x1, matrix products, body(): jnp.einsum('rkgc,ckd->rkgd', weights.astype(jnp.bfloat16), value_rows, pr...  16.5 us
    all_to_all x1, blocking collectives, summed_on_arrival(): lax.all_to_all(parts, axis, split_axis=0, concat_axis=0, tiled=True)  11.9 us
    all_to_all x2, starting transfers between devices, sent_to_all(): return lax.all_to_all(copies, axis, split_axis=0, concat_axis=0, tiled=True)  10.8 us
  transfers between devices with their start and end apart: 6, of which 5 were waited for; matrix products, arithmetic and copies ran while one was open for 16% of the time, Pallas kernels for 0%

commit v1 on v0

v1 whole, which is shorter than its diff:
```python
import functools
import math

import jax
import jax.numpy as jnp
import numpy as np
from jax import lax
from jax.experimental import pallas as pl
from jax.experimental.pallas import tpu as pltpu
from jax.sharding import Mesh
from jax.sharding import PartitionSpec as P

HID = ("hid_0", "hid_1")
HEAD = ("head_0", "head_1")
HEAD_HID = ("head_0", "head_1", "hid_0", "hid_1")
ALONG_X = ("head_0", "hid_0")

THETA = 500000.0
NEGATIVE = -1e30
BF16 = jnp.bfloat16
F32 = jnp.float32

ROWS = 256
HD = 128
PAIR = 2 * HD
NEW = 64
QUARTER = 512
LOAD = QUARTER + 16
MSG = ROWS + 16
TALL = 1024
EXPONENT = math.log2(math.e) / math.sqrt(HD)
CONTRACT = (((1,), (1,)), ((), ()))

VMEM = pl.BlockSpec(memory_space=pltpu.VMEM)
SMEM = pl.BlockSpec(memory_space=pltpu.SMEM)
ANY = pl.BlockSpec(memory_space=pl.ANY)


def shaped(shape, dtype):
    return jax.ShapeDtypeStruct(shape, dtype)


def params(mib):
    return pltpu.CompilerParams(vmem_limit_bytes=mib * 2**20)


def cost(flops=0, moved=0, exps=0):
    return pl.CostEstimate(flops=flops, bytes_accessed=moved, transcendentals=exps)


def shift(n, by):
    return [(i, (i + by) % n) for i in range(n)]


def swap(array, axis):
    return lax.ppermute(array, axis, shift(2, 1))


def hid_index():
    return 2 * lax.axis_index("hid_0") + lax.axis_index("hid_1")


def pack_kernel(places, keys, values, out, codes, sems):
    quarter = hid_index()
    rows = pl.ds(pl.multiple_of(quarter * QUARTER, QUARTER), QUARTER)
    copies = [
        pltpu.make_async_copy(keys.at[rows, :], out.at[:QUARTER, :HD], sems.at[0]),
        pltpu.make_async_copy(values.at[rows, :], out.at[:QUARTER, HD:], sems.at[1]),
        pltpu.make_async_copy(codes, out.at[QUARTER:, :], sems.at[2]),
    ]
    copies[0].start()
    copies[1].start()
    lane = lax.broadcasted_iota(jnp.int32, (16, PAIR), 1)
    table = jnp.zeros((16, PAIR), jnp.int32)
    for b in range(2):
        place = places[quarter * 2 + b]
        table = jnp.where(lane == 2 * b, place >> 1, table)
        table = jnp.where(lane == 2 * b + 1, place & 1, table)
    codes[...] = table.astype(F32).astype(BF16)
    copies[2].start()
    for copy in copies:
        copy.wait()


def pack(places, keys, values):
    return pl.pallas_call(
        pack_kernel,
        out_shape=shaped((LOAD, PAIR), BF16),
        in_specs=[SMEM, ANY, ANY],
        out_specs=ANY,
        scratch_shapes=[pltpu.VMEM((16, PAIR), BF16), pltpu.SemaphoreType.DMA((3,))],
        compiler_params=params(4),
        cost_estimate=cost(moved=2**19),
        name="pack",
    )(places, keys, values)


def columns_kernel(weight, *refs):
    outs, sems = refs[:4], refs[4]
    y = lax.axis_index("head_1")
    copies = []
    for t, by in enumerate((2, 1, 3, 0)):
        at = lax.rem(y + by, 4) * 1024
        for hi in range(2):
            source = pl.ds(pl.multiple_of(hi * 4096 + at, 1024), 1024)
            copies.append(
                pltpu.make_async_copy(
                    weight.at[:, source],
                    outs[t].at[:, hi * 1024 : (hi + 1) * 1024],
                    sems.at[2 * t + hi],
                )
            )
    for copy in copies:
        copy.start()
    for copy in copies:
        copy.wait()


def columns(weight):
    return pl.pallas_call(
        columns_kernel,
        out_shape=[shaped((ROWS, 2048), BF16)] * 4,
        in_specs=[ANY],
        out_specs=[ANY] * 4,
        scratch_shapes=[pltpu.SemaphoreType.DMA((8,))],
        compiler_params=params(4),
        cost_estimate=cost(moved=2**23),
        name="columns",
    )(weight)


def first_kernel(core_ref, tokens, query, key, value, send, keep, fresh):
    j = pl.program_id(0)
    core = core_ref[0]
    part = jnp.dot(tokens[...], query[...], preferred_element_type=F32)
    for t in range(2):
        cols = slice(t * ROWS, (t + 1) * ROWS)

        @pl.when(j == t)
        def _(cols=cols):
            send[:ROWS, cols] = part.astype(BF16)

        @pl.when(j == 2 + t)
        def _(cols=cols):
            keep[:ROWS, cols] = part

    @pl.when(j == 0)
    def _():
        fresh[:, :HD] = jnp.dot(tokens[...], key[...], preferred_element_type=F32)
        fresh[:, HD:] = jnp.dot(tokens[...], value[...], preferred_element_type=F32)
        for t in range(2):
            cols = slice(t * PAIR, (t + 1) * PAIR)
            far = pl.ds(pl.multiple_of((1 - core) * 128 + t * NEW, NEW), NEW)
            near = pl.ds(pl.multiple_of(core * 128 + t * NEW, NEW), NEW)
            send[ROWS:, cols] = fresh[far, :].astype(BF16)
            keep[ROWS:, cols] = fresh[near, :]


def first(core, tokens, query, key, value):
    def tile(j, core):
        return (0, jnp.where(j < 2, (1 - core[0]) * 2 + j, core[0] * 2 + j - 2))

    whole = lambda a: pl.BlockSpec(a.shape, lambda j, core: (0, 0))
    grid_spec = pltpu.PrefetchScalarGridSpec(
        num_scalar_prefetch=1,
        grid=(4,),
        in_specs=[
            whole(tokens),
            pl.BlockSpec((query.shape[0], ROWS), tile),
            whole(key),
            whole(value),
        ],
        out_specs=[pl.BlockSpec((320, 512), lambda j, core: (0, 0))] * 2,
        scratch_shapes=[pltpu.VMEM((ROWS, PAIR), F32)],
    )
    return pl.pallas_call(
        first_kernel,
        out_shape=[shaped((320, 512), BF16), shaped((320, 512), F32)],
        grid_spec=grid_spec,
        compiler_params=params(20),
        cost_estimate=cost(flops=2 * 256 * 2048 * 1280, moved=6 * 2**20),
        name="first",
    )(core, tokens, query, key, value)


def second_kernel(keep, got, send, onward):
    x = lax.axis_index("hid_0")
    q = keep[:ROWS, :] + got[:ROWS, :].astype(F32)
    send[:ROWS, :] = q.astype(BF16)
    onward[:ROWS, :] = q
    low = keep[ROWS:, :] + got[ROWS:, :].astype(F32)
    sides = [low[:, :PAIR], low[:, PAIR:]]
    sides = [jnp.concatenate([s[:32], s[32:]], axis=1) for s in sides]
    mine = jnp.where(x == 0, sides[0], sides[1])
    other = jnp.where(x == 0, sides[1], sides[0])
    send[ROWS:, :] = other.astype(BF16)
    onward[ROWS:, :] = mine


def second(keep, got):
    return pl.pallas_call(
        second_kernel,
        out_shape=[shaped((288, 512), BF16), shaped((288, 512), F32)],
        in_specs=[VMEM] * 2,
        out_specs=[VMEM] * 2,
        compiler_params=params(8),
        cost_estimate=cost(flops=2**18, moved=2**20),
        name="second",
    )(keep, got)


def new_offset():
    return lax.axis_index("hid_1") * 128 + lax.axis_index("hid_0") * NEW


def rotate_kernel(keep, got, cosine, sine, queries, notes):
    for h in range(4):
        cols = slice(h * HD, (h + 1) * HD)
        u = keep[:ROWS, cols] + got[:ROWS, cols].astype(F32)
        turned = u * cosine[...] + pltpu.roll(u, HD // 2, 1) * sine[...]
        queries[:, cols] = turned.astype(BF16)
    low = keep[ROWS:, :] + got[ROWS:, :].astype(F32)
    low = jnp.concatenate([low[:, :PAIR], low[:, PAIR:]], axis=0)
    rows = pl.ds(pl.multiple_of(new_offset(), NEW), NEW)
    u = low[:, :HD]
    turned = u * cosine[rows, :] + pltpu.roll(u, HD // 2, 1) * sine[rows, :]
    for z in range(8):
        notes[z, :, :HD] = turned.astype(BF16)
        notes[z, :, HD:] = low[:, HD:].astype(BF16)


def rotated(keep, got, cosine, sine):
    return pl.pallas_call(
        rotate_kernel,
        out_shape=[shaped((ROWS, 512), BF16), shaped((8, NEW, PAIR), BF16)],
        in_specs=[VMEM] * 4,
        out_specs=[VMEM] * 2,
        compiler_params=params(8),
        cost_estimate=cost(flops=2**20, moved=2**20),
        name="rotated",
    )(keep, got, cosine, sine)


def gather_visible(mine, slabs, loads, new, keys, values, chunk):
    height = keys.shape[0]
    values[:, HD:] = jnp.ones((height, HD), BF16)
    n = jnp.int32(0)
    lane = lax.broadcasted_iota(jnp.int32, (16, HD), 1)
    for load in loads:
        codes = load[QUARTER:, :HD].astype(F32)
        codes = jnp.where(lane % 2 == 0, 2.0, 1.0) * codes
        for b in range(2):
            part = jnp.where(lane // 2 == b, codes, 0.0)
            place = jnp.max(part[:1] + pltpu.roll(part, HD - 1, 1)[:1]).astype(jnp.int32)
            seen = place < mine

            @pl.when(seen)
            def _(load=load, b=b, n=n):
                at = pl.ds(pl.multiple_of(n * NEW, NEW), ROWS)
                rows = slice(b * ROWS, (b + 1) * ROWS)
                keys[at, :] = load[rows, :HD]
                values[at, :HD] = load[rows, HD:]

            n = n + jnp.where(seen, ROWS // NEW, 0)
    if new is not None:
        for z in range(8):
            seen = slabs[z] < mine

            @pl.when(seen)
            def _(z=z, n=n):
                at = pl.ds(pl.multiple_of(n * NEW, NEW), NEW)
                keys[at, :] = new[z, :, :HD]
                values[at, :HD] = new[z, :, HD:]

            n = n + jnp.where(seen, 1, 0)
    per = chunk // NEW
    chunks = (n + per - 1) // per

    def pad(t, carry):
        at = pl.ds(pl.multiple_of(t * NEW, NEW), NEW)
        keys[at, :] = keys[:NEW, :]
        values[at, :] = jnp.zeros((NEW, PAIR), BF16)
        return carry

    lax.fori_loop(n, chunks * per, pad, 0)
    return chunks


def attend(q, peak_ref, chunks, keys, values, scores, chunk, acc_at, before):
    def peaks(i, carry):
        at = pl.ds(pl.multiple_of(i * chunk, chunk), chunk)
        s = lax.dot_general(q, keys[at, :], CONTRACT, preferred_element_type=F32)
        scores[i] = s
        best = peak_ref[...]
        for t in range(chunk // HD):
            best = jnp.maximum(best, s[:, t * HD : (t + 1) * HD])
        peak_ref[...] = best
        return carry

    lax.fori_loop(0, chunks, peaks, 0)
    peak = jnp.max(peak_ref[...], axis=1, keepdims=True)
    acc_at[...] = before(peak)

    def weigh(i, carry):
        at = pl.ds(pl.multiple_of(i * chunk, chunk), chunk)
        p = jnp.exp2((scores[i] - peak) * EXPONENT).astype(BF16)
        acc_at[...] += jnp.dot(p, values[at, :], preferred_element_type=F32)
        return carry

    lax.fori_loop(0, chunks, weigh, 0)
    return peak


def near_kernel(
    slabs, near, far, own, *refs, chunk, count
):
    loads, (q_out, acc_out, peak_out) = refs[:count], refs[count : count + 3]
    keys, values, scores, peak_ref = refs[count + 3 :]
    mine = slabs[lax.axis_index("key")]
    core = lax.axis_index("hid_1")
    x = lax.axis_index("hid_0")
    for j in range(4):
        half = x if j < 2 else 1 - x
        parity = core if j % 2 == 0 else 1 - core
        cols = pl.ds(pl.multiple_of(parity * PAIR, PAIR), PAIR)
        rows = [slice((2 * j + t) * ROWS, (2 * j + t + 1) * ROWS) for t in range(2)]

        @pl.when(half == core)
        def _(cols=cols, rows=rows):
            both = near[:, cols]
            q_out[rows[0], :] = both[:, :HD]
            q_out[rows[1], :] = both[:, HD:]

        @pl.when(half != core)
        def _(cols=cols, rows=rows):
            both = far[:, cols]
            q_out[rows[0], :] = both[:, :HD]
            q_out[rows[1], :] = both[:, HD:]

    chunks = gather_visible(mine, None, loads, None, keys, values, chunk)
    zeros = jnp.zeros((NEW, HD), BF16)
    own_keys = jnp.concatenate([own[0, :, :HD], zeros], axis=0)
    own_values = jnp.concatenate([own[0, :, HD:], zeros], axis=0)
    own_values = jnp.concatenate([own_values, jnp.ones((HD, HD), BF16)], axis=1)
    row = lax.broadcasted_iota(jnp.int32, (TALL, HD), 0) % ROWS
    lane = lax.broadcasted_iota(jnp.int32, (TALL, HD), 1)
    visible = jnp.logical_and(lane < NEW, lane + new_offset() <= row)

    def tall(step, carry):
        at = pl.ds(pl.multiple_of(step * TALL, TALL), TALL)
        q = q_out[at, :]
        s = lax.dot_general(q, own_keys, CONTRACT, preferred_element_type=F32)
        s = jnp.where(visible, s, NEGATIVE)
        peak_ref[...] = s

        def before(peak):
            p = jnp.where(visible, jnp.exp2((s - peak) * EXPONENT), 0.0)
            return jnp.dot(p.astype(BF16), own_values, preferred_element_type=F32)

        peak = attend(
            q, peak_ref, chunks, keys, values, scores, chunk, acc_out.at[at, :], before
        )
        peak_out[at, :] = jnp.broadcast_to(peak, (TALL, HD))
        return carry

    lax.fori_loop(0, 8 * ROWS // TALL, tall, 0)


def attend_near(slabs, near, far, own, loads):
    count, chunk = len(loads), 1280
    height = count * QUARTER
    return pl.pallas_call(
        functools.partial(near_kernel, chunk=chunk, count=count),
        out_shape=[
            shaped((8 * ROWS, HD), BF16),
            shaped((8 * ROWS, PAIR), F32),
            shaped((8 * ROWS, HD), F32),
        ],
        in_specs=[SMEM] + [VMEM] * (3 + count),
        out_specs=[VMEM] * 3,
        scratch_shapes=[
            pltpu.VMEM((height, HD), BF16),
            pltpu.VMEM((height, PAIR), BF16),
            pltpu.VMEM((height // chunk, TALL, chunk), F32),
            pltpu.VMEM((TALL, HD), F32),
        ],
        compiler_params=params(30),
        cost_estimate=cost(8 * ROWS * height * HD * 6, 2**23, 8 * ROWS * height),
        name="near",
    )(slabs, near, far, own, *loads)


def far_kernel(slabs, queries, acc_in, peak_in, new, *refs, chunk, count):
    loads, outs = refs[:count], refs[count : count + 4]
    keys, values, scores, peak_ref, acc = refs[count + 4 :]
    mine = slabs[lax.axis_index("key")]
    chunks = gather_visible(mine, slabs, loads, new, keys, values, chunk)
    where = lax.broadcasted_iota(jnp.int32, (16, ROWS), 0)
    for step in range(8 * ROWS // TALL):
        at = slice(step * TALL, (step + 1) * TALL)
        peak_ref[...] = peak_in[at, :]

        def before(peak, at=at):
            factor = jnp.exp2((peak_in[at, :1] - peak) * EXPONENT)
            return acc_in[at, :] * factor

        peak = attend(
            queries[at, :], peak_ref, chunks, keys, values, scores, chunk, acc, before
        )
        total = acc[:, HD:]
        some = total > 0.0
        safe = jnp.where(some, total, 1.0)
        heads = (acc[:, :HD] / safe).astype(BF16)
        level = jnp.where(some, peak * EXPONENT + jnp.log2(safe), NEGATIVE)
        level = jnp.transpose(level)[:1, :]
        for t in range(TALL // (2 * ROWS)):
            out = outs[step * (TALL // (2 * ROWS)) + t]
            table = jnp.zeros((16, ROWS), F32)
            for half in range(2):
                rows = slice((2 * t + half) * ROWS, (2 * t + half + 1) * ROWS)
                out[:ROWS, half * HD : (half + 1) * HD] = heads[rows]
                rest = level[:, rows]
                for k in range(3):
                    coded = rest.astype(BF16).astype(F32)
                    table = jnp.where(where == 3 * half + k, coded, table)
                    rest = rest - coded
            out[ROWS:, :] = table.astype(BF16)


def attend_far(slabs, queries, acc, peak, new, loads):
    count, chunk = len(loads), 1024
    height = -(-(count * QUARTER + 8 * NEW) // chunk) * chunk
    return pl.pallas_call(
        functools.partial(far_kernel, chunk=chunk, count=count),
        out_shape=[shaped((MSG, PAIR), BF16)] * 4,
        in_specs=[SMEM] + [VMEM] * (4 + count),
        out_specs=[VMEM] * 4,
        scratch_shapes=[
            pltpu.VMEM((height, HD), BF16),
            pltpu.VMEM((height, PAIR), BF16),
            pltpu.VMEM((height // chunk, TALL, chunk), F32),
            pltpu.VMEM((TALL, HD), F32),
            pltpu.VMEM((TALL, PAIR), F32),
        ],
        compiler_params=params(30),
        cost_estimate=cost(8 * ROWS * height * HD * 6, 2**23, 8 * ROWS * height),
        name="far",
    )(slabs, queries, acc, peak, new, *loads)


def merge_kernel(*refs):
    parts, out = refs[:4], refs[4]
    levels = []
    for ref in parts:
        t = ref[ROWS:, :].astype(F32)
        levels.append([t[0:1] + t[1:2] + t[2:3], t[3:4] + t[4:5] + t[5:6]])
    rows = []
    for half in range(2):
        top = functools.reduce(jnp.maximum, [lv[half] for lv in levels])
        w = [jnp.exp2(lv[half] - top) for lv in levels]
        total = w[0] + w[1] + w[2] + w[3]
        rows.extend([x / total for x in w])
    table = jnp.concatenate(rows, axis=0)
    table = jnp.transpose(jnp.concatenate([table, jnp.zeros((HD - 8, ROWS), F32)], axis=0))
    for half in range(2):
        cols = slice(half * HD, (half + 1) * HD)
        so_far = None
        for t, ref in enumerate(parts):
            w = table[:, half * 4 + t : half * 4 + t + 1]
            term = ref[:ROWS, cols].astype(F32) * w
            so_far = term if so_far is None else so_far + term
        out[:, cols] = so_far.astype(BF16)


def merge(parts):
    return pl.pallas_call(
        merge_kernel,
        out_shape=shaped((ROWS, PAIR), BF16),
        in_specs=[VMEM] * 4,
        out_specs=VMEM,
        compiler_params=params(8),
        cost_estimate=cost(10**6, 10**6, 4096),
        name="merge",
    )(*parts)


def project_kernel(*refs):
    heads, weights, send, keep = refs[:4], refs[4:8], refs[8], refs[9]
    core = lax.axis_index("hid_1")
    h = jnp.concatenate([ref[...] for ref in heads], axis=1)
    for out, side in ((send, 1 - core), (keep, core)):
        for t in range(4):
            cols = pl.ds(pl.multiple_of(t * 512 + side * ROWS, ROWS), ROWS)
            w = jnp.concatenate([ref[:, cols] for ref in weights], axis=0)
            total = jnp.dot(h, w, preferred_element_type=F32)
            out[:, t * ROWS : (t + 1) * ROWS] = total.astype(out.dtype)


def project(heads, weights):
    width = weights[0].shape[1]
    return pl.pallas_call(
        project_kernel,
        out_shape=[shaped((ROWS, width // 2), BF16), shaped((ROWS, width // 2), F32)],
        in_specs=[VMEM] * 8,
        out_specs=[VMEM] * 2,
        compiler_params=params(16),
        cost_estimate=cost(flops=2 * ROWS * 8 * HD * width, moved=6 * 2**20),
        name="project",
    )(*heads, *weights)


def split_kernel(keep, got, own, *sends):
    spot = 2 * lax.axis_index("head_0") + lax.axis_index("hid_0")
    for by in range(4):
        cols = pl.ds(pl.multiple_of(lax.rem(spot + by, 4) * ROWS, ROWS), ROWS)
        total = keep[:, cols] + got[:, cols].astype(F32)
        if by == 0:
            own[...] = total
        else:
            sends[by - 1][...] = total.astype(BF16)


def split(keep, got):
    return pl.pallas_call(
        split_kernel,
        out_shape=[shaped((ROWS, ROWS), F32)] + [shaped((ROWS, ROWS), BF16)] * 3,
        in_specs=[VMEM] * 2,
        out_specs=[VMEM] * 4,
        compiler_params=params(8),
        cost_estimate=cost(flops=2**18, moved=2**21),
        name="split",
    )(keep, got)


def body(
    tokens,
    query_weight,
    key_weight,
    value_weight,
    output_weight,
    key_cache,
    value_cache,
    cache_places,
    slab_places,
):
    key_index = lax.axis_index("key")
    core = lax.axis_index("hid_1")

    load = pack(cache_places, key_cache.reshape(-1, HD), value_cache.reshape(-1, HD))
    up = [load]
    for _ in range(4):
        up.append(lax.ppermute(up[-1], "key", shift(8, 1)))
    down = [load]
    for _ in range(3):
        down.append(lax.ppermute(down[-1], "key", shift(8, -1)))

    pieces = columns(output_weight)
    weights = [pieces[3]]
    for piece, by in zip(pieces, (2, 1, 3)):
        weights.append(lax.ppermute(piece, "head_1", shift(4, by)))

    send, keep = first(
        core.astype(jnp.int32).reshape(1), tokens, query_weight, key_weight, value_weight
    )
    send, keep = second(keep, swap(send, "hid_1"))
    got = swap(send, "hid_0")

    middle = HD // 2
    index = np.arange(HD) % middle
    frequency = jnp.exp(jnp.asarray(index, F32) * (-2.0 * math.log(THETA) / HD))
    sign = np.where(np.arange(HD) < middle, -1.0, 1.0).astype(np.float32)
    spots = slab_places[key_index] * ROWS + jnp.arange(ROWS, dtype=jnp.int32)
    angles = spots.astype(F32)[:, None] * frequency[None, :]
    queries, notes = rotated(keep, got, jnp.cos(angles), jnp.sin(angles) * sign[None, :])
    far = swap(queries, "hid_1")

    new = lax.all_to_all(notes, "key", split_axis=0, concat_axis=0, tiled=True)

    state = attend_near(slab_places, queries, far, notes, up[:3] + down[1:3])
    parts = attend_far(slab_places, *state, new, [up[3], down[3], up[4]])
    flip = [(0, 3), (1, 2), (2, 1), (3, 0)]
    merged = merge(
        [
            parts[0],
            swap(parts[1], "hid_1"),
            swap(parts[2], "hid_0"),
            lax.ppermute(parts[3], HID, flip),
        ]
    )

    heads = [merged] + [lax.ppermute(merged, "head_1", shift(4, by)) for by in (2, 1, 3)]
    send, keep = project(heads, weights)
    own, *blocks = split(keep, swap(send, "hid_1"))
    out = own
    for by in (2, 1, 3):
        out = out + lax.ppermute(blocks[by - 1], ALONG_X, shift(4, by)).astype(F32)
    return out.astype(BF16)


def solution(mesh):
    finer = Mesh(
        mesh.devices.reshape(2, 4, mesh.shape["key"], 2, 2),
        ("head_0", "head_1", "key", "hid_0", "hid_1"),
    )
    return jax.shard_map(
        body,
        mesh=finer,
        in_specs=(
            P("key", HID),
            P(HID, HEAD),
            P(HID, HEAD),
            P(HID, HEAD),
            P(HEAD_HID, None),
            P("key", HEAD, None),
            P("key", HEAD, None),
            P("key"),
            P(),
        ),
        out_specs=P("key", HEAD_HID),
        check_vma=False,
    )
```

time: 300 us -> 119 us (0.40)
  blocking collectives: 68.8 us -> 0 us
  waiting for transfers between devices: 84.4 us -> 21.3 us
  matrix products: 42 us -> 0 us
  other arithmetic: 41.3 us -> 1.25 us
  Pallas kernels: 0 us -> 30.9 us
  starting transfers between devices: 31 us -> 41.2 us
  local copies, waits for them, and re-layouts: 30.1 us -> 22.6 us
    all_to_all x6 -> x1, waiting for transfers between devices: 84.4 us -> 0.01 us  [body(): new = lax.all_to_all(notes, 'key', split_axis=0, concat_axis=0, tiled=True)]
    all_to_all x2 -> x0, blocking collectives: 68.8 us -> none  [the longest x1 56.9 us: summed_rows(): return jnp.sum(lax.all_to_all(own, far, 0, 0, tiled=True), axis=0)]
    dot_general x6 -> x0, matrix products: 42 us -> none  [the longest x1 17.8 us: body(): jnp.einsum('rkgd,ckd->rkgc', grouped, key_rows, preferred_element_type=jn...]
    ppermute x0 -> x23, starting transfers between devices: none -> 35.1 us  [the longest x3 9.88 us: body(): down.append(lax.ppermute(down[-1], 'key', shift(8, -1)))]
    reduce_sum x10 -> x0, other arithmetic: 31.2 us -> none  [the longest x2 17.5 us: body(): totals = jnp.sum(weights, axis=-1)]
    pallas_call x0 -> x10, Pallas kernels: none -> 30.9 us  [the longest x1 12 us: attend_near(): pl.pallas_call(functools.partial(near_kernel, chunk=chunk, count=count),...]
    all_to_all x6 -> x1, starting transfers between devices: 31 us -> 6.1 us  [body(): new = lax.all_to_all(notes, 'key', split_axis=0, concat_axis=0, tiled=True)]
    ppermute x0 -> x23, waiting for transfers between devices: none -> 21.3 us  [the longest x3 6.55 us: body(): lax.ppermute(merged, 'head_1', shift(4, by))]
  transfers between devices with their start and end apart: 6 -> 24, of which waited for: 5 -> 8; matrix products, arithmetic and copies ran while one was open for 16% -> 1% of each run, Pallas kernels for 0% -> 23%
where the time goes in v1:
time: 119 us; the launch traced here: 118 us
  starting transfers between devices  41.2 us (35%)
  Pallas kernels  30.9 us (26%)
  local copies, waits for them, and re-layouts  22.6 us (19%)
  waiting for transfers between devices  21.3 us (18%)
  other arithmetic  1.25 us (1%)
    unnamed x46, local copies, waits for them, and re-layouts  22.1 us
    pallas_call x1, Pallas kernels, attend_near(): pl.pallas_call(functools.partial(near_kernel, chunk=chunk, count=count),...  12 us
    ppermute x3, starting transfers between devices, body(): down.append(lax.ppermute(down[-1], 'key', shift(8, -1)))  9.88 us
    pallas_call x1, Pallas kernels, attend_far(): pl.pallas_call(functools.partial(far_kernel, chunk=chunk, count=count), o...  9.59 us
    ppermute x6, starting transfers between devices, swap(): return lax.ppermute(array, axis, shift(2, 1))  7.5 us
    ppermute x3, waiting for transfers between devices, body(): lax.ppermute(merged, 'head_1', shift(4, by))  6.55 us
    all_to_all x1, starting transfers between devices, body(): new = lax.all_to_all(notes, 'key', split_axis=0, concat_axis=0, tiled=True)  6.1 us
    ppermute x3, starting transfers between devices, body(): weights.append(lax.ppermute(piece, 'head_1', shift(4, by)))  5.6 us
  transfers between devices with their start and end apart: 24, of which 8 were waited for; matrix products, arithmetic and copies ran while one was open for 1% of the time, Pallas kernels for 23%

profile of v1, /device:TPU:1, one launch (start us, length us, event | category | flops | bytes accessed | tf_op | source)
XLA Modules:
  0.0 118.1 jit_solution(13274739674866920745)
XLA Ops:
  0.0 1.1 copy-done.3
  1.1 1.0 copy-done.4
  3.4 2.5 %collective-permute-start.3 = (bf16[528,256]{1,0:T(8,128)(2,1)S(1)}, bf16[528,256]{1,0:T(8,128)(2,1)S(1)}, u32[]{:S(2)}, u32[]{:S(2)}) collective-permute-start(bf16[528,256]{1,0:T(8,128)(2,1)S(1)} %pack.1.refs_0_), channel_id=1, source_target_pairs={{0,4},{4,8},{8,12},{12,16},{16,20},{20,24},{24,28},{28,0},{1,5},{5... | collective-permute-start | bytes 811016 | tf_op jit(solution)/shard_map/ppermute | solution.py:552
  6.0 2.2 %copy-done = bf16[2048,1024]{1,0:T(8,128)(2,1)S(1)} copy-done((bf16[2048,1024]{1,0:T(8,128)(2,1)S(1)}, bf16[2048,1024]{1,0:T(8,128)(2,1)}, u32[]{:S(2)}) %copy-start) | copy-done | bytes 4194328
  8.2 1.2 %copy-done.2 = bf16[256,2048]{1,0:T(8,128)(2,1)S(1)} copy-done((bf16[256,2048]{1,0:T(8,128)(2,1)S(1)}, bf16[256,2048]{1,0:T(8,128)(2,1)}, u32[]{:S(2)}) %copy-start.2) | copy-done | bytes 1048600
  9.4 1.0 copy-done.5
  10.4 1.0 copy-done.6
  11.5 3.2 %first.1 = (bf16[320,512]{1,0:T(8,128)(2,1)S(1)}, f32[320,512]{1,0:T(8,128)S(1)}) custom-call(s32[1]{0:T(128)} %bitcast.core_ref, bf16[256,2048]{1,0:T(8,128)(2,1)S(1)} %copy-done.2, bf16[2048,1024]{1,0:T(8,128)(2,1)S(1)} %copy-done, bf16[2048,128]{1,0:T(8,128)(2,1)S(1)} %copy-done.5, bf16[2048,128]{1,0:T(8,128)(2,1)S(1)} %copy-done.6), custom_call_target="tpu_custom_call" | custom-call | flops 1342177280 | bytes 6291456 | tf_op jit(solution)/shard_map/first/pallas_call | solution.py:176
  14.7 1.0 collective-permute-start
  15.7 3.7 %collective-permute-start.5 = (bf16[528,256]{1,0:T(8,128)(2,1)S(1)}, bf16[528,256]{1,0:T(8,128)(2,1)}, u32[]{:S(2)}, u32[]{:S(2)}) collective-permute-start(bf16[528,256]{1,0:T(8,128)(2,1)S(1)} %pack.1.refs_0_), channel_id=1, source_target_pairs={{0,28},{4,0},{8,4},{12,8},{16,12},{20,16},{24,20},{28,24},{1,29},{... | collective-permute-start | bytes 811016 | tf_op jit(solution)/shard_map/ppermute | solution.py:555
  20.8 1.3 %collective-permute-start.1 = (bf16[288,512]{1,0:T(8,128)(2,1)S(1)}, bf16[288,512]{1,0:T(8,128)(2,1)S(1)}, u32[]{:S(2)}, u32[]{:S(2)}) collective-permute-start(bf16[288,512]{1,0:T(8,128)(2,1)S(1)} %get-tuple-element.31), channel_id=1, source_target_pairs={{0,2},{2,0},{1,3},{3,1},{4,6},{6,4},{5,7},{7,5},{8,10},{10,8},{9,1... | collective-permute-start | bytes 884744 | tf_op jit(solution)/shard_map/ppermute | solution.py:56
  22.1 3.2 %collective-permute-done.5.refs_3_ = bf16[528,256]{1,0:T(8,128)(2,1)} collective-permute-done((bf16[528,256]{1,0:T(8,128)(2,1)S(1)}, bf16[528,256]{1,0:T(8,128)(2,1)}, u32[]{:S(2)}, u32[]{:S(2)}) %collective-permute-start.5) | collective-permute-done | bytes 270368 | tf_op jit(solution)/shard_map/ppermute | solution.py:555
  25.3 3.5 %collective-permute-start.6 = (bf16[528,256]{1,0:T(8,128)(2,1)}, bf16[528,256]{1,0:T(8,128)(2,1)}, u32[]{:S(2)}, u32[]{:S(2)}) collective-permute-start(bf16[528,256]{1,0:T(8,128)(2,1)} %collective-permute-done.5.refs_3_), channel_id=1, source_target_pairs={{0,28},{4,0},{8,4},{12,8},{16,12},{20,16},{24,20},{28,24},{1,29},{... | collective-permute-start | bytes 811016 | tf_op jit(solution)/shard_map/ppermute | solution.py:555
  29.3 1.0 rotated.1
  30.4 1.1 collective-permute-start.2
  31.5 2.2 %copy-done.1 = bf16[256,8192]{1,0:T(8,128)(2,1)S(1)} copy-done((bf16[256,8192]{1,0:T(8,128)(2,1)S(1)}, bf16[256,8192]{1,0:T(8,128)(2,1)}, u32[]{:S(2)}) %copy-start.1) | copy-done | bytes 4194328
  33.7 1.1 columns.1
  34.8 1.0 copy-done.8
  35.8 1.0 copy-done.9
  36.8 2.9 %collective-permute-start.16 = (bf16[256,2048]{1,0:T(8,128)(2,1)}, bf16[256,2048]{1,0:T(8,128)(2,1)S(1)}, u32[]{:S(2)}, u32[]{:S(2)}) collective-permute-start(bf16[256,2048]{1,0:T(8,128)(2,1)} %get-tuple-element.42), channel_id=1, source_target_pairs={{0,64},{32,96},{64,0},{96,32},{1,65},{33,97},{65,1},{97,33},{2,66}... | collective-permute-start | bytes 3145736 | tf_op jit(solution)/shard_map/ppermute | solution.py:560
  39.7 6.1 %all-to-all-start = ((bf16[8,64,256]{2,1,0:T(8,128)(2,1)}), bf16[8,64,256]{2,1,0:T(8,128)(2,1)}, u32[]{:S(2)}, u32[]{:S(2)}) async-start(bf16[8,64,256]{2,1,0:T(8,128)(2,1)} %get-tuple-element.33.own), calls=%async_computation | async-start | bytes 524288 | tf_op jit(solution)/shard_map/all_to_all | solution.py:577
  46.2 2.3 %collective-permute-start.18 = (bf16[256,2048]{1,0:T(8,128)(2,1)}, bf16[256,2048]{1,0:T(8,128)(2,1)}, u32[]{:S(2)}, u32[]{:S(2)}) collective-permute-start(bf16[256,2048]{1,0:T(8,128)(2,1)} %copy-done.8), channel_id=1, source_target_pairs={{0,96},{32,0},{64,32},{96,64},{1,97},{33,1},{65,33},{97,65},{2,98}... | collective-permute-start | bytes 3145736 | tf_op jit(solution)/shard_map/ppermute | solution.py:560
  48.5 2.7 %collective-permute-start.8 = (bf16[528,256]{1,0:T(8,128)(2,1)}, bf16[528,256]{1,0:T(8,128)(2,1)S(1)}, u32[]{:S(2)}, u32[]{:S(2)}) collective-permute-start(bf16[528,256]{1,0:T(8,128)(2,1)} %collective-permute-done.6.refs_4_), channel_id=1, source_target_pairs={{0,28},{4,0},{8,4},{12,8},{16,12},{20,16},{24,20},{28,24},{1,29},{... | collective-permute-start | bytes 811016 | tf_op jit(solution)/shard_map/ppermute | solution.py:555
  51.2 0.9 copy-done.11
  52.1 12.0 %near.1 = (bf16[2048,128]{1,0:T(8,128)(2,1)S(1)}, f32[2048,256]{1,0:T(8,128)S(1)}, f32[2048,128]{1,0:T(8,128)S(1)}) custom-call(s32[8]{0:T(128)S(1)} %copy-done.14, bf16[256,512]{1,0:T(8,128)(2,1)} %get-tuple-element.32.near, bf16[256,512]{1,0:T(8,128)(2,1)} %collective-permute-done.2.far, bf16[8,64,256]{2,1,0:T(8,128)(2,1)} %get-tuple-element.33.own, ...), custom_call_target="tpu_custom_call" | custom-call | flops 4026531840 | bytes 8388608 | tf_op jit(solution)/shard_map/near/pallas_call | solution.py:372
  64.2 1.3 %copy-done.15 = f32[2048,256]{1,0:T(8,128)} copy-done((f32[2048,256]{1,0:T(8,128)}, f32[2048,256]{1,0:T(8,128)S(1)}, u32[]{:S(2)}) %copy-start.15) | copy-done | bytes 2097176
  65.6 1.0 copy-done.17
  66.5 0.8 copy-done.19
  68.1 0.9 copy-done.13
  69.1 1.6 %copy-done.16 = f32[2048,256]{1,0:T(8,128)S(1)} copy-done((f32[2048,256]{1,0:T(8,128)S(1)}, f32[2048,256]{1,0:T(8,128)}, u32[]{:S(2)}) %copy-start.16) | copy-done | bytes 2097176
  70.6 1.2 %copy-done.18 = f32[2048,128]{1,0:T(8,128)S(1)} copy-done((f32[2048,128]{1,0:T(8,128)S(1)}, f32[2048,128]{1,0:T(8,128)}, u32[]{:S(2)}) %copy-start.18) | copy-done | bytes 1048600
  71.9 1.0 copy-done.20
  72.9 9.6 %far.1 = (bf16[272,256]{1,0:T(8,128)(2,1)S(1)}, bf16[272,256]{1,0:T(8,128)(2,1)S(1)}, bf16[272,256]{1,0:T(8,128)(2,1)S(1)}, bf16[272,256]{1,0:T(8,128)(2,1)S(1)}) custom-call(s32[8]{0:T(128)S(1)} %copy-done.14, bf16[2048,128]{1,0:T(8,128)(2,1)S(1)} %copy-done.20, f32[2048,256]{1,0:T(8,128)S(1)} %copy-done.16, f32[2048,128]{1,0:T(8,128)S(1)} %copy-done.18, ...), custom_call_target="tpu_custom_call" | custom-call | flops 3221225472 | bytes 8388608 | tf_op jit(solution)/shard_map/far/pallas_call | solution.py:433
  82.5 1.8 %collective-permute-start.10 = (bf16[272,256]{1,0:T(8,128)(2,1)S(1)}, bf16[272,256]{1,0:T(8,128)(2,1)S(1)}, u32[]{:S(2)}, u32[]{:S(2)}) collective-permute-start(bf16[272,256]{1,0:T(8,128)(2,1)S(1)} %get-tuple-element.38), channel_id=1, source_target_pairs={{0,1},{1,0},{2,3},{3,2},{4,5},{5,4},{6,7},{7,6},{8,9},{9,8},{10,11... | collective-permute-start | bytes 417800 | tf_op jit(solution)/shard_map/ppermute | solution.py:56
  84.3 1.2 %collective-permute-start.11 = (bf16[272,256]{1,0:T(8,128)(2,1)S(1)}, bf16[272,256]{1,0:T(8,128)(2,1)S(1)}, u32[]{:S(2)}, u32[]{:S(2)}) collective-permute-start(bf16[272,256]{1,0:T(8,128)(2,1)S(1)} %get-tuple-element.39), channel_id=1, source_target_pairs={{0,2},{2,0},{1,3},{3,1},{4,6},{6,4},{5,7},{7,5},{8,10},{10,8},{9,1... | collective-permute-start | bytes 417800 | tf_op jit(solution)/shard_map/ppermute | solution.py:56
  85.5 1.2 %collective-permute-start.12 = (bf16[272,256]{1,0:T(8,128)(2,1)S(1)}, bf16[272,256]{1,0:T(8,128)(2,1)S(1)}, u32[]{:S(2)}, u32[]{:S(2)}) collective-permute-start(bf16[272,256]{1,0:T(8,128)(2,1)S(1)} %get-tuple-element.40), channel_id=1, source_target_pairs={{0,3},{1,2},{2,1},{3,0},{4,7},{5,6},{6,5},{7,4},{8,11},{9,10},{10,... | collective-permute-start | bytes 417800 | tf_op jit(solution)/shard_map/ppermute | solution.py:587
  86.7 2.8 %collective-permute-done.11.refs_2_ = bf16[272,256]{1,0:T(8,128)(2,1)S(1)} collective-permute-done((bf16[272,256]{1,0:T(8,128)(2,1)S(1)}, bf16[272,256]{1,0:T(8,128)(2,1)S(1)}, u32[]{:S(2)}, u32[]{:S(2)}) %collective-permute-start.11) | collective-permute-done | bytes 139296 | tf_op jit(solution)/shard_map/ppermute | solution.py:56
  89.5 3.2 %collective-permute-done.12.refs_3_ = bf16[272,256]{1,0:T(8,128)(2,1)S(1)} collective-permute-done((bf16[272,256]{1,0:T(8,128)(2,1)S(1)}, bf16[272,256]{1,0:T(8,128)(2,1)S(1)}, u32[]{:S(2)}, u32[]{:S(2)}) %collective-permute-start.12) | collective-permute-done | bytes 139296 | tf_op jit(solution)/shard_map/ppermute | solution.py:587
  93.7 2.4 %collective-permute-start.15 = (bf16[256,256]{1,0:T(8,128)(2,1)S(1)}, bf16[256,256]{1,0:T(8,128)(2,1)S(1)}, u32[]{:S(2)}, u32[]{:S(2)}) collective-permute-start(bf16[256,256]{1,0:T(8,128)(2,1)S(1)} %merge.1.refs_0_), channel_id=1, source_target_pairs={{0,96},{32,0},{64,32},{96,64},{1,97},{33,1},{65,33},{97,65},{2,98}... | collective-permute-start | bytes 393224 | tf_op jit(solution)/shard_map/ppermute | solution.py:591
  96.1 3.7 %collective-permute-done.13.refs_1_ = bf16[256,256]{1,0:T(8,128)(2,1)S(1)} collective-permute-done((bf16[256,256]{1,0:T(8,128)(2,1)S(1)}, bf16[256,256]{1,0:T(8,128)(2,1)S(1)}, u32[]{:S(2)}, u32[]{:S(2)}) %collective-permute-start.13) | collective-permute-done | bytes 131104 | tf_op jit(solution)/shard_map/ppermute | solution.py:591
  99.8 2.9 %collective-permute-done.14.refs_2_ = bf16[256,256]{1,0:T(8,128)(2,1)S(1)} collective-permute-done((bf16[256,256]{1,0:T(8,128)(2,1)S(1)}, bf16[256,256]{1,0:T(8,128)(2,1)S(1)}, u32[]{:S(2)}, u32[]{:S(2)}) %collective-permute-start.14) | collective-permute-done | bytes 131104 | tf_op jit(solution)/shard_map/ppermute | solution.py:591
  102.6 2.5 %project.1 = (bf16[256,1024]{1,0:T(8,128)(2,1)S(1)}, f32[256,1024]{1,0:T(8,128)S(1)}) custom-call(bf16[256,256]{1,0:T(8,128)(2,1)S(1)} %merge.1.refs_0_, bf16[256,256]{1,0:T(8,128)(2,1)S(1)} %collective-permute-done.13.refs_1_, bf16[256,256]{1,0:T(8,128)(2,1)S(1)} %collective-permute-done.14.refs_2_, bf16[256,256]{1,0:T(8,128)(2,1)S(1)} %collective-permute-done.15.refs_3_, ...), custom_call_target="tpu_custom_call" | custom-call | flops 1073741824 | bytes 6291456 | tf_op jit(solution)/shard_map/project/pallas_call | solution.py:501
  105.2 1.0 collective-permute-start.19
  106.2 1.5 %collective-permute-done.19.got = bf16[256,1024]{1,0:T(8,128)(2,1)S(1)} collective-permute-done((bf16[256,1024]{1,0:T(8,128)(2,1)S(1)}, bf16[256,1024]{1,0:T(8,128)(2,1)S(1)}, u32[]{:S(2)}, u32[]{:S(2)}) %collective-permute-start.19) | collective-permute-done | bytes 524320 | tf_op jit(solution)/shard_map/ppermute | solution.py:56
  107.9 2.8 %collective-permute-start.20 = (bf16[256,256]{1,0:T(8,128)(2,1)S(1)}, bf16[256,256]{1,0:T(8,128)(2,1)S(1)}, u32[]{:S(2)}, u32[]{:S(2)}) collective-permute-start(bf16[256,256]{1,0:T(8,128)(2,1)S(1)} %get-tuple-element.48), channel_id=1, source_target_pairs={{0,128},{2,130},{128,0},{130,2},{1,129},{3,131},{129,1},{131,3},{4... | collective-permute-start | bytes 393224 | tf_op jit(solution)/shard_map/ppermute | solution.py:596
  111.0 2.3 %collective-permute-start.22 = (bf16[256,256]{1,0:T(8,128)(2,1)S(1)}, bf16[256,256]{1,0:T(8,128)(2,1)S(1)}, u32[]{:S(2)}, u32[]{:S(2)}) collective-permute-start(bf16[256,256]{1,0:T(8,128)(2,1)S(1)} %get-tuple-element.50), channel_id=1, source_target_pairs={{0,130},{2,0},{128,2},{130,128},{1,131},{3,1},{129,3},{131,129},{4... | collective-permute-start | bytes 393224 | tf_op jit(solution)/shard_map/ppermute | solution.py:596
  113.4 0.8 collective-permute-done.20
  114.2 3.3 %collective-permute-done.21 = bf16[256,256]{1,0:T(8,128)(2,1)S(1)} collective-permute-done((bf16[256,256]{1,0:T(8,128)(2,1)S(1)}, bf16[256,256]{1,0:T(8,128)(2,1)S(1)}, u32[]{:S(2)}, u32[]{:S(2)}) %collective-permute-start.21) | collective-permute-done | bytes 131104 | tf_op jit(solution)/shard_map/ppermute | solution.py:596
  (60 shorter events, 5.9 us)
Async XLA Ops:
  0.0 19.4 %copy-start.14 = (s32[8]{0:T(128)S(1)}, s32[8]{0:T(128)}, u32[]{:S(2)}) copy-start(s32[8]{0:T(128)} %slabs.3) | copy-start | bytes 100
  0.0 1.1 copy-start.3
  1.1 1.0 copy-start.4
  2.1 0.7 copy-start.7
  2.8 26.0 %copy-start.21 = (f32[128]{0:T(128)S(1)}, f32[128]{0:T(128)}, u32[]{:S(2)}) copy-start(f32[128]{0:T(128)} %constant.28) | copy-start | bytes 1540
  2.8 26.0 %copy-start.22 = (f32[128]{0:T(128)S(1)}, f32[128]{0:T(128)}, u32[]{:S(2)}) copy-start(f32[128]{0:T(128)} %constant.29) | copy-start | bytes 1540
  3.4 16.0 %collective-permute-start.3 = (bf16[528,256]{1,0:T(8,128)(2,1)S(1)}, bf16[528,256]{1,0:T(8,128)(2,1)S(1)}, u32[]{:S(2)}, u32[]{:S(2)}) collective-permute-start(bf16[528,256]{1,0:T(8,128)(2,1)S(1)} %pack.1.refs_0_), channel_id=1, source_target_pairs={{0,4},{4,8},{8,12},{12,16},{16,20},{20,24},{24,28},{28,0},{1,5},{5... | collective-permute-start | bytes 811016 | tf_op jit(solution)/shard_map/ppermute | solution.py:552
  6.0 2.2 %copy-start = (bf16[2048,1024]{1,0:T(8,128)(2,1)S(1)}, bf16[2048,1024]{1,0:T(8,128)(2,1)}, u32[]{:S(2)}) copy-start(bf16[2048,1024]{1,0:T(8,128)(2,1)} %query.1) | copy-start | bytes 12582916
  8.2 1.2 %copy-start.2 = (bf16[256,2048]{1,0:T(8,128)(2,1)S(1)}, bf16[256,2048]{1,0:T(8,128)(2,1)}, u32[]{:S(2)}) copy-start(bf16[256,2048]{1,0:T(8,128)(2,1)} %tokens.1) | copy-start | bytes 3145732
  9.4 1.0 copy-start.5
  10.4 1.0 copy-start.6
  14.7 6.0 %collective-permute-start = (bf16[320,512]{1,0:T(8,128)(2,1)S(1)}, bf16[320,512]{1,0:T(8,128)(2,1)S(1)}, u32[]{:S(2)}, u32[]{:S(2)}) collective-permute-start(bf16[320,512]{1,0:T(8,128)(2,1)S(1)} %get-tuple-element.29), channel_id=1, source_target_pairs={{0,1},{1,0},{2,3},{3,2},{4,5},{5,4},{6,7},{7,6},{8,9},{9,8},{10,11... | collective-permute-start | bytes 983048 | tf_op jit(solution)/shard_map/ppermute | solution.py:56
  15.7 9.5 %collective-permute-start.5 = (bf16[528,256]{1,0:T(8,128)(2,1)S(1)}, bf16[528,256]{1,0:T(8,128)(2,1)}, u32[]{:S(2)}, u32[]{:S(2)}) collective-permute-start(bf16[528,256]{1,0:T(8,128)(2,1)S(1)} %pack.1.refs_0_), channel_id=1, source_target_pairs={{0,28},{4,0},{8,4},{12,8},{16,12},{20,16},{24,20},{28,24},{1,29},{... | collective-permute-start | bytes 811016 | tf_op jit(solution)/shard_map/ppermute | solution.py:555
  19.4 15.4 %copy-start.10 = (bf16[528,256]{1,0:T(8,128)(2,1)}, bf16[528,256]{1,0:T(8,128)(2,1)S(1)}, u32[]{:S(2)}) copy-start(bf16[528,256]{1,0:T(8,128)(2,1)S(1)} %collective-permute-done.3.refs_1_) | copy-start | bytes 811012
  19.4 9.3 %collective-permute-start.4 = (bf16[528,256]{1,0:T(8,128)(2,1)S(1)}, bf16[528,256]{1,0:T(8,128)(2,1)}, u32[]{:S(2)}, u32[]{:S(2)}) collective-permute-start(bf16[528,256]{1,0:T(8,128)(2,1)S(1)} %collective-permute-done.3.refs_1_), channel_id=1, source_target_pairs={{0,4},{4,8},{8,12},{12,16},{16,20},{20,24},{24,28},{28,0},{1,5},{5... | collective-permute-start | bytes 811016 | tf_op jit(solution)/shard_map/ppermute | solution.py:552
  20.8 8.6 %collective-permute-start.1 = (bf16[288,512]{1,0:T(8,128)(2,1)S(1)}, bf16[288,512]{1,0:T(8,128)(2,1)S(1)}, u32[]{:S(2)}, u32[]{:S(2)}) collective-permute-start(bf16[288,512]{1,0:T(8,128)(2,1)S(1)} %get-tuple-element.31), channel_id=1, source_target_pairs={{0,2},{2,0},{1,3},{3,1},{4,6},{6,4},{5,7},{7,5},{8,10},{10,8},{9,1... | collective-permute-start | bytes 884744 | tf_op jit(solution)/shard_map/ppermute | solution.py:56
  25.3 21.0 %collective-permute-start.6 = (bf16[528,256]{1,0:T(8,128)(2,1)}, bf16[528,256]{1,0:T(8,128)(2,1)}, u32[]{:S(2)}, u32[]{:S(2)}) collective-permute-start(bf16[528,256]{1,0:T(8,128)(2,1)} %collective-permute-done.5.refs_3_), channel_id=1, source_target_pairs={{0,28},{4,0},{8,4},{12,8},{16,12},{20,16},{24,20},{28,24},{1,29},{... | collective-permute-start | bytes 811016 | tf_op jit(solution)/shard_map/ppermute | solution.py:555
  28.8 19.7 %collective-permute-start.7 = (bf16[528,256]{1,0:T(8,128)(2,1)}, bf16[528,256]{1,0:T(8,128)(2,1)}, u32[]{:S(2)}, u32[]{:S(2)}) collective-permute-start(bf16[528,256]{1,0:T(8,128)(2,1)} %collective-permute-done.4.refs_2_), channel_id=1, source_target_pairs={{0,4},{4,8},{8,12},{12,16},{16,20},{20,24},{24,28},{28,0},{1,5},{5... | collective-permute-start | bytes 811016 | tf_op jit(solution)/shard_map/ppermute | solution.py:552
  30.4 20.8 %collective-permute-start.2 = (bf16[256,512]{1,0:T(8,128)(2,1)}, bf16[256,512]{1,0:T(8,128)(2,1)}, u32[]{:S(2)}, u32[]{:S(2)}) collective-permute-start(bf16[256,512]{1,0:T(8,128)(2,1)} %get-tuple-element.32.near), channel_id=1, source_target_pairs={{0,1},{1,0},{2,3},{3,2},{4,5},{5,4},{6,7},{7,6},{8,9},{9,8},{10,11... | collective-permute-start | bytes 786440 | tf_op jit(solution)/shard_map/ppermute | solution.py:56
  31.5 2.2 %copy-start.1 = (bf16[256,8192]{1,0:T(8,128)(2,1)S(1)}, bf16[256,8192]{1,0:T(8,128)(2,1)}, u32[]{:S(2)}) copy-start(bf16[256,8192]{1,0:T(8,128)(2,1)} %weight.1) | copy-start | bytes 12582916
  34.8 1.0 copy-start.8
  35.8 1.0 copy-start.9
  36.8 56.9 %collective-permute-start.16 = (bf16[256,2048]{1,0:T(8,128)(2,1)}, bf16[256,2048]{1,0:T(8,128)(2,1)S(1)}, u32[]{:S(2)}, u32[]{:S(2)}) collective-permute-start(bf16[256,2048]{1,0:T(8,128)(2,1)} %get-tuple-element.42), channel_id=1, source_target_pairs={{0,64},{32,96},{64,0},{96,32},{1,65},{33,97},{65,1},{97,33},{2,66}... | collective-permute-start | bytes 3145736 | tf_op jit(solution)/shard_map/ppermute | solution.py:560
  39.7 28.4 %all-to-all-start = ((bf16[8,64,256]{2,1,0:T(8,128)(2,1)}), bf16[8,64,256]{2,1,0:T(8,128)(2,1)}, u32[]{:S(2)}, u32[]{:S(2)}) async-start(bf16[8,64,256]{2,1,0:T(8,128)(2,1)} %get-tuple-element.33.own), calls=%async_computation | async-start | bytes 524288 | tf_op jit(solution)/shard_map/all_to_all | solution.py:577
  45.8 50.3 %collective-permute-start.17 = (bf16[256,2048]{1,0:T(8,128)(2,1)}, bf16[256,2048]{1,0:T(8,128)(2,1)S(1)}, u32[]{:S(2)}, u32[]{:S(2)}) collective-permute-start(bf16[256,2048]{1,0:T(8,128)(2,1)} %copy-done.9), channel_id=1, source_target_pairs={{0,32},{32,64},{64,96},{96,0},{1,33},{33,65},{65,97},{97,1},{2,34}... | collective-permute-start | bytes 3145736 | tf_op jit(solution)/shard_map/ppermute | solution.py:560
  46.2 49.9 %collective-permute-start.18 = (bf16[256,2048]{1,0:T(8,128)(2,1)}, bf16[256,2048]{1,0:T(8,128)(2,1)}, u32[]{:S(2)}, u32[]{:S(2)}) collective-permute-start(bf16[256,2048]{1,0:T(8,128)(2,1)} %copy-done.8), channel_id=1, source_target_pairs={{0,96},{32,0},{64,32},{96,64},{1,97},{33,1},{65,33},{97,65},{2,98}... | collective-permute-start | bytes 3145736 | tf_op jit(solution)/shard_map/ppermute | solution.py:560
  48.5 18.9 %collective-permute-start.8 = (bf16[528,256]{1,0:T(8,128)(2,1)}, bf16[528,256]{1,0:T(8,128)(2,1)S(1)}, u32[]{:S(2)}, u32[]{:S(2)}) collective-permute-start(bf16[528,256]{1,0:T(8,128)(2,1)} %collective-permute-done.6.refs_4_), channel_id=1, source_target_pairs={{0,28},{4,0},{8,4},{12,8},{16,12},{20,16},{24,20},{28,24},{1,29},{... | collective-permute-start | bytes 811016 | tf_op jit(solution)/shard_map/ppermute | solution.py:555
  51.2 16.9 %collective-permute-start.9 = (bf16[528,256]{1,0:T(8,128)(2,1)}, bf16[528,256]{1,0:T(8,128)(2,1)}, u32[]{:S(2)}, u32[]{:S(2)}) collective-permute-start(bf16[528,256]{1,0:T(8,128)(2,1)} %collective-permute-done.7.refs_0_), channel_id=1, source_target_pairs={{0,4},{4,8},{8,12},{12,16},{16,20},{20,24},{24,28},{28,0},{1,5},{5... | collective-permute-start | bytes 811016 | tf_op jit(solution)/shard_map/ppermute | solution.py:552
  51.2 1.0 copy-start.11
  64.2 1.4 %copy-start.15 = (f32[2048,256]{1,0:T(8,128)}, f32[2048,256]{1,0:T(8,128)S(1)}, u32[]{:S(2)}) copy-start(f32[2048,256]{1,0:T(8,128)S(1)} %get-tuple-element.35.acc_in) | copy-start | bytes 6291460
  65.5 1.0 copy-start.17
  66.5 0.8 copy-start.19
  67.4 0.7 copy-start.12
  68.1 1.0 copy-start.13
  69.1 1.6 %copy-start.16 = (f32[2048,256]{1,0:T(8,128)S(1)}, f32[2048,256]{1,0:T(8,128)}, u32[]{:S(2)}) copy-start(f32[2048,256]{1,0:T(8,128)} %copy-done.15) | copy-start | bytes 6291460
  70.6 1.2 %copy-start.18 = (f32[2048,128]{1,0:T(8,128)S(1)}, f32[2048,128]{1,0:T(8,128)}, u32[]{:S(2)}) copy-start(f32[2048,128]{1,0:T(8,128)} %copy-done.17) | copy-start | bytes 3145732
  71.9 1.0 copy-start.20
  82.5 3.0 %collective-permute-start.10 = (bf16[272,256]{1,0:T(8,128)(2,1)S(1)}, bf16[272,256]{1,0:T(8,128)(2,1)S(1)}, u32[]{:S(2)}, u32[]{:S(2)}) collective-permute-start(bf16[272,256]{1,0:T(8,128)(2,1)S(1)} %get-tuple-element.38), channel_id=1, source_target_pairs={{0,1},{1,0},{2,3},{3,2},{4,5},{5,4},{6,7},{7,6},{8,9},{9,8},{10,11... | collective-permute-start | bytes 417800 | tf_op jit(solution)/shard_map/ppermute | solution.py:56
  84.3 5.2 %collective-permute-start.11 = (bf16[272,256]{1,0:T(8,128)(2,1)S(1)}, bf16[272,256]{1,0:T(8,128)(2,1)S(1)}, u32[]{:S(2)}, u32[]{:S(2)}) collective-permute-start(bf16[272,256]{1,0:T(8,128)(2,1)S(1)} %get-tuple-element.39), channel_id=1, source_target_pairs={{0,2},{2,0},{1,3},{3,1},{4,6},{6,4},{5,7},{7,5},{8,10},{10,8},{9,1... | collective-permute-start | bytes 417800 | tf_op jit(solution)/shard_map/ppermute | solution.py:56
  85.5 7.2 %collective-permute-start.12 = (bf16[272,256]{1,0:T(8,128)(2,1)S(1)}, bf16[272,256]{1,0:T(8,128)(2,1)S(1)}, u32[]{:S(2)}, u32[]{:S(2)}) collective-permute-start(bf16[272,256]{1,0:T(8,128)(2,1)S(1)} %get-tuple-element.40), channel_id=1, source_target_pairs={{0,3},{1,2},{2,1},{3,0},{4,7},{5,6},{6,5},{7,4},{8,11},{9,10},{10,... | collective-permute-start | bytes 417800 | tf_op jit(solution)/shard_map/ppermute | solution.py:587
  93.2 6.5 %collective-permute-start.13 = (bf16[256,256]{1,0:T(8,128)(2,1)S(1)}, bf16[256,256]{1,0:T(8,128)(2,1)S(1)}, u32[]{:S(2)}, u32[]{:S(2)}) collective-permute-start(bf16[256,256]{1,0:T(8,128)(2,1)S(1)} %merge.1.refs_0_), channel_id=1, source_target_pairs={{0,64},{32,96},{64,0},{96,32},{1,65},{33,97},{65,1},{97,33},{2,66}... | collective-permute-start | bytes 393224 | tf_op jit(solution)/shard_map/ppermute | solution.py:591
  93.3 9.3 %collective-permute-start.14 = (bf16[256,256]{1,0:T(8,128)(2,1)S(1)}, bf16[256,256]{1,0:T(8,128)(2,1)S(1)}, u32[]{:S(2)}, u32[]{:S(2)}) collective-permute-start(bf16[256,256]{1,0:T(8,128)(2,1)S(1)} %merge.1.refs_0_), channel_id=1, source_target_pairs={{0,32},{32,64},{64,96},{96,0},{1,33},{33,65},{65,97},{97,1},{2,34}... | collective-permute-start | bytes 393224 | tf_op jit(solution)/shard_map/ppermute | solution.py:591
  93.7 8.9 %collective-permute-start.15 = (bf16[256,256]{1,0:T(8,128)(2,1)S(1)}, bf16[256,256]{1,0:T(8,128)(2,1)S(1)}, u32[]{:S(2)}, u32[]{:S(2)}) collective-permute-start(bf16[256,256]{1,0:T(8,128)(2,1)S(1)} %merge.1.refs_0_), channel_id=1, source_target_pairs={{0,96},{32,0},{64,32},{96,64},{1,97},{33,1},{65,33},{97,65},{2,98}... | collective-permute-start | bytes 393224 | tf_op jit(solution)/shard_map/ppermute | solution.py:591
  105.2 2.5 %collective-permute-start.19 = (bf16[256,1024]{1,0:T(8,128)(2,1)S(1)}, bf16[256,1024]{1,0:T(8,128)(2,1)S(1)}, u32[]{:S(2)}, u32[]{:S(2)}) collective-permute-start(bf16[256,1024]{1,0:T(8,128)(2,1)S(1)} %get-tuple-element.46), channel_id=1, source_target_pairs={{0,1},{1,0},{2,3},{3,2},{4,5},{5,4},{6,7},{7,6},{8,9},{9,8},{10,11... | collective-permute-start | bytes 1572872 | tf_op jit(solution)/shard_map/ppermute | solution.py:56
  107.9 6.3 %collective-permute-start.20 = (bf16[256,256]{1,0:T(8,128)(2,1)S(1)}, bf16[256,256]{1,0:T(8,128)(2,1)S(1)}, u32[]{:S(2)}, u32[]{:S(2)}) collective-permute-start(bf16[256,256]{1,0:T(8,128)(2,1)S(1)} %get-tuple-element.48), channel_id=1, source_target_pairs={{0,128},{2,130},{128,0},{130,2},{1,129},{3,131},{129,1},{131,3},{4... | collective-permute-start | bytes 393224 | tf_op jit(solution)/shard_map/ppermute | solution.py:596
  110.7 6.7 %collective-permute-start.21 = (bf16[256,256]{1,0:T(8,128)(2,1)S(1)}, bf16[256,256]{1,0:T(8,128)(2,1)S(1)}, u32[]{:S(2)}, u32[]{:S(2)}) collective-permute-start(bf16[256,256]{1,0:T(8,128)(2,1)S(1)} %get-tuple-element.49), channel_id=1, source_target_pairs={{0,2},{2,128},{128,130},{130,0},{1,3},{3,129},{129,131},{131,1},{4... | collective-permute-start | bytes 393224 | tf_op jit(solution)/shard_map/ppermute | solution.py:596
  111.0 6.4 %collective-permute-start.22 = (bf16[256,256]{1,0:T(8,128)(2,1)S(1)}, bf16[256,256]{1,0:T(8,128)(2,1)S(1)}, u32[]{:S(2)}, u32[]{:S(2)}) collective-permute-start(bf16[256,256]{1,0:T(8,128)(2,1)S(1)} %get-tuple-element.50), channel_id=1, source_target_pairs={{0,130},{2,0},{128,2},{130,128},{1,131},{3,1},{129,3},{131,129},{4... | collective-permute-start | bytes 393224 | tf_op jit(solution)/shard_map/ppermute | solution.py:596

commit v2 on v1

--- a/solution.py
+++ b/solution.py
@@ -25,7 +25,8 @@
 PAIR = 2 * HD
 NEW = 64
 QUARTER = 512
-LOAD = QUARTER + 16
+HALF = ROWS + 16
+LOAD = 2 * HALF
 MSG = ROWS + 16
 TALL = 1024
 EXPONENT = math.log2(math.e) / math.sqrt(HD)
@@ -33,14 +34,14 @@
 
 VMEM = pl.BlockSpec(memory_space=pltpu.VMEM)
 SMEM = pl.BlockSpec(memory_space=pltpu.SMEM)
-ANY = pl.BlockSpec(memory_space=pl.ANY)
+HBM = pl.BlockSpec(memory_space=pltpu.HBM)
 
 
 def shaped(shape, dtype):
     return jax.ShapeDtypeStruct(shape, dtype)
 
 
-def params(mib):
+def params(mib=60):
     return pltpu.CompilerParams(vmem_limit_bytes=mib * 2**20)
 
 
@@ -60,24 +61,32 @@
     return 2 * lax.axis_index("hid_0") + lax.axis_index("hid_1")
 
 
+def fetch(pairs, sems):
+    copies = [
+        pltpu.make_async_copy(source, target, sems.at[i])
+        for i, (source, target) in enumerate(pairs)
+    ]
+    for copy in copies:
+        copy.start()
+    return copies
+
+
 def pack_kernel(places, keys, values, out, codes, sems):
     quarter = hid_index()
-    rows = pl.ds(pl.multiple_of(quarter * QUARTER, QUARTER), QUARTER)
-    copies = [
-        pltpu.make_async_copy(keys.at[rows, :], out.at[:QUARTER, :HD], sems.at[0]),
-        pltpu.make_async_copy(values.at[rows, :], out.at[:QUARTER, HD:], sems.at[1]),
-        pltpu.make_async_copy(codes, out.at[QUARTER:, :], sems.at[2]),
-    ]
-    copies[0].start()
-    copies[1].start()
+    pairs = []
+    for b in range(2):
+        rows = pl.ds(pl.multiple_of(quarter * QUARTER + b * ROWS, ROWS), ROWS)
+        to = slice(b * HALF, b * HALF + ROWS)
+        pairs.append((keys.at[rows, :], out.at[to, :HD]))
+        pairs.append((values.at[rows, :], out.at[to, HD:]))
+    copies = fetch(pairs, sems.at[:4])
     lane = lax.broadcasted_iota(jnp.int32, (16, PAIR), 1)
-    table = jnp.zeros((16, PAIR), jnp.int32)
     for b in range(2):
         place = places[quarter * 2 + b]
-        table = jnp.where(lane == 2 * b, place >> 1, table)
-        table = jnp.where(lane == 2 * b + 1, place & 1, table)
-    codes[...] = table.astype(F32).astype(BF16)
-    copies[2].start()
+        table = jnp.where(lane == 0, place >> 1, jnp.where(lane == 1, place & 1, 0))
+        codes[b] = table.astype(F32).astype(BF16)
+    pairs = [(codes.at[b], out.at[b * HALF + ROWS : (b + 1) * HALF, :]) for b in range(2)]
+    copies += fetch(pairs, sems.at[4:])
     for copy in copies:
         copy.wait()
 
@@ -86,10 +95,10 @@
     return pl.pallas_call(
         pack_kernel,
         out_shape=shaped((LOAD, PAIR), BF16),
-        in_specs=[SMEM, ANY, ANY],
-        out_specs=ANY,
-        scratch_shapes=[pltpu.VMEM((16, PAIR), BF16), pltpu.SemaphoreType.DMA((3,))],
-        compiler_params=params(4),
+        in_specs=[SMEM, HBM, HBM],
+        out_specs=HBM,
+        scratch_shapes=[pltpu.VMEM((2, 16, PAIR), BF16), pltpu.SemaphoreType.DMA((6,))],
+        compiler_params=params(),
         cost_estimate=cost(moved=2**19),
         name="pack",
     )(places, keys, values)
@@ -120,67 +129,69 @@
     return pl.pallas_call(
         columns_kernel,
         out_shape=[shaped((ROWS, 2048), BF16)] * 4,
-        in_specs=[ANY],
-        out_specs=[ANY] * 4,
+        in_specs=[HBM],
+        out_specs=[HBM] * 4,
         scratch_shapes=[pltpu.SemaphoreType.DMA((8,))],
-        compiler_params=params(4),
+        compiler_params=params(),
         cost_estimate=cost(moved=2**23),
         name="columns",
     )(weight)
 
 
-def first_kernel(core_ref, tokens, query, key, value, send, keep, fresh):
-    j = pl.program_id(0)
-    core = core_ref[0]
-    part = jnp.dot(tokens[...], query[...], preferred_element_type=F32)
+def first_kernel(
+    tokens, query, key, value, send, keep, tok, tiles, kv, fresh, sems
+):
+    core = lax.axis_index("hid_1")
+    pairs = [(tokens, tok)]
+    for t in range(4):
+        side = 1 - core if t < 2 else core
+        cols = pl.ds(pl.multiple_of(side * 512 + (t % 2) * ROWS, ROWS), ROWS)
+        pairs.append((query.at[:, cols], tiles.at[t]))
+        if t == 1:
+            pairs.append((key, kv.at[0]))
+            pairs.append((value, kv.at[1]))
+    copies = fetch(pairs, sems)
+    copies[0].wait()
+
+    def part(t):
+        return jnp.dot(tok[...], tiles[t], preferred_element_type=F32)
+
     for t in range(2):
-        cols = slice(t * ROWS, (t + 1) * ROWS)
-
-        @pl.when(j == t)
-        def _(cols=cols):
-            send[:ROWS, cols] = part.astype(BF16)
-
-        @pl.when(j == 2 + t)
-        def _(cols=cols):
-            keep[:ROWS, cols] = part
-
-    @pl.when(j == 0)
-    def _():
-        fresh[:, :HD] = jnp.dot(tokens[...], key[...], preferred_element_type=F32)
-        fresh[:, HD:] = jnp.dot(tokens[...], value[...], preferred_element_type=F32)
-        for t in range(2):
-            cols = slice(t * PAIR, (t + 1) * PAIR)
-            far = pl.ds(pl.multiple_of((1 - core) * 128 + t * NEW, NEW), NEW)
-            near = pl.ds(pl.multiple_of(core * 128 + t * NEW, NEW), NEW)
-            send[ROWS:, cols] = fresh[far, :].astype(BF16)
-            keep[ROWS:, cols] = fresh[near, :]
-
-
-def first(core, tokens, query, key, value):
-    def tile(j, core):
-        return (0, jnp.where(j < 2, (1 - core[0]) * 2 + j, core[0] * 2 + j - 2))
-
-    whole = lambda a: pl.BlockSpec(a.shape, lambda j, core: (0, 0))
-    grid_spec = pltpu.PrefetchScalarGridSpec(
-        num_scalar_prefetch=1,
-        grid=(4,),
-        in_specs=[
-            whole(tokens),
-            pl.BlockSpec((query.shape[0], ROWS), tile),
-            whole(key),
-            whole(value),
-        ],
-        out_specs=[pl.BlockSpec((320, 512), lambda j, core: (0, 0))] * 2,
-        scratch_shapes=[pltpu.VMEM((ROWS, PAIR), F32)],
-    )
+        copies[1 + t].wait()
+        send[:ROWS, t * ROWS : (t + 1) * ROWS] = part(t).astype(BF16)
+    copies[3].wait()
+    copies[4].wait()
+    both = jnp.concatenate([kv[0], kv[1]], axis=1)
+    fresh[...] = jnp.dot(tok[...], both, preferred_element_type=F32)
+    for t in range(2):
+        cols = slice(t * PAIR, (t + 1) * PAIR)
+        far = pl.ds(pl.multiple_of((1 - core) * 128 + t * NEW, NEW), NEW)
+        near = pl.ds(pl.multiple_of(core * 128 + t * NEW, NEW), NEW)
+        send[ROWS:, cols] = fresh[far, :].astype(BF16)
+        keep[ROWS:, cols] = fresh[near, :]
+    for t in range(2):
+        copies[5 + t].wait()
+        keep[:ROWS, t * ROWS : (t + 1) * ROWS] = part(2 + t)
+
+
+def first(tokens, query, key, value):
+    deep = tokens.shape[1]
     return pl.pallas_call(
         first_kernel,
         out_shape=[shaped((320, 512), BF16), shaped((320, 512), F32)],
-        grid_spec=grid_spec,
-        compiler_params=params(20),
+        in_specs=[HBM] * 4,
+        out_specs=[VMEM] * 2,
+        scratch_shapes=[
+            pltpu.VMEM((ROWS, deep), BF16),
+            pltpu.VMEM((4, deep, ROWS), BF16),
+            pltpu.VMEM((2, deep, HD), BF16),
+            pltpu.VMEM((ROWS, PAIR), F32),
+            pltpu.SemaphoreType.DMA((7,)),
+        ],
+        compiler_params=params(),
         cost_estimate=cost(flops=2 * 256 * 2048 * 1280, moved=6 * 2**20),
         name="first",
-    )(core, tokens, query, key, value)
+    )(tokens, query, key, value)
 
 
 def second_kernel(keep, got, send, onward):
@@ -241,27 +252,24 @@
     )(keep, got, cosine, sine)
 
 
-def gather_visible(mine, slabs, loads, new, keys, values, chunk):
+def gather_visible(mine, slabs, halves, new, keys, values, chunk):
     height = keys.shape[0]
     values[:, HD:] = jnp.ones((height, HD), BF16)
     n = jnp.int32(0)
     lane = lax.broadcasted_iota(jnp.int32, (16, HD), 1)
-    for load in loads:
-        codes = load[QUARTER:, :HD].astype(F32)
-        codes = jnp.where(lane % 2 == 0, 2.0, 1.0) * codes
-        for b in range(2):
-            part = jnp.where(lane // 2 == b, codes, 0.0)
-            place = jnp.max(part[:1] + pltpu.roll(part, HD - 1, 1)[:1]).astype(jnp.int32)
-            seen = place < mine
-
-            @pl.when(seen)
-            def _(load=load, b=b, n=n):
-                at = pl.ds(pl.multiple_of(n * NEW, NEW), ROWS)
-                rows = slice(b * ROWS, (b + 1) * ROWS)
-                keys[at, :] = load[rows, :HD]
-                values[at, :HD] = load[rows, HD:]
-
-            n = n + jnp.where(seen, ROWS // NEW, 0)
+    for load in halves:
+        codes = load[ROWS:, :HD].astype(F32)
+        codes = jnp.where(lane == 0, 2.0, 1.0) * codes
+        place = jnp.max(codes + pltpu.roll(codes, HD - 1, 1)).astype(jnp.int32)
+        seen = place < mine
+
+        @pl.when(seen)
+        def _(load=load, n=n):
+            at = pl.ds(pl.multiple_of(n * NEW, NEW), ROWS)
+            keys[at, :] = load[:ROWS, :HD]
+            values[at, :HD] = load[:ROWS, HD:]
+
+        n = n + jnp.where(seen, ROWS // NEW, 0)
     if new is not None:
         for z in range(8):
             seen = slabs[z] < mine
@@ -311,14 +319,30 @@
     return peak
 
 
-def near_kernel(
-    slabs, near, far, own, *refs, chunk, count
-):
-    loads, (q_out, acc_out, peak_out) = refs[:count], refs[count : count + 3]
-    keys, values, scores, peak_ref = refs[count + 3 :]
+def halves_of(buffers):
+    halves = []
+    for ref in buffers:
+        for b in range(ref.shape[0] // HALF):
+            halves.append(ref.at[b * HALF : (b + 1) * HALF, :])
+    return halves
+
+
+def near_kernel(slabs, near, far, notes, *refs, chunk, count):
+    sources, (q_out, acc_out, peak_out) = refs[:count], refs[count : count + 3]
+    refs = refs[count + 3 :]
+    near_in, far_in, own, *loads = refs[: 3 + count]
+    q_all, acc_all, peak_all, keys, values, scores, peak_ref, sems = refs[3 + count :]
+    pairs = list(zip(sources, loads))
+    pairs += [(notes.at[0], own), (near, near_in), (far, far_in)]
+    copies = fetch(pairs, sems.at[: count + 3])
     mine = slabs[lax.axis_index("key")]
     core = lax.axis_index("hid_1")
     x = lax.axis_index("hid_0")
+    for copy in copies[:count]:
+        copy.wait()
+    chunks = gather_visible(mine, None, halves_of(loads), None, keys, values, chunk)
+    for copy in copies[count:]:
+        copy.wait()
     for j in range(4):
         half = x if j < 2 else 1 - x
         parity = core if j % 2 == 0 else 1 - core
@@ -327,74 +351,91 @@
 
         @pl.when(half == core)
         def _(cols=cols, rows=rows):
-            both = near[:, cols]
-            q_out[rows[0], :] = both[:, :HD]
-            q_out[rows[1], :] = both[:, HD:]
+            both = near_in[:, cols]
+            q_all[rows[0], :] = both[:, :HD]
+            q_all[rows[1], :] = both[:, HD:]
 
         @pl.when(half != core)
         def _(cols=cols, rows=rows):
-            both = far[:, cols]
-            q_out[rows[0], :] = both[:, :HD]
-            q_out[rows[1], :] = both[:, HD:]
-
-    chunks = gather_visible(mine, None, loads, None, keys, values, chunk)
+            both = far_in[:, cols]
+            q_all[rows[0], :] = both[:, :HD]
+            q_all[rows[1], :] = both[:, HD:]
+
+    out = fetch([(q_all, q_out)], sems.at[count + 3 : count + 4])
     zeros = jnp.zeros((NEW, HD), BF16)
-    own_keys = jnp.concatenate([own[0, :, :HD], zeros], axis=0)
-    own_values = jnp.concatenate([own[0, :, HD:], zeros], axis=0)
+    own_keys = jnp.concatenate([own[:, :HD], zeros], axis=0)
+    own_values = jnp.concatenate([own[:, HD:], zeros], axis=0)
     own_values = jnp.concatenate([own_values, jnp.ones((HD, HD), BF16)], axis=1)
     row = lax.broadcasted_iota(jnp.int32, (TALL, HD), 0) % ROWS
     lane = lax.broadcasted_iota(jnp.int32, (TALL, HD), 1)
     visible = jnp.logical_and(lane < NEW, lane + new_offset() <= row)
-
-    def tall(step, carry):
-        at = pl.ds(pl.multiple_of(step * TALL, TALL), TALL)
-        q = q_out[at, :]
+    for step in range(8 * ROWS // TALL):
+        at = pl.ds(step * TALL, TALL)
+        q = q_all[at, :]
         s = lax.dot_general(q, own_keys, CONTRACT, preferred_element_type=F32)
         s = jnp.where(visible, s, NEGATIVE)
         peak_ref[...] = s
 
-        def before(peak):
+        def before(peak, s=s):
             p = jnp.where(visible, jnp.exp2((s - peak) * EXPONENT), 0.0)
             return jnp.dot(p.astype(BF16), own_values, preferred_element_type=F32)
 
         peak = attend(
-            q, peak_ref, chunks, keys, values, scores, chunk, acc_out.at[at, :], before
+            q, peak_ref, chunks, keys, values, scores, chunk, acc_all.at[at, :], before
         )
-        peak_out[at, :] = jnp.broadcast_to(peak, (TALL, HD))
-        return carry
-
-    lax.fori_loop(0, 8 * ROWS // TALL, tall, 0)
-
-
-def attend_near(slabs, near, far, own, loads):
+        peak_all[at, :] = jnp.broadcast_to(peak, (TALL, HD))
+        first_sem = count + 4 + 2 * step
+        out += fetch(
+            [
+                (acc_all.at[at, :], acc_out.at[at, :]),
+                (peak_all.at[at, :], peak_out.at[at, :]),
+            ],
+            sems.at[first_sem : first_sem + 2],
+        )
+    for copy in out:
+        copy.wait()
+
+
+def attend_near(slabs, near, far, notes, loads):
     count, chunk = len(loads), 1280
     height = count * QUARTER
+    state = [((8 * ROWS, HD), BF16), ((8 * ROWS, PAIR), F32), ((8 * ROWS, HD), F32)]
     return pl.pallas_call(
         functools.partial(near_kernel, chunk=chunk, count=count),
-        out_shape=[
-            shaped((8 * ROWS, HD), BF16),
-            shaped((8 * ROWS, PAIR), F32),
-            shaped((8 * ROWS, HD), F32),
-        ],
-        in_specs=[SMEM] + [VMEM] * (3 + count),
-        out_specs=[VMEM] * 3,
+        out_shape=[shaped(*s) for s in state],
+        in_specs=[SMEM] + [HBM] * (3 + count),
+        out_specs=[HBM] * 3,
         scratch_shapes=[
+            pltpu.VMEM((ROWS, 4 * HD), BF16),
+            pltpu.VMEM((ROWS, 4 * HD), BF16),
+            pltpu.VMEM((NEW, PAIR), BF16),
+            *[pltpu.VMEM((LOAD, PAIR), BF16)] * count,
+            *[pltpu.VMEM(*s) for s in state],
             pltpu.VMEM((height, HD), BF16),
             pltpu.VMEM((height, PAIR), BF16),
             pltpu.VMEM((height // chunk, TALL, chunk), F32),
             pltpu.VMEM((TALL, HD), F32),
+            pltpu.SemaphoreType.DMA((count + 4 + 2 * (8 * ROWS // TALL),)),
         ],
-        compiler_params=params(30),
+        compiler_params=params(),
         cost_estimate=cost(8 * ROWS * height * HD * 6, 2**23, 8 * ROWS * height),
         name="near",
-    )(slabs, near, far, own, *loads)
-
-
-def far_kernel(slabs, queries, acc_in, peak_in, new, *refs, chunk, count):
-    loads, outs = refs[:count], refs[count : count + 4]
-    keys, values, scores, peak_ref, acc = refs[count + 4 :]
+    )(slabs, near, far, notes, *loads)
+
+
+def far_kernel(slabs, *refs, chunk, count):
+    sources, outs = refs[: 4 + count], refs[4 + count : 8 + count]
+    refs = refs[8 + count :]
+    buffers = refs[: 4 + count]
+    queries, acc_in, peak_in, new, *loads = buffers
+    keys, values, scores, peak_ref, acc, sems = refs[4 + count :]
+    copies = fetch(list(zip(sources, buffers))[::-1], sems)
     mine = slabs[lax.axis_index("key")]
-    chunks = gather_visible(mine, slabs, loads, new, keys, values, chunk)
+    for copy in copies[: count + 1]:
+        copy.wait()
+    chunks = gather_visible(mine, slabs, halves_of(loads), new, keys, values, chunk)
+    for copy in copies[count + 1 :]:
+        copy.wait()
     where = lax.broadcasted_iota(jnp.int32, (16, ROWS), 0)
     for step in range(8 * ROWS // TALL):
         at = slice(step * TALL, (step + 1) * TALL)
@@ -428,24 +469,28 @@
 
 
 def attend_far(slabs, queries, acc, peak, new, loads):
+    operands = [queries, acc, peak, new, *loads]
     count, chunk = len(loads), 1024
-    height = -(-(count * QUARTER + 8 * NEW) // chunk) * chunk
+    height = sum(a.shape[0] // HALF * ROWS for a in loads) + 8 * NEW
+    height = -(-height // chunk) * chunk
     return pl.pallas_call(
         functools.partial(far_kernel, chunk=chunk, count=count),
         out_shape=[shaped((MSG, PAIR), BF16)] * 4,
-        in_specs=[SMEM] + [VMEM] * (4 + count),
+        in_specs=[SMEM] + [HBM] * len(operands),
         out_specs=[VMEM] * 4,
         scratch_shapes=[
+            *[pltpu.VMEM(a.shape, a.dtype) for a in operands],
             pltpu.VMEM((height, HD), BF16),
             pltpu.VMEM((height, PAIR), BF16),
             pltpu.VMEM((height // chunk, TALL, chunk), F32),
             pltpu.VMEM((TALL, HD), F32),
             pltpu.VMEM((TALL, PAIR), F32),
+            pltpu.SemaphoreType.DMA((len(operands),)),
         ],
-        compiler_params=params(30),
+        compiler_params=params(),
         cost_estimate=cost(8 * ROWS * height * HD * 6, 2**23, 8 * ROWS * height),
         name="far",
-    )(slabs, queries, acc, peak, new, *loads)
+    )(slabs, *operands)
 
 
 def merge_kernel(*refs):
@@ -544,24 +589,20 @@
     slab_places,
 ):
     key_index = lax.axis_index("key")
-    core = lax.axis_index("hid_1")
 
     load = pack(cache_places, key_cache.reshape(-1, HD), value_cache.reshape(-1, HD))
-    up = [load]
-    for _ in range(4):
-        up.append(lax.ppermute(up[-1], "key", shift(8, 1)))
-    down = [load]
-    for _ in range(3):
-        down.append(lax.ppermute(down[-1], "key", shift(8, -1)))
+
+    def along(array, by):
+        return lax.ppermute(array, "key", shift(8, by))
+
+    near_loads = [load] + [along(load, by) for by in (2, -2, 1, -1)]
 
     pieces = columns(output_weight)
     weights = [pieces[3]]
     for piece, by in zip(pieces, (2, 1, 3)):
         weights.append(lax.ppermute(piece, "head_1", shift(4, by)))
 
-    send, keep = first(
-        core.astype(jnp.int32).reshape(1), tokens, query_weight, key_weight, value_weight
-    )
+    send, keep = first(tokens, query_weight, key_weight, value_weight)
     send, keep = second(keep, swap(send, "hid_1"))
     got = swap(send, "hid_0")
 
@@ -576,8 +617,10 @@
 
     new = lax.all_to_all(notes, "key", split_axis=0, concat_axis=0, tiled=True)
 
-    state = attend_near(slab_places, queries, far, notes, up[:3] + down[1:3])
-    parts = attend_far(slab_places, *state, new, [up[3], down[3], up[4]])
+    _, up, down, _, _ = near_loads
+    far_loads = [along(up[:HALF], 2), along(down[HALF:], -2), along(up, 1), along(down, -1)]
+    state = attend_near(slab_places, queries, far, notes, near_loads)
+    parts = attend_far(slab_places, *state, new, far_loads)
     flip = [(0, 3), (1, 2), (2, 1), (3, 0)]
     merged = merge(
         [

time: 119 us -> 248 us (2.08)
  the two profiles are of different devices: /device:TPU:1 before, /device:TPU:70 now
where the time goes in v2:
time: 248 us; the launch traced here: 246 us
  Pallas kernels  173 us (70%)
  starting transfers between devices  38.1 us (15%)
  waiting for transfers between devices  29.5 us (12%)
  local copies, waits for them, and re-layouts  3.4 us (1%)
    pallas_call x1, Pallas kernels, columns(): pl.pallas_call(columns_kernel, out_shape=[shaped((ROWS, 2048), BF16)] * 4...  128 us
    ppermute x6, waiting for transfers between devices, swap(): return lax.ppermute(array, axis, shift(2, 1))  14.3 us
    ppermute x8, starting transfers between devices, along(): return lax.ppermute(array, 'key', shift(8, by))  13.8 us
    pallas_call x1, Pallas kernels, attend_near(): pl.pallas_call(functools.partial(near_kernel, chunk=chunk, count=count),...  13.7 us
    pallas_call x1, Pallas kernels, attend_far(): pl.pallas_call(functools.partial(far_kernel, chunk=chunk, count=count), o...  11.2 us
    pallas_call x1, Pallas kernels, pack(): pl.pallas_call(pack_kernel, out_shape=shaped((LOAD, PAIR), BF16), in_spec...  9.77 us
    all_to_all x1, starting transfers between devices, body(): new = lax.all_to_all(notes, 'key', split_axis=0, concat_axis=0, tiled=True)  7.74 us
    ppermute x3, waiting for transfers between devices, body(): out = out + lax.ppermute(blocks[by - 1], ALONG_X, shift(4, by)).astype(F32)  6.66 us
  transfers between devices with their start and end apart: 25, of which 9 were waited for; matrix products, arithmetic and copies ran while one was open for 0% of the time, Pallas kernels for 67%

profile of v2, /device:TPU:70, one launch (start us, length us, event | category | flops | bytes accessed | tf_op | source)
XLA Modules:
  0.0 246.0 jit_solution(11479193408390149337)
XLA Ops:
  0.0 5.7 %first.1 = (bf16[320,512]{1,0:T(8,128)(2,1)}, f32[320,512]{1,0:T(8,128)}) custom-call(bf16[256,2048]{1,0:T(8,128)(2,1)} %tokens.1, bf16[2048,1024]{1,0:T(8,128)(2,1)} %query.1, bf16[2048,128]{1,0:T(8,128)(2,1)} %key.1, bf16[2048,128]{1,0:T(8,128)(2,1)} %value.1), custom_call_target="tpu_custom_call" | custom-call | flops 1342177280 | bytes 6291456 | tf_op jit(solution)/shard_map/first/pallas_call | solution.py:179
  5.7 0.1 collective-permute-start
  5.8 9.8 %pack.1.refs_0_ = bf16[544,256]{1,0:T(8,128)(2,1)} custom-call(s32[8]{0:T(128)} %places.1, bf16[2048,128]{1,0:T(8,128)(2,1)} %bitcast.3, bf16[2048,128]{1,0:T(8,128)(2,1)} %bitcast.4), custom_call_target="tpu_custom_call" | custom-call | bytes 524288 | tf_op jit(solution)/shard_map/pack/pallas_call | solution.py:95
  15.6 4.6 %collective-permute-start.3 = (bf16[544,256]{1,0:T(8,128)(2,1)}, bf16[544,256]{1,0:T(8,128)(2,1)S(1)}, u32[]{:S(2)}, u32[]{:S(2)}) collective-permute-start(bf16[544,256]{1,0:T(8,128)(2,1)} %pack.1.refs_0_), channel_id=1, source_target_pairs={{0,8},{4,12},{8,16},{12,20},{16,24},{20,28},{24,0},{28,4},{1,9},{5... | collective-permute-start | bytes 835592 | tf_op jit(solution)/shard_map/ppermute | solution.py:596
  20.2 1.0 collective-permute-start.5
  21.2 1.0 collective-permute-start.6
  22.2 0.6 dynamic_slice.3
  23.5 1.1 copy-done.1
  24.5 0.1 second.1
  24.6 0.9 collective-permute-start.1
  25.5 0.5 fusion
  26.1 7.2 %collective-permute-done.1.got = bf16[288,512]{1,0:T(8,128)(2,1)S(1)} collective-permute-done((bf16[288,512]{1,0:T(8,128)(2,1)S(1)}, bf16[288,512]{1,0:T(8,128)(2,1)S(1)}, u32[]{:S(2)}, u32[]{:S(2)}) %collective-permute-start.1) | collective-permute-done | bytes 294944 | tf_op jit(solution)/shard_map/ppermute | solution.py:57
  33.3 0.9 rotated.1
  34.2 5.1 %collective-permute-start.7 = (bf16[272,256]{1,0:T(8,128)(2,1)S(1)}, bf16[272,256]{1,0:T(8,128)(2,1)S(1)}, u32[]{:S(2)}, u32[]{:S(2)}) collective-permute-start(bf16[272,256]{1,0:T(8,128)(2,1)S(1)} %slice.8), channel_id=1, source_target_pairs={{0,8},{4,12},{8,16},{12,20},{16,24},{20,28},{24,0},{28,4},{1,9},{5... | collective-permute-start | bytes 417800 | tf_op jit(solution)/shard_map/ppermute | solution.py:596
  39.4 0.1 collective-permute-start.8
  39.5 128.2 %columns.1 = (bf16[256,2048]{1,0:T(8,128)(2,1)}, bf16[256,2048]{1,0:T(8,128)(2,1)}, bf16[256,2048]{1,0:T(8,128)(2,1)}, bf16[256,2048]{1,0:T(8,128)(2,1)}) custom-call(bf16[256,8192]{1,0:T(8,128)(2,1)} %weight.1), custom_call_target="tpu_custom_call" | custom-call | bytes 8388608 | tf_op jit(solution)/shard_map/columns/pallas_call | solution.py:129
  167.7 3.3 %collective-permute-start.17 = (bf16[256,2048]{1,0:T(8,128)(2,1)}, bf16[256,2048]{1,0:T(8,128)(2,1)S(1)}, u32[]{:S(2)}, u32[]{:S(2)}) collective-permute-start(bf16[256,2048]{1,0:T(8,128)(2,1)} %get-tuple-element.42), channel_id=1, source_target_pairs={{0,64},{32,96},{64,0},{96,32},{1,65},{33,97},{65,1},{97,33},{2,66}... | collective-permute-start | bytes 3145736 | tf_op jit(solution)/shard_map/ppermute | solution.py:603
  171.0 7.7 %all-to-all-start = ((bf16[8,64,256]{2,1,0:T(8,128)(2,1)}), bf16[8,64,256]{2,1,0:T(8,128)(2,1)S(1)}, u32[]{:S(2)}, u32[]{:S(2)}) async-start(bf16[8,64,256]{2,1,0:T(8,128)(2,1)} %get-tuple-element.33.notes), calls=%async_computation | async-start | bytes 524288 | tf_op jit(solution)/shard_map/all_to_all | solution.py:618
  178.8 0.8 collective-permute-start.18
  179.5 2.6 %collective-permute-start.19 = (bf16[256,2048]{1,0:T(8,128)(2,1)}, bf16[256,2048]{1,0:T(8,128)(2,1)}, u32[]{:S(2)}, u32[]{:S(2)}) collective-permute-start(bf16[256,2048]{1,0:T(8,128)(2,1)} %get-tuple-element.44), channel_id=1, source_target_pairs={{0,96},{32,0},{64,32},{96,64},{1,97},{33,1},{65,33},{97,65},{2,98}... | collective-permute-start | bytes 3145736 | tf_op jit(solution)/shard_map/ppermute | solution.py:603
  182.1 0.6 collective-permute-start.10
  182.7 1.5 collective-permute-start.9
  184.1 13.7 %near.1 = (bf16[2048,128]{1,0:T(8,128)(2,1)}, f32[2048,256]{1,0:T(8,128)}, f32[2048,128]{1,0:T(8,128)}) custom-call(s32[8]{0:T(128)} %slabs.3, bf16[256,512]{1,0:T(8,128)(2,1)} %copy-done.3, bf16[256,512]{1,0:T(8,128)(2,1)} %collective-permute-done.2.far, bf16[8,64,256]{2,1,0:T(8,128)(2,1)} %get-tuple-element.33.notes, bf16[544,256]{1,0:T(8,128)(2,1)} %pack.1.refs_0_, ...), custom_call_target="tpu_custom_call" | custom-call | flops 4026531840 | bytes 8388608 | tf_op jit(solution)/shard_map/near/pallas_call | solution.py:403
  197.9 0.7 copy-done.10
  198.6 0.1 copy-done.4
  198.7 11.2 %far.1 = (bf16[272,256]{1,0:T(8,128)(2,1)}, bf16[272,256]{1,0:T(8,128)(2,1)}, bf16[272,256]{1,0:T(8,128)(2,1)}, bf16[272,256]{1,0:T(8,128)(2,1)}) custom-call(s32[8]{0:T(128)} %slabs.3, bf16[2048,128]{1,0:T(8,128)(2,1)} %get-tuple-element.34.refs_0_, f32[2048,256]{1,0:T(8,128)} %get-tuple-element.35.refs_1_, f32[2048,128]{1,0:T(8,128)} %get-tuple-element.36.refs_2_, ...), custom_call_target="tpu_custom_call" | custom-call | flops 3221225472 | bytes 8388608 | tf_op jit(solution)/shard_map/far/pallas_call | solution.py:476
  209.9 0.1 collective-permute-start.11
  210.0 0.9 collective-permute-start.12
  210.9 0.6 collective-permute-done.11.refs_1_
  211.5 0.6 collective-permute-start.13
  212.1 4.6 %collective-permute-done.12.refs_2_ = bf16[272,256]{1,0:T(8,128)(2,1)S(1)} collective-permute-done((bf16[272,256]{1,0:T(8,128)(2,1)}, bf16[272,256]{1,0:T(8,128)(2,1)S(1)}, u32[]{:S(2)}, u32[]{:S(2)}) %collective-permute-start.12) | collective-permute-done | bytes 139296 | tf_op jit(solution)/shard_map/ppermute | solution.py:57
  216.8 2.0 collective-permute-done.13.refs_3_
  218.8 0.9 copy-done.2
  219.7 0.6 merge.1.refs_0_
  220.3 0.3 collective-permute-start.14
  220.6 0.9 collective-permute-start.15
  221.5 2.4 collective-permute-start.16
  223.9 4.5 %collective-permute-done.14.refs_1_ = bf16[256,256]{1,0:T(8,128)(2,1)S(1)} collective-permute-done((bf16[256,256]{1,0:T(8,128)(2,1)S(1)}, bf16[256,256]{1,0:T(8,128)(2,1)S(1)}, u32[]{:S(2)}, u32[]{:S(2)}) %collective-permute-start.14) | collective-permute-done | bytes 131104 | tf_op jit(solution)/shard_map/ppermute | solution.py:634
  228.4 1.9 collective-permute-done.15.refs_2_
  230.4 2.5 %project.1 = (bf16[256,1024]{1,0:T(8,128)(2,1)S(1)}, f32[256,1024]{1,0:T(8,128)S(1)}) custom-call(bf16[256,256]{1,0:T(8,128)(2,1)S(1)} %merge.1.refs_0_, bf16[256,256]{1,0:T(8,128)(2,1)S(1)} %collective-permute-done.14.refs_1_, bf16[256,256]{1,0:T(8,128)(2,1)S(1)} %collective-permute-done.15.refs_2_, bf16[256,256]{1,0:T(8,128)(2,1)S(1)} %collective-permute-done.16.refs_3_, ...), custom_call_target="tpu_custom_call" | custom-call | flops 1073741824 | bytes 6291456 | tf_op jit(solution)/shard_map/project/pallas_call | solution.py:546
  232.9 0.1 collective-permute-start.20
  233.0 1.9 collective-permute-done.20.got
  234.9 0.1 split.1
  235.1 1.5 collective-permute-start.21
  236.6 2.1 collective-permute-start.22
  238.7 4.3 %collective-permute-done.21 = bf16[256,256]{1,0:T(8,128)(2,1)S(1)} collective-permute-done((bf16[256,256]{1,0:T(8,128)(2,1)S(1)}, bf16[256,256]{1,0:T(8,128)(2,1)S(1)}, u32[]{:S(2)}, u32[]{:S(2)}) %collective-permute-start.21) | collective-permute-done | bytes 131104 | tf_op jit(solution)/shard_map/ppermute | solution.py:639
  243.0 2.3 collective-permute-done.23
  245.3 0.7 add_convert_fusion
  (44 shorter events, 0.1 us)
Async XLA Ops:
  0.0 25.5 %copy-start.7 = (f32[128]{0:T(128)S(1)}, f32[128]{0:T(128)}, u32[]{:S(2)}) copy-start(f32[128]{0:T(128)} %constant.24) | copy-start | bytes 1540
  0.0 25.5 %copy-start.8 = (f32[128]{0:T(128)S(1)}, f32[128]{0:T(128)}, u32[]{:S(2)}) copy-start(f32[128]{0:T(128)} %constant.25) | copy-start | bytes 1540
  0.0 22.2 %copy-start.12 = (s32[8]{0:T(128)S(1)}, s32[8]{0:T(128)}, u32[]{:S(2)}) copy-start(s32[8]{0:T(128)} %slabs.3) | copy-start | bytes 100
  5.7 17.7 %collective-permute-start = (bf16[320,512]{1,0:T(8,128)(2,1)}, bf16[320,512]{1,0:T(8,128)(2,1)S(1)}, u32[]{:S(2)}, u32[]{:S(2)}) collective-permute-start(bf16[320,512]{1,0:T(8,128)(2,1)} %get-tuple-element.29), channel_id=1, source_target_pairs={{0,1},{1,0},{2,3},{3,2},{4,5},{5,4},{6,7},{7,6},{8,9},{9,8},{10,11... | collective-permute-start | bytes 983048 | tf_op jit(solution)/shard_map/ppermute | solution.py:57
  15.6 18.6 %collective-permute-start.3 = (bf16[544,256]{1,0:T(8,128)(2,1)}, bf16[544,256]{1,0:T(8,128)(2,1)S(1)}, u32[]{:S(2)}, u32[]{:S(2)}) collective-permute-start(bf16[544,256]{1,0:T(8,128)(2,1)} %pack.1.refs_0_), channel_id=1, source_target_pairs={{0,8},{4,12},{8,16},{12,20},{16,24},{20,28},{24,0},{28,4},{1,9},{5... | collective-permute-start | bytes 835592 | tf_op jit(solution)/shard_map/ppermute | solution.py:596
  20.2 19.2 %collective-permute-start.4 = (bf16[544,256]{1,0:T(8,128)(2,1)}, bf16[544,256]{1,0:T(8,128)(2,1)S(1)}, u32[]{:S(2)}, u32[]{:S(2)}) collective-permute-start(bf16[544,256]{1,0:T(8,128)(2,1)} %pack.1.refs_0_), channel_id=1, source_target_pairs={{0,24},{4,28},{8,0},{12,4},{16,8},{20,12},{24,16},{28,20},{1,25},{... | collective-permute-start | bytes 835592 | tf_op jit(solution)/shard_map/ppermute | solution.py:596
  20.2 147.5 %collective-permute-start.5 = (bf16[544,256]{1,0:T(8,128)(2,1)}, bf16[544,256]{1,0:T(8,128)(2,1)S(1)}, u32[]{:S(2)}, u32[]{:S(2)}) collective-permute-start(bf16[544,256]{1,0:T(8,128)(2,1)} %pack.1.refs_0_), channel_id=1, source_target_pairs={{0,4},{4,8},{8,12},{12,16},{16,20},{20,24},{24,28},{28,0},{1,5},{5... | collective-permute-start | bytes 835592 | tf_op jit(solution)/shard_map/ppermute | solution.py:596
  21.2 157.6 %collective-permute-start.6 = (bf16[544,256]{1,0:T(8,128)(2,1)}, bf16[544,256]{1,0:T(8,128)(2,1)}, u32[]{:S(2)}, u32[]{:S(2)}) collective-permute-start(bf16[544,256]{1,0:T(8,128)(2,1)} %pack.1.refs_0_), channel_id=1, source_target_pairs={{0,28},{4,0},{8,4},{12,8},{16,12},{20,16},{24,20},{28,24},{1,29},{... | collective-permute-start | bytes 835592 | tf_op jit(solution)/shard_map/ppermute | solution.py:596
  23.5 1.1 copy-start.1
  24.6 8.7 %collective-permute-start.1 = (bf16[288,512]{1,0:T(8,128)(2,1)S(1)}, bf16[288,512]{1,0:T(8,128)(2,1)S(1)}, u32[]{:S(2)}, u32[]{:S(2)}) collective-permute-start(bf16[288,512]{1,0:T(8,128)(2,1)S(1)} %get-tuple-element.31), channel_id=1, source_target_pairs={{0,2},{2,0},{1,3},{3,1},{4,6},{6,4},{5,7},{7,5},{8,10},{10,8},{9,1... | collective-permute-start | bytes 884744 | tf_op jit(solution)/shard_map/ppermute | solution.py:57
  34.2 150.0 %copy-start.3 = (bf16[256,512]{1,0:T(8,128)(2,1)}, bf16[256,512]{1,0:T(8,128)(2,1)S(1)}, u32[]{:S(2)}) copy-start(bf16[256,512]{1,0:T(8,128)(2,1)S(1)} %get-tuple-element.32.near) | copy-start | bytes 786436
  34.2 148.5 %collective-permute-start.2 = (bf16[256,512]{1,0:T(8,128)(2,1)S(1)}, bf16[256,512]{1,0:T(8,128)(2,1)}, u32[]{:S(2)}, u32[]{:S(2)}) collective-permute-start(bf16[256,512]{1,0:T(8,128)(2,1)S(1)} %get-tuple-element.32.near), channel_id=1, source_target_pairs={{0,1},{1,0},{2,3},{3,2},{4,5},{5,4},{6,7},{7,6},{8,9},{9,8},{10,11... | collective-permute-start | bytes 786440 | tf_op jit(solution)/shard_map/ppermute | solution.py:57
  34.2 149.9 %copy-start.5 = (bf16[544,256]{1,0:T(8,128)(2,1)}, bf16[544,256]{1,0:T(8,128)(2,1)S(1)}, u32[]{:S(2)}) copy-start(bf16[544,256]{1,0:T(8,128)(2,1)S(1)} %collective-permute-done.3.refs_1_) | copy-start | bytes 835588
  34.2 145.3 %collective-permute-start.7 = (bf16[272,256]{1,0:T(8,128)(2,1)S(1)}, bf16[272,256]{1,0:T(8,128)(2,1)S(1)}, u32[]{:S(2)}, u32[]{:S(2)}) collective-permute-start(bf16[272,256]{1,0:T(8,128)(2,1)S(1)} %slice.8), channel_id=1, source_target_pairs={{0,8},{4,12},{8,16},{12,20},{16,24},{20,28},{24,0},{28,4},{1,9},{5... | collective-permute-start | bytes 417800 | tf_op jit(solution)/shard_map/ppermute | solution.py:596
  39.4 139.4 %copy-start.6 = (bf16[544,256]{1,0:T(8,128)(2,1)}, bf16[544,256]{1,0:T(8,128)(2,1)S(1)}, u32[]{:S(2)}) copy-start(bf16[544,256]{1,0:T(8,128)(2,1)S(1)} %collective-permute-done.4.refs_2_) | copy-start | bytes 835588
  39.4 142.7 %collective-permute-start.8 = (bf16[272,256]{1,0:T(8,128)(2,1)S(1)}, bf16[272,256]{1,0:T(8,128)(2,1)}, u32[]{:S(2)}, u32[]{:S(2)}) collective-permute-start(bf16[272,256]{1,0:T(8,128)(2,1)S(1)} %slice.9), channel_id=1, source_target_pairs={{0,24},{4,28},{8,0},{12,4},{16,8},{20,12},{24,16},{28,20},{1,25},{... | collective-permute-start | bytes 417800 | tf_op jit(solution)/shard_map/ppermute | solution.py:596
  167.7 3.3 %copy-start.9 = (bf16[544,256]{1,0:T(8,128)(2,1)}, bf16[544,256]{1,0:T(8,128)(2,1)S(1)}, u32[]{:S(2)}) copy-start(bf16[544,256]{1,0:T(8,128)(2,1)S(1)} %collective-permute-done.5.refs_3_) | copy-start | bytes 835588
  167.7 53.8 %collective-permute-start.17 = (bf16[256,2048]{1,0:T(8,128)(2,1)}, bf16[256,2048]{1,0:T(8,128)(2,1)S(1)}, u32[]{:S(2)}, u32[]{:S(2)}) collective-permute-start(bf16[256,2048]{1,0:T(8,128)(2,1)} %get-tuple-element.42), channel_id=1, source_target_pairs={{0,64},{32,96},{64,0},{96,32},{1,65},{33,97},{65,1},{97,33},{2,66}... | collective-permute-start | bytes 3145736 | tf_op jit(solution)/shard_map/ppermute | solution.py:603
  171.0 26.8 %all-to-all-start = ((bf16[8,64,256]{2,1,0:T(8,128)(2,1)}), bf16[8,64,256]{2,1,0:T(8,128)(2,1)S(1)}, u32[]{:S(2)}, u32[]{:S(2)}) async-start(bf16[8,64,256]{2,1,0:T(8,128)(2,1)} %get-tuple-element.33.notes), calls=%async_computation | async-start | bytes 524288 | tf_op jit(solution)/shard_map/all_to_all | solution.py:618
  178.8 45.1 %collective-permute-start.18 = (bf16[256,2048]{1,0:T(8,128)(2,1)}, bf16[256,2048]{1,0:T(8,128)(2,1)S(1)}, u32[]{:S(2)}, u32[]{:S(2)}) collective-permute-start(bf16[256,2048]{1,0:T(8,128)(2,1)} %get-tuple-element.43), channel_id=1, source_target_pairs={{0,32},{32,64},{64,96},{96,0},{1,33},{33,65},{65,97},{97,1},{2,34}... | collective-permute-start | bytes 3145736 | tf_op jit(solution)/shard_map/ppermute | solution.py:603
  179.5 18.3 %copy-start.11 = (bf16[272,256]{1,0:T(8,128)(2,1)}, bf16[272,256]{1,0:T(8,128)(2,1)S(1)}, u32[]{:S(2)}) copy-start(bf16[272,256]{1,0:T(8,128)(2,1)S(1)} %collective-permute-done.7.refs_4_) | copy-start | bytes 417796
  179.5 44.4 %collective-permute-start.19 = (bf16[256,2048]{1,0:T(8,128)(2,1)}, bf16[256,2048]{1,0:T(8,128)(2,1)}, u32[]{:S(2)}, u32[]{:S(2)}) collective-permute-start(bf16[256,2048]{1,0:T(8,128)(2,1)} %get-tuple-element.44), channel_id=1, source_target_pairs={{0,96},{32,0},{64,32},{96,64},{1,97},{33,1},{65,33},{97,65},{2,98}... | collective-permute-start | bytes 3145736 | tf_op jit(solution)/shard_map/ppermute | solution.py:603
  182.1 15.7 %collective-permute-start.10 = (bf16[544,256]{1,0:T(8,128)(2,1)}, bf16[544,256]{1,0:T(8,128)(2,1)S(1)}, u32[]{:S(2)}, u32[]{:S(2)}) collective-permute-start(bf16[544,256]{1,0:T(8,128)(2,1)} %copy-done.6), channel_id=1, source_target_pairs={{0,28},{4,0},{8,4},{12,8},{16,12},{20,16},{24,20},{28,24},{1,29},{... | collective-permute-start | bytes 835592 | tf_op jit(solution)/shard_map/ppermute | solution.py:596
  182.7 15.2 %collective-permute-start.9 = (bf16[544,256]{1,0:T(8,128)(2,1)S(1)}, bf16[544,256]{1,0:T(8,128)(2,1)}, u32[]{:S(2)}, u32[]{:S(2)}) collective-permute-start(bf16[544,256]{1,0:T(8,128)(2,1)S(1)} %collective-permute-done.3.refs_1_), channel_id=1, source_target_pairs={{0,4},{4,8},{8,12},{12,16},{16,20},{20,24},{24,28},{28,0},{1,5},{5... | collective-permute-start | bytes 835592 | tf_op jit(solution)/shard_map/ppermute | solution.py:596
  197.9 0.7 copy-start.10
  197.9 0.8 copy-start.4
  198.7 31.7 %copy-start = (bf16[256,2048]{1,0:T(8,128)(2,1)S(1)}, bf16[256,2048]{1,0:T(8,128)(2,1)}, u32[]{:S(2)}) copy-start(bf16[256,2048]{1,0:T(8,128)(2,1)} %get-tuple-element.41.refs_4_) | copy-start | bytes 3145732
  209.9 1.7 collective-permute-start.11
  210.0 6.8 %collective-permute-start.12 = (bf16[272,256]{1,0:T(8,128)(2,1)}, bf16[272,256]{1,0:T(8,128)(2,1)S(1)}, u32[]{:S(2)}, u32[]{:S(2)}) collective-permute-start(bf16[272,256]{1,0:T(8,128)(2,1)} %get-tuple-element.39), channel_id=1, source_target_pairs={{0,2},{2,0},{1,3},{3,1},{4,6},{6,4},{5,7},{7,5},{8,10},{10,8},{9,1... | collective-permute-start | bytes 417800 | tf_op jit(solution)/shard_map/ppermute | solution.py:57
  211.5 7.3 %collective-permute-start.13 = (bf16[272,256]{1,0:T(8,128)(2,1)}, bf16[272,256]{1,0:T(8,128)(2,1)S(1)}, u32[]{:S(2)}, u32[]{:S(2)}) collective-permute-start(bf16[272,256]{1,0:T(8,128)(2,1)} %get-tuple-element.40), channel_id=1, source_target_pairs={{0,3},{1,2},{2,1},{3,0},{4,7},{5,6},{6,5},{7,4},{8,11},{9,10},{10,... | collective-permute-start | bytes 417800 | tf_op jit(solution)/shard_map/ppermute | solution.py:630
  218.8 0.9 copy-start.2
  220.3 8.2 %collective-permute-start.14 = (bf16[256,256]{1,0:T(8,128)(2,1)S(1)}, bf16[256,256]{1,0:T(8,128)(2,1)S(1)}, u32[]{:S(2)}, u32[]{:S(2)}) collective-permute-start(bf16[256,256]{1,0:T(8,128)(2,1)S(1)} %merge.1.refs_0_), channel_id=1, source_target_pairs={{0,64},{32,96},{64,0},{96,32},{1,65},{33,97},{65,1},{97,33},{2,66}... | collective-permute-start | bytes 393224 | tf_op jit(solution)/shard_map/ppermute | solution.py:634
  220.6 9.8 %collective-permute-start.15 = (bf16[256,256]{1,0:T(8,128)(2,1)S(1)}, bf16[256,256]{1,0:T(8,128)(2,1)S(1)}, u32[]{:S(2)}, u32[]{:S(2)}) collective-permute-start(bf16[256,256]{1,0:T(8,128)(2,1)S(1)} %merge.1.refs_0_), channel_id=1, source_target_pairs={{0,32},{32,64},{64,96},{96,0},{1,33},{33,65},{65,97},{97,1},{2,34}... | collective-permute-start | bytes 393224 | tf_op jit(solution)/shard_map/ppermute | solution.py:634
  221.5 8.9 %collective-permute-start.16 = (bf16[256,256]{1,0:T(8,128)(2,1)S(1)}, bf16[256,256]{1,0:T(8,128)(2,1)S(1)}, u32[]{:S(2)}, u32[]{:S(2)}) collective-permute-start(bf16[256,256]{1,0:T(8,128)(2,1)S(1)} %merge.1.refs_0_), channel_id=1, source_target_pairs={{0,96},{32,0},{64,32},{96,64},{1,97},{33,1},{65,33},{97,65},{2,98}... | collective-permute-start | bytes 393224 | tf_op jit(solution)/shard_map/ppermute | solution.py:634
  232.9 2.0 collective-permute-start.20
  235.1 7.9 %collective-permute-start.21 = (bf16[256,256]{1,0:T(8,128)(2,1)S(1)}, bf16[256,256]{1,0:T(8,128)(2,1)S(1)}, u32[]{:S(2)}, u32[]{:S(2)}) collective-permute-start(bf16[256,256]{1,0:T(8,128)(2,1)S(1)} %get-tuple-element.48), channel_id=1, source_target_pairs={{0,128},{2,130},{128,0},{130,2},{1,129},{3,131},{129,1},{131,3},{4... | collective-permute-start | bytes 393224 | tf_op jit(solution)/shard_map/ppermute | solution.py:639
  236.6 6.4 %collective-permute-start.22 = (bf16[256,256]{1,0:T(8,128)(2,1)S(1)}, bf16[256,256]{1,0:T(8,128)(2,1)S(1)}, u32[]{:S(2)}, u32[]{:S(2)}) collective-permute-start(bf16[256,256]{1,0:T(8,128)(2,1)S(1)} %get-tuple-element.49), channel_id=1, source_target_pairs={{0,2},{2,128},{128,130},{130,0},{1,3},{3,129},{129,131},{131,1},{4... | collective-permute-start | bytes 393224 | tf_op jit(solution)/shard_map/ppermute | solution.py:639
  238.7 6.7 %collective-permute-start.23 = (bf16[256,256]{1,0:T(8,128)(2,1)S(1)}, bf16[256,256]{1,0:T(8,128)(2,1)S(1)}, u32[]{:S(2)}, u32[]{:S(2)}) collective-permute-start(bf16[256,256]{1,0:T(8,128)(2,1)S(1)} %get-tuple-element.50), channel_id=1, source_target_pairs={{0,130},{2,0},{128,2},{130,128},{1,131},{3,1},{129,3},{131,129},{4... | collective-permute-start | bytes 393224 | tf_op jit(solution)/shard_map/ppermute | solution.py:639

commit v3 on v2

--- a/solution.py
+++ b/solution.py
@@ -26,7 +26,7 @@
 NEW = 64
 QUARTER = 512
 HALF = ROWS + 16
-LOAD = 2 * HALF
+LOAD = 4 * HALF
 MSG = ROWS + 16
 TALL = 1024
 EXPONENT = math.log2(math.e) / math.sqrt(HD)
@@ -71,23 +71,23 @@
     return copies
 
 
-def pack_kernel(places, keys, values, out, codes, sems):
-    quarter = hid_index()
+def pack_kernel(places, keys, values, out, load, sems):
+    core = lax.axis_index("hid_1")
+    lane = lax.broadcasted_iota(jnp.int32, (16, PAIR), 1)
     pairs = []
-    for b in range(2):
-        rows = pl.ds(pl.multiple_of(quarter * QUARTER + b * ROWS, ROWS), ROWS)
-        to = slice(b * HALF, b * HALF + ROWS)
-        pairs.append((keys.at[rows, :], out.at[to, :HD]))
-        pairs.append((values.at[rows, :], out.at[to, HD:]))
-    copies = fetch(pairs, sems.at[:4])
-    lane = lax.broadcasted_iota(jnp.int32, (16, PAIR), 1)
-    for b in range(2):
-        place = places[quarter * 2 + b]
+    for i in range(4):
+        block = 4 * lax.axis_index("hid_0") + lax.rem(2 * core + i, 4)
+        rows = pl.ds(pl.multiple_of(block * ROWS, ROWS), ROWS)
+        to = slice(i * HALF, i * HALF + ROWS)
+        pairs.append((keys.at[rows, :], load.at[to, :HD]))
+        pairs.append((values.at[rows, :], load.at[to, HD:]))
+        place = places[block]
         table = jnp.where(lane == 0, place >> 1, jnp.where(lane == 1, place & 1, 0))
-        codes[b] = table.astype(F32).astype(BF16)
-    pairs = [(codes.at[b], out.at[b * HALF + ROWS : (b + 1) * HALF, :]) for b in range(2)]
-    copies += fetch(pairs, sems.at[4:])
+        load[i * HALF + ROWS : (i + 1) * HALF, :] = table.astype(F32).astype(BF16)
+    copies = fetch(pairs, sems.at[:8])
     for copy in copies:
+        copy.wait()
+    for copy in fetch([(load, out)], sems.at[8:]):
         copy.wait()
 
 
@@ -97,7 +97,7 @@
         out_shape=shaped((LOAD, PAIR), BF16),
         in_specs=[SMEM, HBM, HBM],
         out_specs=HBM,
-        scratch_shapes=[pltpu.VMEM((2, 16, PAIR), BF16), pltpu.SemaphoreType.DMA((6,))],
+        scratch_shapes=[pltpu.VMEM((LOAD, PAIR), BF16), pltpu.SemaphoreType.DMA((9,))],
         compiler_params=params(),
         cost_estimate=cost(moved=2**19),
         name="pack",
@@ -105,23 +105,21 @@
 
 
 def columns_kernel(weight, *refs):
-    outs, sems = refs[:4], refs[4]
+    outs, pieces, sems, out_sems = refs[:4], refs[4], refs[5], refs[6]
     y = lax.axis_index("head_1")
-    copies = []
+    pairs = []
     for t, by in enumerate((2, 1, 3, 0)):
         at = lax.rem(y + by, 4) * 1024
         for hi in range(2):
             source = pl.ds(pl.multiple_of(hi * 4096 + at, 1024), 1024)
-            copies.append(
-                pltpu.make_async_copy(
-                    weight.at[:, source],
-                    outs[t].at[:, hi * 1024 : (hi + 1) * 1024],
-                    sems.at[2 * t + hi],
-                )
-            )
-    for copy in copies:
-        copy.start()
-    for copy in copies:
+            pairs.append((weight.at[:, source], pieces.at[t, :, hi * 1024 : (hi + 1) * 1024]))
+    copies = fetch(pairs, sems)
+    leaving = []
+    for t in range(4):
+        copies[2 * t].wait()
+        copies[2 * t + 1].wait()
+        leaving += fetch([(pieces.at[t], outs[t])], out_sems.at[t : t + 1])
+    for copy in leaving:
         copy.wait()
 
 
@@ -131,9 +129,13 @@
         out_shape=[shaped((ROWS, 2048), BF16)] * 4,
         in_specs=[HBM],
         out_specs=[HBM] * 4,
-        scratch_shapes=[pltpu.SemaphoreType.DMA((8,))],
+        scratch_shapes=[
+            pltpu.VMEM((4, ROWS, 2048), BF16),
+            pltpu.SemaphoreType.DMA((8,)),
+            pltpu.SemaphoreType.DMA((4,)),
+        ],
         compiler_params=params(),
-        cost_estimate=cost(moved=2**23),
+        cost_estimate=cost(moved=8 * 2**20),
         name="columns",
     )(weight)
 
@@ -332,7 +334,7 @@
     refs = refs[count + 3 :]
     near_in, far_in, own, *loads = refs[: 3 + count]
     q_all, acc_all, peak_all, keys, values, scores, peak_ref, sems = refs[3 + count :]
-    pairs = list(zip(sources, loads))
+    pairs = [(sources[0].at[: 2 * HALF, :], loads[0])] + list(zip(sources[1:], loads[1:]))
     pairs += [(notes.at[0], own), (near, near_in), (far, far_in)]
     copies = fetch(pairs, sems.at[: count + 3])
     mine = slabs[lax.axis_index("key")]
@@ -397,8 +399,8 @@
 
 
 def attend_near(slabs, near, far, notes, loads):
-    count, chunk = len(loads), 1280
-    height = count * QUARTER
+    count, chunk = len(loads), 1792
+    height = (2 + 4 * (count - 1)) * ROWS
     state = [((8 * ROWS, HD), BF16), ((8 * ROWS, PAIR), F32), ((8 * ROWS, HD), F32)]
     return pl.pallas_call(
         functools.partial(near_kernel, chunk=chunk, count=count),
@@ -409,7 +411,8 @@
             pltpu.VMEM((ROWS, 4 * HD), BF16),
             pltpu.VMEM((ROWS, 4 * HD), BF16),
             pltpu.VMEM((NEW, PAIR), BF16),
-            *[pltpu.VMEM((LOAD, PAIR), BF16)] * count,
+            pltpu.VMEM((2 * HALF, PAIR), BF16),
+            *[pltpu.VMEM((LOAD, PAIR), BF16)] * (count - 1),
             *[pltpu.VMEM(*s) for s in state],
             pltpu.VMEM((height, HD), BF16),
             pltpu.VMEM((height, PAIR), BF16),
@@ -592,19 +595,26 @@
 
     load = pack(cache_places, key_cache.reshape(-1, HD), value_cache.reshape(-1, HD))
 
-    def along(array, by):
-        return lax.ppermute(array, "key", shift(8, by))
-
-    near_loads = [load] + [along(load, by) for by in (2, -2, 1, -1)]
+    def away(array, by):
+        pairs = []
+        for k in range(8):
+            pairs.append((2 * k, 2 * ((k + by) % 8)))
+            pairs.append((2 * k + 1, 2 * ((k - by) % 8) + 1))
+        return lax.ppermute(array, ("key", "hid_1"), pairs)
+
+    one = away(load, 1)
 
     pieces = columns(output_weight)
+
+    send, keep = first(tokens, query_weight, key_weight, value_weight)
+    one, keep = lax.optimization_barrier((one, keep))
+    two = away(one, 1)
+    send, keep = second(keep, swap(send, "hid_1"))
+    got = swap(send, "hid_0")
+    keep, pieces = lax.optimization_barrier((keep, pieces))
     weights = [pieces[3]]
     for piece, by in zip(pieces, (2, 1, 3)):
         weights.append(lax.ppermute(piece, "head_1", shift(4, by)))
-
-    send, keep = first(tokens, query_weight, key_weight, value_weight)
-    send, keep = second(keep, swap(send, "hid_1"))
-    got = swap(send, "hid_0")
 
     middle = HD // 2
     index = np.arange(HD) % middle
@@ -613,14 +623,15 @@
     spots = slab_places[key_index] * ROWS + jnp.arange(ROWS, dtype=jnp.int32)
     angles = spots.astype(F32)[:, None] * frequency[None, :]
     queries, notes = rotated(keep, got, jnp.cos(angles), jnp.sin(angles) * sign[None, :])
+    two, queries, notes = lax.optimization_barrier((two, queries, notes))
+    three = away(two, 1)
     far = swap(queries, "hid_1")
 
     new = lax.all_to_all(notes, "key", split_axis=0, concat_axis=0, tiled=True)
 
-    _, up, down, _, _ = near_loads
-    far_loads = [along(up[:HALF], 2), along(down[HALF:], -2), along(up, 1), along(down, -1)]
-    state = attend_near(slab_places, queries, far, notes, near_loads)
-    parts = attend_far(slab_places, *state, new, far_loads)
+    four = away(three[: 2 * HALF], 1)
+    state = attend_near(slab_places, queries, far, notes, [load, one, two, three])
+    parts = attend_far(slab_places, *state, new, [four])
     flip = [(0, 3), (1, 2), (2, 1), (3, 0)]
     merged = merge(
         [

time: 248 us -> 107 us (0.43)
  the two profiles are of different devices: /device:TPU:70 before, /device:TPU:1 now
where the time goes in v3:
time: 107 us
  starting transfers between devices  41.5 us (39%)
  Pallas kernels  36.3 us (34%)
  waiting for transfers between devices  25.7 us (24%)
  local copies, waits for them, and re-layouts  1.56 us (1%)
  other arithmetic  1.25 us (1%)
    pallas_call x1, Pallas kernels, attend_near(): pl.pallas_call(functools.partial(near_kernel, chunk=chunk, count=count),...  12.4 us
    ppermute x4, starting transfers between devices, away(): return lax.ppermute(array, ('key', 'hid_1'), pairs)  12.3 us
    ppermute x6, waiting for transfers between devices, swap(): return lax.ppermute(array, axis, shift(2, 1))  11.4 us
    ppermute x6, starting transfers between devices, swap(): return lax.ppermute(array, axis, shift(2, 1))  8.49 us
    pallas_call x1, Pallas kernels, attend_far(): pl.pallas_call(functools.partial(far_kernel, chunk=chunk, count=count), o...  7.82 us
    ppermute x3, waiting for transfers between devices, body(): lax.ppermute(merged, 'head_1', shift(4, by))  5.76 us
    pallas_call x1, Pallas kernels, first(): pl.pallas_call(first_kernel, out_shape=[shaped((320, 512), BF16), shaped(...  5.7 us
    ppermute x3, starting transfers between devices, body(): weights.append(lax.ppermute(piece, 'head_1', shift(4, by)))  5.59 us
  transfers between devices with their start and end apart: 21, of which 10 were waited for; matrix products, arithmetic and copies ran while one was open for 1% of the time, Pallas kernels for 29%

profile of v3, /device:TPU:1, one launch (start us, length us, event | category | flops | bytes accessed | tf_op | source)
XLA Modules:
  0.0 107.1 jit_solution(3936644033119568281)
XLA Ops:
  0.0 2.7 %pack.1.refs_0_ = bf16[1088,256]{1,0:T(8,128)(2,1)} custom-call(s32[8]{0:T(128)} %places.1, bf16[2048,128]{1,0:T(8,128)(2,1)} %bitcast.3, bf16[2048,128]{1,0:T(8,128)(2,1)} %bitcast.4), custom_call_target="tpu_custom_call" | custom-call | bytes 524288 | tf_op jit(solution)/shard_map/pack/pallas_call | solution.py:95
  2.7 0.0 copy-start.9
  2.7 0.0 copy-start.5
  2.7 0.0 copy-start.6
  2.7 6.5 %collective-permute-start = (bf16[1088,256]{1,0:T(8,128)(2,1)}, bf16[1088,256]{1,0:T(8,128)(2,1)S(1)}, u32[]{:S(2)}, u32[]{:S(2)}) collective-permute-start(bf16[1088,256]{1,0:T(8,128)(2,1)} %pack.1.refs_0_), channel_id=1, source_target_pairs={{0,4},{1,29},{4,8},{5,1},{8,12},{9,5},{12,16},{13,9},{16,20},{17,1... | collective-permute-start | bytes 1671176 | tf_op jit(solution)/shard_map/ppermute | solution.py:603
  9.2 5.7 %first.1 = (bf16[320,512]{1,0:T(8,128)(2,1)}, f32[320,512]{1,0:T(8,128)}) custom-call(bf16[256,2048]{1,0:T(8,128)(2,1)} %tokens.1, bf16[2048,1024]{1,0:T(8,128)(2,1)} %query.1, bf16[2048,128]{1,0:T(8,128)(2,1)} %key.1, bf16[2048,128]{1,0:T(8,128)(2,1)} %value.1), custom_call_target="tpu_custom_call" | custom-call | flops 1342177280 | bytes 6291456 | tf_op jit(solution)/shard_map/first/pallas_call | solution.py:181
  14.9 0.1 collective-permute-start.2
  15.0 1.0 collective-permute-done.refs_1_
  16.0 3.0 %collective-permute-start.1 = (bf16[1088,256]{1,0:T(8,128)(2,1)S(1)}, bf16[1088,256]{1,0:T(8,128)(2,1)S(1)}, u32[]{:S(2)}, u32[]{:S(2)}) collective-permute-start(bf16[1088,256]{1,0:T(8,128)(2,1)S(1)} %collective-permute-done.refs_1_), channel_id=1, source_target_pairs={{0,4},{1,29},{4,8},{5,1},{8,12},{9,5},{12,16},{13,9},{16,20},{17,1... | collective-permute-start | bytes 1671176 | tf_op jit(solution)/shard_map/ppermute | solution.py:603
  19.0 3.4 %columns.1 = (bf16[256,2048]{1,0:T(8,128)(2,1)}, bf16[256,2048]{1,0:T(8,128)(2,1)}, bf16[256,2048]{1,0:T(8,128)(2,1)}, bf16[256,2048]{1,0:T(8,128)(2,1)}) custom-call(bf16[256,8192]{1,0:T(8,128)(2,1)} %weight.1), custom_call_target="tpu_custom_call" | custom-call | bytes 8388608 | tf_op jit(solution)/shard_map/columns/pallas_call | solution.py:127
  22.5 0.6 dynamic_slice.3
  23.7 0.0 collective-permute-done.2.got
  23.7 0.1 second.1
  23.8 1.3 %collective-permute-start.3 = (bf16[288,512]{1,0:T(8,128)(2,1)S(1)}, bf16[288,512]{1,0:T(8,128)(2,1)S(1)}, u32[]{:S(2)}, u32[]{:S(2)}) collective-permute-start(bf16[288,512]{1,0:T(8,128)(2,1)S(1)} %get-tuple-element.48), channel_id=1, source_target_pairs={{0,2},{2,0},{1,3},{3,1},{4,6},{6,4},{5,7},{7,5},{8,10},{10,8},{9,1... | collective-permute-start | bytes 884744 | tf_op jit(solution)/shard_map/ppermute | solution.py:57
  25.1 0.5 fusion
  25.6 6.5 %collective-permute-done.3.got = bf16[288,512]{1,0:T(8,128)(2,1)S(1)} collective-permute-done((bf16[288,512]{1,0:T(8,128)(2,1)S(1)}, bf16[288,512]{1,0:T(8,128)(2,1)S(1)}, u32[]{:S(2)}, u32[]{:S(2)}) %collective-permute-start.3) | collective-permute-done | bytes 294944 | tf_op jit(solution)/shard_map/ppermute | solution.py:57
  32.1 0.9 rotated.1
  33.1 0.1 collective-permute-start.5
  33.2 0.4 collective-permute-start.4
  33.6 2.9 %collective-permute-start.13 = (bf16[256,2048]{1,0:T(8,128)(2,1)}, bf16[256,2048]{1,0:T(8,128)(2,1)S(1)}, u32[]{:S(2)}, u32[]{:S(2)}) collective-permute-start(bf16[256,2048]{1,0:T(8,128)(2,1)} %get-tuple-element.62), channel_id=1, source_target_pairs={{0,64},{32,96},{64,0},{96,32},{1,65},{33,97},{65,1},{97,33},{2,66}... | collective-permute-start | bytes 3145736 | tf_op jit(solution)/shard_map/ppermute | solution.py:617
  36.5 0.4 collective-permute-start.14
  36.9 2.3 %collective-permute-start.15 = (bf16[256,2048]{1,0:T(8,128)(2,1)}, bf16[256,2048]{1,0:T(8,128)(2,1)}, u32[]{:S(2)}, u32[]{:S(2)}) collective-permute-start(bf16[256,2048]{1,0:T(8,128)(2,1)} %get-tuple-element.64), channel_id=1, source_target_pairs={{0,96},{32,0},{64,32},{96,64},{1,97},{33,1},{65,33},{97,65},{2,98}... | collective-permute-start | bytes 3145736 | tf_op jit(solution)/shard_map/ppermute | solution.py:617
  39.2 4.2 %all-to-all-start = ((bf16[8,64,256]{2,1,0:T(8,128)(2,1)}), bf16[8,64,256]{2,1,0:T(8,128)(2,1)}, u32[]{:S(2)}, u32[]{:S(2)}) async-start(bf16[8,64,256]{2,1,0:T(8,128)(2,1)} %get-tuple-element.52.notes), calls=%async_computation | async-start | bytes 524288 | tf_op jit(solution)/shard_map/all_to_all | solution.py:630
  43.4 2.8 %collective-permute-start.6 = (bf16[544,256]{1,0:T(8,128)(2,1)S(1)}, bf16[544,256]{1,0:T(8,128)(2,1)}, u32[]{:S(2)}, u32[]{:S(2)}) collective-permute-start(bf16[544,256]{1,0:T(8,128)(2,1)S(1)} %slice.4), channel_id=1, source_target_pairs={{0,4},{1,29},{4,8},{5,1},{8,12},{9,5},{12,16},{13,9},{16,20},{17,1... | collective-permute-start | bytes 835592 | tf_op jit(solution)/shard_map/ppermute | solution.py:603
  46.2 12.4 %near.1 = (bf16[2048,128]{1,0:T(8,128)(2,1)}, f32[2048,256]{1,0:T(8,128)}, f32[2048,128]{1,0:T(8,128)}) custom-call(s32[8]{0:T(128)} %slabs.3, bf16[256,512]{1,0:T(8,128)(2,1)} %copy-done.3, bf16[256,512]{1,0:T(8,128)(2,1)} %collective-permute-done.4.far, bf16[8,64,256]{2,1,0:T(8,128)(2,1)} %get-tuple-element.52.notes, bf16[1088,256]{1,0:T(8,128)(2,1)} %pack.1.refs_0_, ...), custom_call_target="tpu_custom_call" | custom-call | flops 5637144576 | bytes 8388608 | tf_op jit(solution)/shard_map/near/pallas_call | solution.py:405
  58.6 7.8 %far.1 = (bf16[272,256]{1,0:T(8,128)(2,1)}, bf16[272,256]{1,0:T(8,128)(2,1)}, bf16[272,256]{1,0:T(8,128)(2,1)}, bf16[272,256]{1,0:T(8,128)(2,1)}) custom-call(s32[8]{0:T(128)} %slabs.3, bf16[2048,128]{1,0:T(8,128)(2,1)} %get-tuple-element.54.refs_0_, f32[2048,256]{1,0:T(8,128)} %get-tuple-element.55.refs_1_, f32[2048,128]{1,0:T(8,128)} %get-tuple-element.56.refs_2_, ...), custom_call_target="tpu_custom_call" | custom-call | flops 1610612736 | bytes 8388608 | tf_op jit(solution)/shard_map/far/pallas_call | solution.py:479
  66.5 5.2 %collective-permute-start.7 = (bf16[272,256]{1,0:T(8,128)(2,1)}, bf16[272,256]{1,0:T(8,128)(2,1)S(1)}, u32[]{:S(2)}, u32[]{:S(2)}) collective-permute-start(bf16[272,256]{1,0:T(8,128)(2,1)} %get-tuple-element.58), channel_id=1, source_target_pairs={{0,1},{1,0},{2,3},{3,2},{4,5},{5,4},{6,7},{7,6},{8,9},{9,8},{10,11... | collective-permute-start | bytes 417800 | tf_op jit(solution)/shard_map/ppermute | solution.py:57
  71.7 0.9 collective-permute-start.8
  72.6 0.3 collective-permute-done.7.refs_1_
  72.9 1.2 %collective-permute-start.9 = (bf16[272,256]{1,0:T(8,128)(2,1)}, bf16[272,256]{1,0:T(8,128)(2,1)S(1)}, u32[]{:S(2)}, u32[]{:S(2)}) collective-permute-start(bf16[272,256]{1,0:T(8,128)(2,1)} %get-tuple-element.60), channel_id=1, source_target_pairs={{0,3},{1,2},{2,1},{3,0},{4,7},{5,6},{6,5},{7,4},{8,11},{9,10},{10,... | collective-permute-start | bytes 417800 | tf_op jit(solution)/shard_map/ppermute | solution.py:641
  74.2 3.1 %collective-permute-done.8.refs_2_ = bf16[272,256]{1,0:T(8,128)(2,1)S(1)} collective-permute-done((bf16[272,256]{1,0:T(8,128)(2,1)}, bf16[272,256]{1,0:T(8,128)(2,1)S(1)}, u32[]{:S(2)}, u32[]{:S(2)}) %collective-permute-start.8) | collective-permute-done | bytes 139296 | tf_op jit(solution)/shard_map/ppermute | solution.py:57
  77.3 3.5 %collective-permute-done.9.refs_3_ = bf16[272,256]{1,0:T(8,128)(2,1)S(1)} collective-permute-done((bf16[272,256]{1,0:T(8,128)(2,1)}, bf16[272,256]{1,0:T(8,128)(2,1)S(1)}, u32[]{:S(2)}, u32[]{:S(2)}) %collective-permute-start.9) | collective-permute-done | bytes 139296 | tf_op jit(solution)/shard_map/ppermute | solution.py:641
  80.7 0.9 copy-done.2
  81.6 0.6 merge.1.refs_0_
  82.2 1.4 %collective-permute-start.10 = (bf16[256,256]{1,0:T(8,128)(2,1)S(1)}, bf16[256,256]{1,0:T(8,128)(2,1)S(1)}, u32[]{:S(2)}, u32[]{:S(2)}) collective-permute-start(bf16[256,256]{1,0:T(8,128)(2,1)S(1)} %merge.1.refs_0_), channel_id=1, source_target_pairs={{0,64},{32,96},{64,0},{96,32},{1,65},{33,97},{65,1},{97,33},{2,66}... | collective-permute-start | bytes 393224 | tf_op jit(solution)/shard_map/ppermute | solution.py:645
  83.6 0.4 collective-permute-start.11
  84.0 2.3 %collective-permute-start.12 = (bf16[256,256]{1,0:T(8,128)(2,1)S(1)}, bf16[256,256]{1,0:T(8,128)(2,1)S(1)}, u32[]{:S(2)}, u32[]{:S(2)}) collective-permute-start(bf16[256,256]{1,0:T(8,128)(2,1)S(1)} %merge.1.refs_0_), channel_id=1, source_target_pairs={{0,96},{32,0},{64,32},{96,64},{1,97},{33,1},{65,33},{97,65},{2,98}... | collective-permute-start | bytes 393224 | tf_op jit(solution)/shard_map/ppermute | solution.py:645
  86.3 2.7 %collective-permute-done.10.refs_1_ = bf16[256,256]{1,0:T(8,128)(2,1)S(1)} collective-permute-done((bf16[256,256]{1,0:T(8,128)(2,1)S(1)}, bf16[256,256]{1,0:T(8,128)(2,1)S(1)}, u32[]{:S(2)}, u32[]{:S(2)}) %collective-permute-start.10) | collective-permute-done | bytes 131104 | tf_op jit(solution)/shard_map/ppermute | solution.py:645
  89.0 3.0 %collective-permute-done.11.refs_2_ = bf16[256,256]{1,0:T(8,128)(2,1)S(1)} collective-permute-done((bf16[256,256]{1,0:T(8,128)(2,1)S(1)}, bf16[256,256]{1,0:T(8,128)(2,1)S(1)}, u32[]{:S(2)}, u32[]{:S(2)}) %collective-permute-start.11) | collective-permute-done | bytes 131104 | tf_op jit(solution)/shard_map/ppermute | solution.py:645
  92.1 2.5 %project.1 = (bf16[256,1024]{1,0:T(8,128)(2,1)S(1)}, f32[256,1024]{1,0:T(8,128)S(1)}) custom-call(bf16[256,256]{1,0:T(8,128)(2,1)S(1)} %merge.1.refs_0_, bf16[256,256]{1,0:T(8,128)(2,1)S(1)} %collective-permute-done.10.refs_1_, bf16[256,256]{1,0:T(8,128)(2,1)S(1)} %collective-permute-done.11.refs_2_, bf16[256,256]{1,0:T(8,128)(2,1)S(1)} %collective-permute-done.12.refs_3_, ...), custom_call_target="tpu_custom_call" | custom-call | flops 1073741824 | bytes 6291456 | tf_op jit(solution)/shard_map/project/pallas_call | solution.py:549
  94.6 0.5 collective-permute-start.16
  95.1 1.5 %collective-permute-done.16.got = bf16[256,1024]{1,0:T(8,128)(2,1)S(1)} collective-permute-done((bf16[256,1024]{1,0:T(8,128)(2,1)S(1)}, bf16[256,1024]{1,0:T(8,128)(2,1)S(1)}, u32[]{:S(2)}, u32[]{:S(2)}) %collective-permute-start.16) | collective-permute-done | bytes 524320 | tf_op jit(solution)/shard_map/ppermute | solution.py:57
  96.7 0.1 split.1
  96.8 2.8 %collective-permute-start.17 = (bf16[256,256]{1,0:T(8,128)(2,1)S(1)}, bf16[256,256]{1,0:T(8,128)(2,1)S(1)}, u32[]{:S(2)}, u32[]{:S(2)}) collective-permute-start(bf16[256,256]{1,0:T(8,128)(2,1)S(1)} %get-tuple-element.68), channel_id=1, source_target_pairs={{0,128},{2,130},{128,0},{130,2},{1,129},{3,131},{129,1},{131,3},{4... | collective-permute-start | bytes 393224 | tf_op jit(solution)/shard_map/ppermute | solution.py:650
  99.6 2.7 %collective-permute-start.19 = (bf16[256,256]{1,0:T(8,128)(2,1)S(1)}, bf16[256,256]{1,0:T(8,128)(2,1)S(1)}, u32[]{:S(2)}, u32[]{:S(2)}) collective-permute-start(bf16[256,256]{1,0:T(8,128)(2,1)S(1)} %get-tuple-element.70), channel_id=1, source_target_pairs={{0,130},{2,0},{128,2},{130,128},{1,131},{3,1},{129,3},{131,129},{4... | collective-permute-start | bytes 393224 | tf_op jit(solution)/shard_map/ppermute | solution.py:650
  102.3 0.8 collective-permute-done.17
  103.1 3.3 %collective-permute-done.18 = bf16[256,256]{1,0:T(8,128)(2,1)S(1)} collective-permute-done((bf16[256,256]{1,0:T(8,128)(2,1)S(1)}, bf16[256,256]{1,0:T(8,128)(2,1)S(1)}, u32[]{:S(2)}, u32[]{:S(2)}) %collective-permute-start.18) | collective-permute-done | bytes 131104 | tf_op jit(solution)/shard_map/ppermute | solution.py:650
  106.4 0.7 add_convert_fusion
  (29 shorter events, 0.1 us)
Async XLA Ops:
  2.7 19.7 %copy-start.9 = (s32[8]{0:T(128)S(1)}, s32[8]{0:T(128)}, u32[]{:S(2)}) copy-start(s32[8]{0:T(128)} %slabs.3) | copy-start | bytes 100
  2.7 22.4 %copy-start.5 = (f32[128]{0:T(128)S(1)}, f32[128]{0:T(128)}, u32[]{:S(2)}) copy-start(f32[128]{0:T(128)} %constant.24) | copy-start | bytes 1540
  2.7 22.4 %copy-start.6 = (f32[128]{0:T(128)S(1)}, f32[128]{0:T(128)}, u32[]{:S(2)}) copy-start(f32[128]{0:T(128)} %constant.25) | copy-start | bytes 1540
  2.7 13.3 %collective-permute-start = (bf16[1088,256]{1,0:T(8,128)(2,1)}, bf16[1088,256]{1,0:T(8,128)(2,1)S(1)}, u32[]{:S(2)}, u32[]{:S(2)}) collective-permute-start(bf16[1088,256]{1,0:T(8,128)(2,1)} %pack.1.refs_0_), channel_id=1, source_target_pairs={{0,4},{1,29},{4,8},{5,1},{8,12},{9,5},{12,16},{13,9},{16,20},{17,1... | collective-permute-start | bytes 1671176 | tf_op jit(solution)/shard_map/ppermute | solution.py:603
  14.9 8.8 %copy-start.1 = (f32[320,512]{1,0:T(8,128)S(1)}, f32[320,512]{1,0:T(8,128)}, u32[]{:S(2)}) copy-start(f32[320,512]{1,0:T(8,128)} %get-tuple-element.40.keep) | copy-start | bytes 1966084
  14.9 8.8 %collective-permute-start.2 = (bf16[320,512]{1,0:T(8,128)(2,1)}, bf16[320,512]{1,0:T(8,128)(2,1)S(1)}, u32[]{:S(2)}, u32[]{:S(2)}) collective-permute-start(bf16[320,512]{1,0:T(8,128)(2,1)} %get-tuple-element.41), channel_id=1, source_target_pairs={{0,1},{1,0},{2,3},{3,2},{4,5},{5,4},{6,7},{7,6},{8,9},{9,8},{10,11... | collective-permute-start | bytes 983048 | tf_op jit(solution)/shard_map/ppermute | solution.py:57
  16.0 17.1 %copy-start.7 = (bf16[1088,256]{1,0:T(8,128)(2,1)}, bf16[1088,256]{1,0:T(8,128)(2,1)S(1)}, u32[]{:S(2)}) copy-start(bf16[1088,256]{1,0:T(8,128)(2,1)S(1)} %collective-permute-done.refs_1_) | copy-start | bytes 1671172
  16.0 17.1 %collective-permute-start.1 = (bf16[1088,256]{1,0:T(8,128)(2,1)S(1)}, bf16[1088,256]{1,0:T(8,128)(2,1)S(1)}, u32[]{:S(2)}, u32[]{:S(2)}) collective-permute-start(bf16[1088,256]{1,0:T(8,128)(2,1)S(1)} %collective-permute-done.refs_1_), channel_id=1, source_target_pairs={{0,4},{1,29},{4,8},{5,1},{8,12},{9,5},{12,16},{13,9},{16,20},{17,1... | collective-permute-start | bytes 1671176 | tf_op jit(solution)/shard_map/ppermute | solution.py:603
  23.8 8.4 %collective-permute-start.3 = (bf16[288,512]{1,0:T(8,128)(2,1)S(1)}, bf16[288,512]{1,0:T(8,128)(2,1)S(1)}, u32[]{:S(2)}, u32[]{:S(2)}) collective-permute-start(bf16[288,512]{1,0:T(8,128)(2,1)S(1)} %get-tuple-element.48), channel_id=1, source_target_pairs={{0,2},{2,0},{1,3},{3,1},{4,6},{6,4},{5,7},{7,5},{8,10},{10,8},{9,1... | collective-permute-start | bytes 884744 | tf_op jit(solution)/shard_map/ppermute | solution.py:57
  33.1 13.1 %copy-start.3 = (bf16[256,512]{1,0:T(8,128)(2,1)}, bf16[256,512]{1,0:T(8,128)(2,1)S(1)}, u32[]{:S(2)}) copy-start(bf16[256,512]{1,0:T(8,128)(2,1)S(1)} %get-tuple-element.51.near) | copy-start | bytes 786436
  33.1 10.3 %copy-start.8 = (bf16[1088,256]{1,0:T(8,128)(2,1)}, bf16[1088,256]{1,0:T(8,128)(2,1)S(1)}, u32[]{:S(2)}) copy-start(bf16[1088,256]{1,0:T(8,128)(2,1)S(1)} %collective-permute-done.1.refs_2_) | copy-start | bytes 1671172
  33.1 10.3 %collective-permute-start.5 = (bf16[1088,256]{1,0:T(8,128)(2,1)S(1)}, bf16[1088,256]{1,0:T(8,128)(2,1)S(1)}, u32[]{:S(2)}, u32[]{:S(2)}) collective-permute-start(bf16[1088,256]{1,0:T(8,128)(2,1)S(1)} %collective-permute-done.1.refs_2_), channel_id=1, source_target_pairs={{0,4},{1,29},{4,8},{5,1},{8,12},{9,5},{12,16},{13,9},{16,20},{17,1... | collective-permute-start | bytes 1671176 | tf_op jit(solution)/shard_map/ppermute | solution.py:603
  33.2 13.0 %collective-permute-start.4 = (bf16[256,512]{1,0:T(8,128)(2,1)S(1)}, bf16[256,512]{1,0:T(8,128)(2,1)}, u32[]{:S(2)}, u32[]{:S(2)}) collective-permute-start(bf16[256,512]{1,0:T(8,128)(2,1)S(1)} %get-tuple-element.51.near), channel_id=1, source_target_pairs={{0,1},{1,0},{2,3},{3,2},{4,5},{5,4},{6,7},{7,6},{8,9},{9,8},{10,11... | collective-permute-start | bytes 786440 | tf_op jit(solution)/shard_map/ppermute | solution.py:57
  33.6 50.4 %collective-permute-start.13 = (bf16[256,2048]{1,0:T(8,128)(2,1)}, bf16[256,2048]{1,0:T(8,128)(2,1)S(1)}, u32[]{:S(2)}, u32[]{:S(2)}) collective-permute-start(bf16[256,2048]{1,0:T(8,128)(2,1)} %get-tuple-element.62), channel_id=1, source_target_pairs={{0,64},{32,96},{64,0},{96,32},{1,65},{33,97},{65,1},{97,33},{2,66}... | collective-permute-start | bytes 3145736 | tf_op jit(solution)/shard_map/ppermute | solution.py:617
  36.5 49.8 %collective-permute-start.14 = (bf16[256,2048]{1,0:T(8,128)(2,1)}, bf16[256,2048]{1,0:T(8,128)(2,1)S(1)}, u32[]{:S(2)}, u32[]{:S(2)}) collective-permute-start(bf16[256,2048]{1,0:T(8,128)(2,1)} %get-tuple-element.63), channel_id=1, source_target_pairs={{0,32},{32,64},{64,96},{96,0},{1,33},{33,65},{65,97},{97,1},{2,34}... | collective-permute-start | bytes 3145736 | tf_op jit(solution)/shard_map/ppermute | solution.py:617
  36.9 49.4 %collective-permute-start.15 = (bf16[256,2048]{1,0:T(8,128)(2,1)}, bf16[256,2048]{1,0:T(8,128)(2,1)}, u32[]{:S(2)}, u32[]{:S(2)}) collective-permute-start(bf16[256,2048]{1,0:T(8,128)(2,1)} %get-tuple-element.64), channel_id=1, source_target_pairs={{0,96},{32,0},{64,32},{96,64},{1,97},{33,1},{65,33},{97,65},{2,98}... | collective-permute-start | bytes 3145736 | tf_op jit(solution)/shard_map/ppermute | solution.py:617
  39.2 19.5 %all-to-all-start = ((bf16[8,64,256]{2,1,0:T(8,128)(2,1)}), bf16[8,64,256]{2,1,0:T(8,128)(2,1)}, u32[]{:S(2)}, u32[]{:S(2)}) async-start(bf16[8,64,256]{2,1,0:T(8,128)(2,1)} %get-tuple-element.52.notes), calls=%async_computation | async-start | bytes 524288 | tf_op jit(solution)/shard_map/all_to_all | solution.py:630
  43.4 2.8 %copy-start.4 = (bf16[1088,256]{1,0:T(8,128)(2,1)}, bf16[1088,256]{1,0:T(8,128)(2,1)S(1)}, u32[]{:S(2)}) copy-start(bf16[1088,256]{1,0:T(8,128)(2,1)S(1)} %collective-permute-done.5.refs_3_) | copy-start | bytes 1671172
  43.4 15.2 %collective-permute-start.6 = (bf16[544,256]{1,0:T(8,128)(2,1)S(1)}, bf16[544,256]{1,0:T(8,128)(2,1)}, u32[]{:S(2)}, u32[]{:S(2)}) collective-permute-start(bf16[544,256]{1,0:T(8,128)(2,1)S(1)} %slice.4), channel_id=1, source_target_pairs={{0,4},{1,29},{4,8},{5,1},{8,12},{9,5},{12,16},{13,9},{16,20},{17,1... | collective-permute-start | bytes 835592 | tf_op jit(solution)/shard_map/ppermute | solution.py:603
  58.6 33.5 %copy-start = (bf16[256,2048]{1,0:T(8,128)(2,1)S(1)}, bf16[256,2048]{1,0:T(8,128)(2,1)}, u32[]{:S(2)}) copy-start(bf16[256,2048]{1,0:T(8,128)(2,1)} %get-tuple-element.61.refs_4_) | copy-start | bytes 3145732
  66.5 6.5 %collective-permute-start.7 = (bf16[272,256]{1,0:T(8,128)(2,1)}, bf16[272,256]{1,0:T(8,128)(2,1)S(1)}, u32[]{:S(2)}, u32[]{:S(2)}) collective-permute-start(bf16[272,256]{1,0:T(8,128)(2,1)} %get-tuple-element.58), channel_id=1, source_target_pairs={{0,1},{1,0},{2,3},{3,2},{4,5},{5,4},{6,7},{7,6},{8,9},{9,8},{10,11... | collective-permute-start | bytes 417800 | tf_op jit(solution)/shard_map/ppermute | solution.py:57
  71.7 5.5 %collective-permute-start.8 = (bf16[272,256]{1,0:T(8,128)(2,1)}, bf16[272,256]{1,0:T(8,128)(2,1)S(1)}, u32[]{:S(2)}, u32[]{:S(2)}) collective-permute-start(bf16[272,256]{1,0:T(8,128)(2,1)} %get-tuple-element.59), channel_id=1, source_target_pairs={{0,2},{2,0},{1,3},{3,1},{4,6},{6,4},{5,7},{7,5},{8,10},{10,8},{9,1... | collective-permute-start | bytes 417800 | tf_op jit(solution)/shard_map/ppermute | solution.py:57
  72.9 7.8 %collective-permute-start.9 = (bf16[272,256]{1,0:T(8,128)(2,1)}, bf16[272,256]{1,0:T(8,128)(2,1)S(1)}, u32[]{:S(2)}, u32[]{:S(2)}) collective-permute-start(bf16[272,256]{1,0:T(8,128)(2,1)} %get-tuple-element.60), channel_id=1, source_target_pairs={{0,3},{1,2},{2,1},{3,0},{4,7},{5,6},{6,5},{7,4},{8,11},{9,10},{10,... | collective-permute-start | bytes 417800 | tf_op jit(solution)/shard_map/ppermute | solution.py:641
  80.7 0.9 copy-start.2
  82.2 6.8 %collective-permute-start.10 = (bf16[256,256]{1,0:T(8,128)(2,1)S(1)}, bf16[256,256]{1,0:T(8,128)(2,1)S(1)}, u32[]{:S(2)}, u32[]{:S(2)}) collective-permute-start(bf16[256,256]{1,0:T(8,128)(2,1)S(1)} %merge.1.refs_0_), channel_id=1, source_target_pairs={{0,64},{32,96},{64,0},{96,32},{1,65},{33,97},{65,1},{97,33},{2,66}... | collective-permute-start | bytes 393224 | tf_op jit(solution)/shard_map/ppermute | solution.py:645
  83.6 8.5 %collective-permute-start.11 = (bf16[256,256]{1,0:T(8,128)(2,1)S(1)}, bf16[256,256]{1,0:T(8,128)(2,1)S(1)}, u32[]{:S(2)}, u32[]{:S(2)}) collective-permute-start(bf16[256,256]{1,0:T(8,128)(2,1)S(1)} %merge.1.refs_0_), channel_id=1, source_target_pairs={{0,32},{32,64},{64,96},{96,0},{1,33},{33,65},{65,97},{97,1},{2,34}... | collective-permute-start | bytes 393224 | tf_op jit(solution)/shard_map/ppermute | solution.py:645
  84.0 8.1 %collective-permute-start.12 = (bf16[256,256]{1,0:T(8,128)(2,1)S(1)}, bf16[256,256]{1,0:T(8,128)(2,1)S(1)}, u32[]{:S(2)}, u32[]{:S(2)}) collective-permute-start(bf16[256,256]{1,0:T(8,128)(2,1)S(1)} %merge.1.refs_0_), channel_id=1, source_target_pairs={{0,96},{32,0},{64,32},{96,64},{1,97},{33,1},{65,33},{97,65},{2,98}... | collective-permute-start | bytes 393224 | tf_op jit(solution)/shard_map/ppermute | solution.py:645
  94.6 2.1 %collective-permute-start.16 = (bf16[256,1024]{1,0:T(8,128)(2,1)S(1)}, bf16[256,1024]{1,0:T(8,128)(2,1)S(1)}, u32[]{:S(2)}, u32[]{:S(2)}) collective-permute-start(bf16[256,1024]{1,0:T(8,128)(2,1)S(1)} %get-tuple-element.66), channel_id=1, source_target_pairs={{0,1},{1,0},{2,3},{3,2},{4,5},{5,4},{6,7},{7,6},{8,9},{9,8},{10,11... | collective-permute-start | bytes 1572872 | tf_op jit(solution)/shard_map/ppermute | solution.py:57
  96.8 6.3 %collective-permute-start.17 = (bf16[256,256]{1,0:T(8,128)(2,1)S(1)}, bf16[256,256]{1,0:T(8,128)(2,1)S(1)}, u32[]{:S(2)}, u32[]{:S(2)}) collective-permute-start(bf16[256,256]{1,0:T(8,128)(2,1)S(1)} %get-tuple-element.68), channel_id=1, source_target_pairs={{0,128},{2,130},{128,0},{130,2},{1,129},{3,131},{129,1},{131,3},{4... | collective-permute-start | bytes 393224 | tf_op jit(solution)/shard_map/ppermute | solution.py:650
  99.6 6.7 %collective-permute-start.18 = (bf16[256,256]{1,0:T(8,128)(2,1)S(1)}, bf16[256,256]{1,0:T(8,128)(2,1)S(1)}, u32[]{:S(2)}, u32[]{:S(2)}) collective-permute-start(bf16[256,256]{1,0:T(8,128)(2,1)S(1)} %get-tuple-element.69), channel_id=1, source_target_pairs={{0,2},{2,128},{128,130},{130,0},{1,3},{3,129},{129,131},{131,1},{4... | collective-permute-start | bytes 393224 | tf_op jit(solution)/shard_map/ppermute | solution.py:650
  99.6 6.7 %collective-permute-start.19 = (bf16[256,256]{1,0:T(8,128)(2,1)S(1)}, bf16[256,256]{1,0:T(8,128)(2,1)S(1)}, u32[]{:S(2)}, u32[]{:S(2)}) collective-permute-start(bf16[256,256]{1,0:T(8,128)(2,1)S(1)} %get-tuple-element.70), channel_id=1, source_target_pairs={{0,130},{2,0},{128,2},{130,128},{1,131},{3,1},{129,3},{131,129},{4... | collective-permute-start | bytes 393224 | tf_op jit(solution)/shard_map/ppermute | solution.py:650

commit v4 on v3

--- a/solution.py
+++ b/solution.py
@@ -45,8 +45,8 @@
     return pltpu.CompilerParams(vmem_limit_bytes=mib * 2**20)
 
 
-def cost(flops=0, moved=0, exps=0):
-    return pl.CostEstimate(flops=flops, bytes_accessed=moved, transcendentals=exps)
+SMALL = pl.CostEstimate(flops=1, bytes_accessed=1, transcendentals=0)
+MEDIUM = pl.CostEstimate(flops=2**27, bytes_accessed=2**18, transcendentals=2**10)
 
 
 def shift(n, by):
@@ -85,9 +85,13 @@
         table = jnp.where(lane == 0, place >> 1, jnp.where(lane == 1, place & 1, 0))
         load[i * HALF + ROWS : (i + 1) * HALF, :] = table.astype(F32).astype(BF16)
     copies = fetch(pairs, sems.at[:8])
-    for copy in copies:
-        copy.wait()
-    for copy in fetch([(load, out)], sems.at[8:]):
+    leaving = []
+    for i in range(4):
+        copies[2 * i].wait()
+        copies[2 * i + 1].wait()
+        to = slice(i * HALF, (i + 1) * HALF)
+        leaving += fetch([(load.at[to, :], out.at[to, :])], sems.at[8 + i : 9 + i])
+    for copy in leaving:
         copy.wait()
 
 
@@ -97,9 +101,9 @@
         out_shape=shaped((LOAD, PAIR), BF16),
         in_specs=[SMEM, HBM, HBM],
         out_specs=HBM,
-        scratch_shapes=[pltpu.VMEM((LOAD, PAIR), BF16), pltpu.SemaphoreType.DMA((9,))],
+        scratch_shapes=[pltpu.VMEM((LOAD, PAIR), BF16), pltpu.SemaphoreType.DMA((12,))],
         compiler_params=params(),
-        cost_estimate=cost(moved=2**19),
+        cost_estimate=SMALL,
         name="pack",
     )(places, keys, values)
 
@@ -135,63 +139,69 @@
             pltpu.SemaphoreType.DMA((4,)),
         ],
         compiler_params=params(),
-        cost_estimate=cost(moved=8 * 2**20),
+        cost_estimate=SMALL,
         name="columns",
     )(weight)
 
 
-def first_kernel(
-    tokens, query, key, value, send, keep, tok, tiles, kv, fresh, sems
-):
+def first_kernel(tokens, query, key, value, send, keep, tok, wide, kv, sent, fresh, sems):
     core = lax.axis_index("hid_1")
-    pairs = [(tokens, tok)]
+    deep = tok.shape[2]
+    copies = []
     for t in range(4):
-        side = 1 - core if t < 2 else core
-        cols = pl.ds(pl.multiple_of(side * 512 + (t % 2) * ROWS, ROWS), ROWS)
-        pairs.append((query.at[:, cols], tiles.at[t]))
-        if t == 1:
-            pairs.append((key, kv.at[0]))
-            pairs.append((value, kv.at[1]))
-    copies = fetch(pairs, sems)
-    copies[0].wait()
-
-    def part(t):
-        return jnp.dot(tok[...], tiles[t], preferred_element_type=F32)
-
-    for t in range(2):
-        copies[1 + t].wait()
-        send[:ROWS, t * ROWS : (t + 1) * ROWS] = part(t).astype(BF16)
-    copies[3].wait()
-    copies[4].wait()
-    both = jnp.concatenate([kv[0], kv[1]], axis=1)
-    fresh[...] = jnp.dot(tok[...], both, preferred_element_type=F32)
+        part = slice(t * deep, (t + 1) * deep)
+        pairs = [
+            (tokens.at[:, part], tok.at[t]),
+            (query.at[part, :], wide.at[t]),
+            (key.at[part, :], kv.at[t, :, :HD]),
+            (value.at[part, :], kv.at[t, :, HD:]),
+        ]
+        copies.append(fetch(pairs, sems.at[4 * t : 4 * t + 4]))
+    far_cols = pl.ds(pl.multiple_of((1 - core) * 512, 512), 512)
+    near_cols = pl.ds(pl.multiple_of(core * 512, 512), 512)
+    for t in range(4):
+        for copy in copies[t]:
+            copy.wait()
+        a = tok[t]
+        far = jnp.dot(a, wide[t, :, far_cols], preferred_element_type=F32)
+        near = jnp.dot(a, wide[t, :, near_cols], preferred_element_type=F32)
+        new = jnp.dot(a, kv[t], preferred_element_type=F32)
+        if t == 0:
+            sent[...] = far
+            keep[:ROWS, :] = near
+            fresh[...] = new
+        else:
+            keep[:ROWS, :] += near
+            fresh[...] += new
+            if t == 3:
+                send[:ROWS, :] = (sent[...] + far).astype(BF16)
+            else:
+                sent[...] += far
     for t in range(2):
         cols = slice(t * PAIR, (t + 1) * PAIR)
-        far = pl.ds(pl.multiple_of((1 - core) * 128 + t * NEW, NEW), NEW)
-        near = pl.ds(pl.multiple_of(core * 128 + t * NEW, NEW), NEW)
-        send[ROWS:, cols] = fresh[far, :].astype(BF16)
-        keep[ROWS:, cols] = fresh[near, :]
-    for t in range(2):
-        copies[5 + t].wait()
-        keep[:ROWS, t * ROWS : (t + 1) * ROWS] = part(2 + t)
+        far_rows = pl.ds(pl.multiple_of((1 - core) * 128 + t * NEW, NEW), NEW)
+        near_rows = pl.ds(pl.multiple_of(core * 128 + t * NEW, NEW), NEW)
+        send[ROWS:, cols] = fresh[far_rows, :].astype(BF16)
+        keep[ROWS:, cols] = fresh[near_rows, :]
 
 
 def first(tokens, query, key, value):
-    deep = tokens.shape[1]
+    deep = tokens.shape[1] // 4
     return pl.pallas_call(
         first_kernel,
         out_shape=[shaped((320, 512), BF16), shaped((320, 512), F32)],
         in_specs=[HBM] * 4,
         out_specs=[VMEM] * 2,
         scratch_shapes=[
-            pltpu.VMEM((ROWS, deep), BF16),
-            pltpu.VMEM((4, deep, ROWS), BF16),
-            pltpu.VMEM((2, deep, HD), BF16),
+            pltpu.VMEM((4, ROWS, deep), BF16),
+            pltpu.VMEM((4, deep, query.shape[1]), BF16),
+            pltpu.VMEM((4, deep, PAIR), BF16),
+            pltpu.VMEM((ROWS, 512), F32),
             pltpu.VMEM((ROWS, PAIR), F32),
-            pltpu.SemaphoreType.DMA((7,)),
+            pltpu.SemaphoreType.DMA((16,)),
         ],
         compiler_params=params(),
-        cost_estimate=cost(flops=2 * 256 * 2048 * 1280, moved=6 * 2**20),
+        cost_estimate=SMALL,
         name="first",
     )(tokens, query, key, value)
 
@@ -217,7 +227,7 @@
         in_specs=[VMEM] * 2,
         out_specs=[VMEM] * 2,
         compiler_params=params(8),
-        cost_estimate=cost(flops=2**18, moved=2**20),
+        cost_estimate=SMALL,
         name="second",
     )(keep, got)
 
@@ -249,7 +259,7 @@
         in_specs=[VMEM] * 4,
         out_specs=[VMEM] * 2,
         compiler_params=params(8),
-        cost_estimate=cost(flops=2**20, moved=2**20),
+        cost_estimate=SMALL,
         name="rotated",
     )(keep, got, cosine, sine)
 
@@ -333,7 +343,7 @@
     sources, (q_out, acc_out, peak_out) = refs[:count], refs[count : count + 3]
     refs = refs[count + 3 :]
     near_in, far_in, own, *loads = refs[: 3 + count]
-    q_all, acc_all, peak_all, keys, values, scores, peak_ref, sems = refs[3 + count :]
+    q_all, acc_all, peak_all, keys, values, scores, peak_ref, acc, sems = refs[3 + count :]
     pairs = [(sources[0].at[: 2 * HALF, :], loads[0])] + list(zip(sources[1:], loads[1:]))
     pairs += [(notes.at[0], own), (near, near_in), (far, far_in)]
     copies = fetch(pairs, sems.at[: count + 3])
@@ -383,9 +393,10 @@
             return jnp.dot(p.astype(BF16), own_values, preferred_element_type=F32)
 
         peak = attend(
-            q, peak_ref, chunks, keys, values, scores, chunk, acc_all.at[at, :], before
+            q, peak_ref, chunks, keys, values, scores, chunk, acc, before
         )
-        peak_all[at, :] = jnp.broadcast_to(peak, (TALL, HD))
+        acc_all[at, :] = acc[:, :HD]
+        peak_all[at, :] = jnp.where(lane < HD // 2, peak, acc[:, HD:])
         first_sem = count + 4 + 2 * step
         out += fetch(
             [
@@ -399,9 +410,10 @@
 
 
 def attend_near(slabs, near, far, notes, loads):
-    count, chunk = len(loads), 1792
-    height = (2 + 4 * (count - 1)) * ROWS
-    state = [((8 * ROWS, HD), BF16), ((8 * ROWS, PAIR), F32), ((8 * ROWS, HD), F32)]
+    count, chunk = len(loads), 1280
+    shapes = [(2 * HALF, PAIR)] + [a.shape for a in loads[1:]]
+    height = sum(shape[0] // HALF * ROWS for shape in shapes)
+    state = [((8 * ROWS, HD), BF16), ((8 * ROWS, HD), F32), ((8 * ROWS, HD), F32)]
     return pl.pallas_call(
         functools.partial(near_kernel, chunk=chunk, count=count),
         out_shape=[shaped(*s) for s in state],
@@ -411,27 +423,28 @@
             pltpu.VMEM((ROWS, 4 * HD), BF16),
             pltpu.VMEM((ROWS, 4 * HD), BF16),
             pltpu.VMEM((NEW, PAIR), BF16),
-            pltpu.VMEM((2 * HALF, PAIR), BF16),
-            *[pltpu.VMEM((LOAD, PAIR), BF16)] * (count - 1),
+            *[pltpu.VMEM(shape, BF16) for shape in shapes],
             *[pltpu.VMEM(*s) for s in state],
             pltpu.VMEM((height, HD), BF16),
             pltpu.VMEM((height, PAIR), BF16),
             pltpu.VMEM((height // chunk, TALL, chunk), F32),
             pltpu.VMEM((TALL, HD), F32),
+            pltpu.VMEM((TALL, PAIR), F32),
             pltpu.SemaphoreType.DMA((count + 4 + 2 * (8 * ROWS // TALL),)),
         ],
         compiler_params=params(),
-        cost_estimate=cost(8 * ROWS * height * HD * 6, 2**23, 8 * ROWS * height),
+        cost_estimate=SMALL,
         name="near",
     )(slabs, near, far, notes, *loads)
 
 
-def far_kernel(slabs, *refs, chunk, count):
-    sources, outs = refs[: 4 + count], refs[4 + count : 8 + count]
-    refs = refs[8 + count :]
+def far_kernel(slabs, *refs, chunk, count, start, tall):
+    sources, out = refs[: 4 + count], refs[4 + count]
+    refs = refs[5 + count :]
     buffers = refs[: 4 + count]
     queries, acc_in, peak_in, new, *loads = buffers
     keys, values, scores, peak_ref, acc, sems = refs[4 + count :]
+    sources = [ref.at[start : start + tall, :] for ref in sources[:3]] + list(sources[3:])
     copies = fetch(list(zip(sources, buffers))[::-1], sems)
     mine = slabs[lax.axis_index("key")]
     for copy in copies[: count + 1]:
@@ -439,65 +452,75 @@
     chunks = gather_visible(mine, slabs, halves_of(loads), new, keys, values, chunk)
     for copy in copies[count + 1 :]:
         copy.wait()
+    peak_ref[...] = jnp.broadcast_to(peak_in[:, :1], (tall, HD))
+
+    def before(peak):
+        factor = jnp.exp2((peak_in[:, :1] - peak) * EXPONENT)
+        total = jnp.broadcast_to(peak_in[:, HD // 2 : HD // 2 + 1], (tall, HD))
+        return jnp.concatenate([acc_in[...], total], axis=1) * factor
+
+    peak = attend(
+        queries[...], peak_ref, chunks, keys, values, scores, chunk, acc, before
+    )
+    total = acc[:, HD:]
+    heads = (acc[:, :HD] / jnp.where(total > 0.0, total, 1.0)).astype(BF16)
+    lane = lax.broadcasted_iota(jnp.int32, (ROWS, HD), 1)
+    totals = jnp.zeros((ROWS, HD), F32)
+    peaks = jnp.zeros((ROWS, HD), F32)
+    for h in range(tall // ROWS):
+        rows = slice(h * ROWS, (h + 1) * ROWS)
+        totals = jnp.where(lane == h, total[rows], totals)
+        peaks = jnp.where(lane == h, peak[rows], peaks)
+    some = totals > 0.0
+    level = peaks * EXPONENT + jnp.log2(jnp.where(some, totals, 1.0))
+    level = jnp.transpose(jnp.where(some, level, NEGATIVE))
     where = lax.broadcasted_iota(jnp.int32, (16, ROWS), 0)
-    for step in range(8 * ROWS // TALL):
-        at = slice(step * TALL, (step + 1) * TALL)
-        peak_ref[...] = peak_in[at, :]
-
-        def before(peak, at=at):
-            factor = jnp.exp2((peak_in[at, :1] - peak) * EXPONENT)
-            return acc_in[at, :] * factor
-
-        peak = attend(
-            queries[at, :], peak_ref, chunks, keys, values, scores, chunk, acc, before
-        )
-        total = acc[:, HD:]
-        some = total > 0.0
-        safe = jnp.where(some, total, 1.0)
-        heads = (acc[:, :HD] / safe).astype(BF16)
-        level = jnp.where(some, peak * EXPONENT + jnp.log2(safe), NEGATIVE)
-        level = jnp.transpose(level)[:1, :]
-        for t in range(TALL // (2 * ROWS)):
-            out = outs[step * (TALL // (2 * ROWS)) + t]
-            table = jnp.zeros((16, ROWS), F32)
-            for half in range(2):
-                rows = slice((2 * t + half) * ROWS, (2 * t + half + 1) * ROWS)
-                out[:ROWS, half * HD : (half + 1) * HD] = heads[rows]
-                rest = level[:, rows]
-                for k in range(3):
-                    coded = rest.astype(BF16).astype(F32)
-                    table = jnp.where(where == 3 * half + k, coded, table)
-                    rest = rest - coded
-            out[ROWS:, :] = table.astype(BF16)
-
-
-def attend_far(slabs, queries, acc, peak, new, loads):
+    if start > 0:
+        out[hid_index()] = jnp.zeros((MSG, PAIR), BF16)
+    for t in range(tall // (2 * ROWS)):
+        slot = jnp.bitwise_xor(hid_index(), start // (2 * ROWS) + t) if start > 0 else 0
+        table = jnp.zeros((16, ROWS), F32)
+        for half in range(2):
+            h = 2 * t + half
+            cols = slice(half * HD, (half + 1) * HD)
+            out[slot, :ROWS, cols] = heads[h * ROWS : (h + 1) * ROWS]
+            rest = level[h : h + 1, :]
+            for k in range(3):
+                coded = rest.astype(BF16).astype(F32)
+                table = jnp.where(where == 3 * half + k, coded, table)
+                rest = rest - coded
+        out[slot, ROWS:, :] = table.astype(BF16)
+
+
+def attend_far(start, tall, slabs, queries, acc, peak, new, loads):
     operands = [queries, acc, peak, new, *loads]
     count, chunk = len(loads), 1024
     height = sum(a.shape[0] // HALF * ROWS for a in loads) + 8 * NEW
     height = -(-height // chunk) * chunk
-    return pl.pallas_call(
-        functools.partial(far_kernel, chunk=chunk, count=count),
-        out_shape=[shaped((MSG, PAIR), BF16)] * 4,
+    shapes = [(tall, HD)] * 3 + [a.shape for a in operands[3:]]
+    return pl.pallas_call(
+        functools.partial(far_kernel, chunk=chunk, count=count, start=start, tall=tall),
+        out_shape=shaped((4 if start > 0 else 1, MSG, PAIR), BF16),
         in_specs=[SMEM] + [HBM] * len(operands),
-        out_specs=[VMEM] * 4,
+        out_specs=VMEM,
         scratch_shapes=[
-            *[pltpu.VMEM(a.shape, a.dtype) for a in operands],
+            *[pltpu.VMEM(shape, a.dtype) for shape, a in zip(shapes, operands)],
             pltpu.VMEM((height, HD), BF16),
             pltpu.VMEM((height, PAIR), BF16),
-            pltpu.VMEM((height // chunk, TALL, chunk), F32),
-            pltpu.VMEM((TALL, HD), F32),
-            pltpu.VMEM((TALL, PAIR), F32),
+            pltpu.VMEM((height // chunk, tall, chunk), F32),
+            pltpu.VMEM((tall, HD), F32),
+            pltpu.VMEM((tall, PAIR), F32),
             pltpu.SemaphoreType.DMA((len(operands),)),
         ],
         compiler_params=params(),
-        cost_estimate=cost(8 * ROWS * height * HD * 6, 2**23, 8 * ROWS * height),
-        name="far",
+        cost_estimate=MEDIUM,
+        name="far%d" % start,
     )(slabs, *operands)
 
 
-def merge_kernel(*refs):
-    parts, out = refs[:4], refs[4]
+def merge_kernel(own, got, out):
+    quarter = hid_index()
+    parts = [own.at[0]] + [got.at[jnp.bitwise_xor(quarter, j)] for j in range(1, 4)]
     levels = []
     for ref in parts:
         t = ref[ROWS:, :].astype(F32)
@@ -520,16 +543,16 @@
         out[:, cols] = so_far.astype(BF16)
 
 
-def merge(parts):
+def merge(own, got):
     return pl.pallas_call(
         merge_kernel,
         out_shape=shaped((ROWS, PAIR), BF16),
-        in_specs=[VMEM] * 4,
+        in_specs=[VMEM] * 2,
         out_specs=VMEM,
         compiler_params=params(8),
-        cost_estimate=cost(10**6, 10**6, 4096),
+        cost_estimate=SMALL,
         name="merge",
-    )(*parts)
+    )(own, got)
 
 
 def project_kernel(*refs):
@@ -552,7 +575,7 @@
         in_specs=[VMEM] * 8,
         out_specs=[VMEM] * 2,
         compiler_params=params(16),
-        cost_estimate=cost(flops=2 * ROWS * 8 * HD * width, moved=6 * 2**20),
+        cost_estimate=SMALL,
         name="project",
     )(*heads, *weights)
 
@@ -575,7 +598,7 @@
         in_specs=[VMEM] * 2,
         out_specs=[VMEM] * 4,
         compiler_params=params(8),
-        cost_estimate=cost(flops=2**18, moved=2**21),
+        cost_estimate=SMALL,
         name="split",
     )(keep, got)
 
@@ -622,25 +645,23 @@
     sign = np.where(np.arange(HD) < middle, -1.0, 1.0).astype(np.float32)
     spots = slab_places[key_index] * ROWS + jnp.arange(ROWS, dtype=jnp.int32)
     angles = spots.astype(F32)[:, None] * frequency[None, :]
-    queries, notes = rotated(keep, got, jnp.cos(angles), jnp.sin(angles) * sign[None, :])
-    two, queries, notes = lax.optimization_barrier((two, queries, notes))
+    cosine, sine = jnp.cos(angles), jnp.sin(angles) * sign[None, :]
+    two, cosine, sine = lax.optimization_barrier((two, cosine, sine))
     three = away(two, 1)
+    queries, notes = rotated(keep, got, cosine, sine)
     far = swap(queries, "hid_1")
+    far, onward = lax.optimization_barrier((far, two[: 2 * HALF]))
+    four = away(onward, 2)
 
     new = lax.all_to_all(notes, "key", split_axis=0, concat_axis=0, tiled=True)
 
-    four = away(three[: 2 * HALF], 1)
-    state = attend_near(slab_places, queries, far, notes, [load, one, two, three])
-    parts = attend_far(slab_places, *state, new, [four])
-    flip = [(0, 3), (1, 2), (2, 1), (3, 0)]
-    merged = merge(
-        [
-            parts[0],
-            swap(parts[1], "hid_1"),
-            swap(parts[2], "hid_0"),
-            lax.ppermute(parts[3], HID, flip),
-        ]
-    )
+    state = attend_near(slab_places, queries, far, notes, [load, one, two])
+    late = attend_far(2 * ROWS, 6 * ROWS, slab_places, *state, new, [three, four])
+    got = lax.all_to_all(late, HID, split_axis=0, concat_axis=0, tiled=True)
+    state, late = lax.optimization_barrier((state, late))
+    own = attend_far(0, 2 * ROWS, slab_places, *state, new, [three, four])
+    got, weights = lax.optimization_barrier((got, weights))
+    merged = merge(own, got)
 
     heads = [merged] + [lax.ppermute(merged, "head_1", shift(4, by)) for by in (2, 1, 3)]
     send, keep = project(heads, weights)

time: 107 us -> 107 us (level)
  the two profiles are of different devices: /device:TPU:1 before, /device:TPU:64 now
where the time goes in v4:
time: 107 us
  Pallas kernels  45 us (42%)
  starting transfers between devices  36.4 us (34%)
  waiting for transfers between devices  20.1 us (19%)
  local copies, waits for them, and re-layouts  3.56 us (3%)
  other arithmetic  1.25 us (1%)
    pallas_call x2, Pallas kernels, attend_far(): pl.pallas_call(functools.partial(far_kernel, chunk=chunk, count=count, st...  16.1 us
    pallas_call x1, Pallas kernels, attend_near(): pl.pallas_call(functools.partial(near_kernel, chunk=chunk, count=count),...  13.8 us
    ppermute x4, starting transfers between devices, away(): return lax.ppermute(array, ('key', 'hid_1'), pairs)  12 us
    ppermute x3, starting transfers between devices, body(): weights.append(lax.ppermute(piece, 'head_1', shift(4, by)))  6.52 us
    ppermute x3, waiting for transfers between devices, body(): out = out + lax.ppermute(blocks[by - 1], ALONG_X, shift(4, by)).astype(F32)  6.42 us
    ppermute x3, waiting for transfers between devices, body(): lax.ppermute(merged, 'head_1', shift(4, by))  5.82 us
    ppermute x3, starting transfers between devices, body(): out = out + lax.ppermute(blocks[by - 1], ALONG_X, shift(4, by)).astype(F32)  4.82 us
    pallas_call x1, Pallas kernels, first(): pl.pallas_call(first_kernel, out_shape=[shaped((320, 512), BF16), shaped(...  4.54 us
  transfers between devices with their start and end apart: 19, of which 7 were waited for; matrix products, arithmetic and copies ran while one was open for 1% of the time, Pallas kernels for 36%

profile of v4, /device:TPU:64, one launch (start us, length us, event | category | flops | bytes accessed | tf_op | source)
XLA Modules:
  0.0 107.3 jit_solution(11684096042441705410)
XLA Ops:
  0.0 2.7 %pack.1.refs_0_ = bf16[1088,256]{1,0:T(8,128)(2,1)} custom-call(s32[8]{0:T(128)} %places.1, bf16[2048,128]{1,0:T(8,128)(2,1)} %bitcast.3, bf16[2048,128]{1,0:T(8,128)(2,1)} %bitcast.4), custom_call_target="tpu_custom_call" | custom-call | flops 1 | bytes 1 | tf_op jit(solution)/shard_map/pack/pallas_call | solution.py:99
  2.7 0.0 copy-start.10
  2.7 0.0 copy-start.11
  2.7 2.0 %collective-permute-start = (bf16[1088,256]{1,0:T(8,128)(2,1)}, bf16[1088,256]{1,0:T(8,128)(2,1)S(1)}, u32[]{:S(2)}, u32[]{:S(2)}) collective-permute-start(bf16[1088,256]{1,0:T(8,128)(2,1)} %pack.1.refs_0_), channel_id=1, source_target_pairs={{0,4},{1,29},{4,8},{5,1},{8,12},{9,5},{12,16},{13,9},{16,20},{17,1... | collective-permute-start | bytes 1671176 | tf_op jit(solution)/shard_map/ppermute | solution.py:626
  4.7 4.5 %first.1 = (bf16[320,512]{1,0:T(8,128)(2,1)}, f32[320,512]{1,0:T(8,128)}) custom-call(bf16[256,2048]{1,0:T(8,128)(2,1)} %tokens.1, bf16[2048,1024]{1,0:T(8,128)(2,1)} %query.1, bf16[2048,128]{1,0:T(8,128)(2,1)} %key.1, bf16[2048,128]{1,0:T(8,128)(2,1)} %value.1), custom_call_target="tpu_custom_call" | custom-call | flops 1 | bytes 1 | tf_op jit(solution)/shard_map/first/pallas_call | solution.py:190
  9.2 0.1 collective-permute-start.1
  9.3 3.2 %collective-permute-done.refs_1_ = bf16[1088,256]{1,0:T(8,128)(2,1)S(1)} collective-permute-done((bf16[1088,256]{1,0:T(8,128)(2,1)}, bf16[1088,256]{1,0:T(8,128)(2,1)S(1)}, u32[]{:S(2)}, u32[]{:S(2)}) %collective-permute-start) | collective-permute-done | bytes 557088 | tf_op jit(solution)/shard_map/ppermute | solution.py:626
  12.5 2.7 %collective-permute-start.3 = (bf16[1088,256]{1,0:T(8,128)(2,1)S(1)}, bf16[1088,256]{1,0:T(8,128)(2,1)S(1)}, u32[]{:S(2)}, u32[]{:S(2)}) collective-permute-start(bf16[1088,256]{1,0:T(8,128)(2,1)S(1)} %collective-permute-done.refs_1_), channel_id=1, source_target_pairs={{0,4},{1,29},{4,8},{5,1},{8,12},{9,5},{12,16},{13,9},{16,20},{17,1... | collective-permute-start | bytes 1671176 | tf_op jit(solution)/shard_map/ppermute | solution.py:626
  15.2 0.6 dynamic_slice.3
  16.4 0.0 collective-permute-done.1.got
  16.4 1.1 %copy-done.1 = f32[320,512]{1,0:T(8,128)S(1)} copy-done((f32[320,512]{1,0:T(8,128)S(1)}, f32[320,512]{1,0:T(8,128)}, u32[]{:S(2)}) %copy-start.1) | copy-done | bytes 655384
  17.5 0.1 second.1
  17.6 1.6 %collective-permute-start.2 = (bf16[288,512]{1,0:T(8,128)(2,1)S(1)}, bf16[288,512]{1,0:T(8,128)(2,1)S(1)}, u32[]{:S(2)}, u32[]{:S(2)}) collective-permute-start(bf16[288,512]{1,0:T(8,128)(2,1)S(1)} %get-tuple-element.53), channel_id=1, source_target_pairs={{0,2},{2,0},{1,3},{3,1},{4,6},{6,4},{5,7},{7,5},{8,10},{10,8},{9,1... | collective-permute-start | bytes 884744 | tf_op jit(solution)/shard_map/ppermute | solution.py:57
  19.2 3.4 %columns.1 = (bf16[256,2048]{1,0:T(8,128)(2,1)}, bf16[256,2048]{1,0:T(8,128)(2,1)}, bf16[256,2048]{1,0:T(8,128)(2,1)}, bf16[256,2048]{1,0:T(8,128)(2,1)}) custom-call(bf16[256,8192]{1,0:T(8,128)(2,1)} %weight.1), custom_call_target="tpu_custom_call" | custom-call | flops 1 | bytes 1 | tf_op jit(solution)/shard_map/columns/pallas_call | solution.py:131
  22.6 3.3 %collective-permute-start.7 = (bf16[256,2048]{1,0:T(8,128)(2,1)}, bf16[256,2048]{1,0:T(8,128)(2,1)S(1)}, u32[]{:S(2)}, u32[]{:S(2)}) collective-permute-start(bf16[256,2048]{1,0:T(8,128)(2,1)} %get-tuple-element.69), channel_id=1, source_target_pairs={{0,64},{32,96},{64,0},{96,32},{1,65},{33,97},{65,1},{97,33},{2,66}... | collective-permute-start | bytes 3145736 | tf_op jit(solution)/shard_map/ppermute | solution.py:640
  25.8 0.7 collective-permute-start.8
  26.5 2.6 %collective-permute-start.9 = (bf16[256,2048]{1,0:T(8,128)(2,1)}, bf16[256,2048]{1,0:T(8,128)(2,1)}, u32[]{:S(2)}, u32[]{:S(2)}) collective-permute-start(bf16[256,2048]{1,0:T(8,128)(2,1)} %get-tuple-element.71), channel_id=1, source_target_pairs={{0,96},{32,0},{64,32},{96,64},{1,97},{33,1},{65,33},{97,65},{2,98}... | collective-permute-start | bytes 3145736 | tf_op jit(solution)/shard_map/ppermute | solution.py:640
  29.1 0.5 fusion
  29.7 3.7 %collective-permute-start.5 = (bf16[1088,256]{1,0:T(8,128)(2,1)S(1)}, bf16[1088,256]{1,0:T(8,128)(2,1)S(1)}, u32[]{:S(2)}, u32[]{:S(2)}) collective-permute-start(bf16[1088,256]{1,0:T(8,128)(2,1)S(1)} %collective-permute-done.3.refs_2_), channel_id=1, source_target_pairs={{0,4},{1,29},{4,8},{5,1},{8,12},{9,5},{12,16},{13,9},{16,20},{17,1... | collective-permute-start | bytes 1671176 | tf_op jit(solution)/shard_map/ppermute | solution.py:626
  33.3 0.0 collective-permute-done.2.got
  33.3 0.9 rotated.1
  34.3 4.2 %all-to-all-start = ((bf16[8,64,256]{2,1,0:T(8,128)(2,1)}), bf16[8,64,256]{2,1,0:T(8,128)(2,1)S(1)}, u32[]{:S(2)}, u32[]{:S(2)}) async-start(bf16[8,64,256]{2,1,0:T(8,128)(2,1)} %get-tuple-element.60.notes), calls=%async_computation | async-start | bytes 524288 | tf_op jit(solution)/shard_map/all_to_all | solution.py:656
  38.5 3.7 %collective-permute-start.6 = (bf16[544,256]{1,0:T(8,128)(2,1)S(1)}, bf16[544,256]{1,0:T(8,128)(2,1)S(1)}, u32[]{:S(2)}, u32[]{:S(2)}) collective-permute-start(bf16[544,256]{1,0:T(8,128)(2,1)S(1)} %slice.3), channel_id=1, source_target_pairs={{0,8},{1,25},{4,12},{5,29},{8,16},{9,1},{12,20},{13,5},{16,24},{17... | collective-permute-start | bytes 835592 | tf_op jit(solution)/shard_map/ppermute | solution.py:626
  42.1 13.8 %near.1 = (bf16[2048,128]{1,0:T(8,128)(2,1)}, f32[2048,128]{1,0:T(8,128)}, f32[2048,128]{1,0:T(8,128)}) custom-call(s32[8]{0:T(128)} %slabs.5, bf16[256,512]{1,0:T(8,128)(2,1)} %copy-done.3, bf16[256,512]{1,0:T(8,128)(2,1)} %collective-permute-done.4.far, bf16[8,64,256]{2,1,0:T(8,128)(2,1)} %get-tuple-element.60.notes, bf16[1088,256]{1,0:T(8,128)(2,1)} %pack.1.refs_0_, ...), custom_call_target="tpu_custom_call" | custom-call | flops 1 | bytes 1 | tf_op jit(solution)/shard_map/near/pallas_call | solution.py:417
  56.0 0.7 copy-done.7
  56.7 0.0 copy-done.4
  56.8 0.2 copy-done.5
  57.0 9.8 %far512.1 = bf16[4,272,256]{2,1,0:T(8,128)(2,1)} custom-call(s32[8]{0:T(128)} %slabs.5, bf16[2048,128]{1,0:T(8,128)(2,1)} %get-tuple-element.65.refs_0_, f32[2048,128]{1,0:T(8,128)} %get-tuple-element.66.refs_1_, f32[2048,128]{1,0:T(8,128)} %get-tuple-element.67.refs_2_, bf16[8,64,256]{2,1,0:T(8,128)(2,1)} %copy-done.4, bf16[1088,256]{1,0:T(8,128)(2,1)} %copy-done.5, ...), custom_call_target="tpu_custom_call" | custom-call | flops 134217728 | bytes 262144 | tf_op jit(solution)/shard_map/far512/pallas_call | solution.py:501
  66.7 3.5 %all-to-all-start.1 = ((bf16[4,272,256]{2,1,0:T(8,128)(2,1)}), bf16[4,272,256]{2,1,0:T(8,128)(2,1)S(1)}, u32[]{:S(2)}, u32[]{:S(2)}) async-start(bf16[4,272,256]{2,1,0:T(8,128)(2,1)} %far512.1), calls=%async_computation.1 | async-start | bytes 1114112 | tf_op jit(solution)/shard_map/all_to_all | solution.py:660
  70.2 6.3 %far0.1.own = bf16[1,272,256]{2,1,0:T(8,128)(2,1)} custom-call(s32[8]{0:T(128)} %slabs.5, bf16[2048,128]{1,0:T(8,128)(2,1)} %get-tuple-element.65.refs_0_, f32[2048,128]{1,0:T(8,128)} %get-tuple-element.66.refs_1_, f32[2048,128]{1,0:T(8,128)} %get-tuple-element.67.refs_2_, bf16[8,64,256]{2,1,0:T(8,128)(2,1)} %copy-done.4, bf16[1088,256]{1,0:T(8,128)(2,1)} %copy-done.5, ...), custom_call_target="tpu_custom_call" | custom-call | flops 134217728 | bytes 262144 | tf_op jit(solution)/shard_map/far0/pallas_call | solution.py:501
  76.6 2.8 %all-to-all-done.1.got = bf16[4,272,256]{2,1,0:T(8,128)(2,1)S(1)} async-done(((bf16[4,272,256]{2,1,0:T(8,128)(2,1)}), bf16[4,272,256]{2,1,0:T(8,128)(2,1)S(1)}, u32[]{:S(2)}, u32[]{:S(2)}) %all-to-all-start.1) | async-done | bytes 557088 | tf_op jit(solution)/shard_map/all_to_all | solution.py:660
  79.4 0.9 copy-done.2
  80.3 0.6 merge.1.refs_0_
  80.9 0.1 collective-permute-start.10
  81.0 0.8 collective-permute-start.11
  81.8 2.5 %collective-permute-start.12 = (bf16[256,256]{1,0:T(8,128)(2,1)S(1)}, bf16[256,256]{1,0:T(8,128)(2,1)S(1)}, u32[]{:S(2)}, u32[]{:S(2)}) collective-permute-start(bf16[256,256]{1,0:T(8,128)(2,1)S(1)} %merge.1.refs_0_), channel_id=1, source_target_pairs={{0,96},{32,0},{64,32},{96,64},{1,97},{33,1},{65,33},{97,65},{2,98}... | collective-permute-start | bytes 393224 | tf_op jit(solution)/shard_map/ppermute | solution.py:666
  84.3 4.6 %collective-permute-done.10.refs_1_ = bf16[256,256]{1,0:T(8,128)(2,1)S(1)} collective-permute-done((bf16[256,256]{1,0:T(8,128)(2,1)S(1)}, bf16[256,256]{1,0:T(8,128)(2,1)S(1)}, u32[]{:S(2)}, u32[]{:S(2)}) %collective-permute-start.10) | collective-permute-done | bytes 131104 | tf_op jit(solution)/shard_map/ppermute | solution.py:666
  88.9 1.2 %collective-permute-done.11.refs_2_ = bf16[256,256]{1,0:T(8,128)(2,1)S(1)} collective-permute-done((bf16[256,256]{1,0:T(8,128)(2,1)S(1)}, bf16[256,256]{1,0:T(8,128)(2,1)S(1)}, u32[]{:S(2)}, u32[]{:S(2)}) %collective-permute-start.11) | collective-permute-done | bytes 131104 | tf_op jit(solution)/shard_map/ppermute | solution.py:666
  90.1 2.8 %project.1 = (bf16[256,1024]{1,0:T(8,128)(2,1)S(1)}, f32[256,1024]{1,0:T(8,128)S(1)}) custom-call(bf16[256,256]{1,0:T(8,128)(2,1)S(1)} %merge.1.refs_0_, bf16[256,256]{1,0:T(8,128)(2,1)S(1)} %collective-permute-done.10.refs_1_, bf16[256,256]{1,0:T(8,128)(2,1)S(1)} %collective-permute-done.11.refs_2_, bf16[256,256]{1,0:T(8,128)(2,1)S(1)} %collective-permute-done.12.refs_3_, ...), custom_call_target="tpu_custom_call" | custom-call | flops 1 | bytes 1 | tf_op jit(solution)/shard_map/project/pallas_call | solution.py:572
  92.9 0.3 collective-permute-start.13
  93.3 1.9 %collective-permute-done.13.got = bf16[256,1024]{1,0:T(8,128)(2,1)S(1)} collective-permute-done((bf16[256,1024]{1,0:T(8,128)(2,1)S(1)}, bf16[256,1024]{1,0:T(8,128)(2,1)S(1)}, u32[]{:S(2)}, u32[]{:S(2)}) %collective-permute-start.13) | collective-permute-done | bytes 524320 | tf_op jit(solution)/shard_map/ppermute | solution.py:57
  95.2 0.1 split.1
  95.3 2.0 %collective-permute-start.16 = (bf16[256,256]{1,0:T(8,128)(2,1)S(1)}, bf16[256,256]{1,0:T(8,128)(2,1)S(1)}, u32[]{:S(2)}, u32[]{:S(2)}) collective-permute-start(bf16[256,256]{1,0:T(8,128)(2,1)S(1)} %get-tuple-element.82), channel_id=1, source_target_pairs={{0,130},{2,0},{128,2},{130,128},{1,131},{3,1},{129,3},{131,129},{4... | collective-permute-start | bytes 393224 | tf_op jit(solution)/shard_map/ppermute | solution.py:671
  97.3 0.1 collective-permute-start.15
  97.4 2.7 %collective-permute-start.14 = (bf16[256,256]{1,0:T(8,128)(2,1)S(1)}, bf16[256,256]{1,0:T(8,128)(2,1)S(1)}, u32[]{:S(2)}, u32[]{:S(2)}) collective-permute-start(bf16[256,256]{1,0:T(8,128)(2,1)S(1)} %get-tuple-element.80), channel_id=1, source_target_pairs={{0,128},{2,130},{128,0},{130,2},{1,129},{3,131},{129,1},{131,3},{4... | collective-permute-start | bytes 393224 | tf_op jit(solution)/shard_map/ppermute | solution.py:671
  100.1 0.8 collective-permute-done.16
  100.9 5.6 %collective-permute-done.15 = bf16[256,256]{1,0:T(8,128)(2,1)S(1)} collective-permute-done((bf16[256,256]{1,0:T(8,128)(2,1)S(1)}, bf16[256,256]{1,0:T(8,128)(2,1)S(1)}, u32[]{:S(2)}, u32[]{:S(2)}) %collective-permute-start.15) | collective-permute-done | bytes 131104 | tf_op jit(solution)/shard_map/ppermute | solution.py:671
  106.5 0.7 add_convert_fusion
  (30 shorter events, 0.1 us)
Async XLA Ops:
  0.0 15.2 %copy-start.9 = (s32[8]{0:T(128)S(1)}, s32[8]{0:T(128)}, u32[]{:S(2)}) copy-start(s32[8]{0:T(128)} %slabs.5) | copy-start | bytes 100
  2.7 26.4 %copy-start.10 = (f32[128]{0:T(128)S(1)}, f32[128]{0:T(128)}, u32[]{:S(2)}) copy-start(f32[128]{0:T(128)} %constant.25) | copy-start | bytes 1540
  2.7 26.4 %copy-start.11 = (f32[128]{0:T(128)S(1)}, f32[128]{0:T(128)}, u32[]{:S(2)}) copy-start(f32[128]{0:T(128)} %constant.24) | copy-start | bytes 1540
  2.7 9.8 %collective-permute-start = (bf16[1088,256]{1,0:T(8,128)(2,1)}, bf16[1088,256]{1,0:T(8,128)(2,1)S(1)}, u32[]{:S(2)}, u32[]{:S(2)}) collective-permute-start(bf16[1088,256]{1,0:T(8,128)(2,1)} %pack.1.refs_0_), channel_id=1, source_target_pairs={{0,4},{1,29},{4,8},{5,1},{8,12},{9,5},{12,16},{13,9},{16,20},{17,1... | collective-permute-start | bytes 1671176 | tf_op jit(solution)/shard_map/ppermute | solution.py:626
  9.2 7.2 %collective-permute-start.1 = (bf16[320,512]{1,0:T(8,128)(2,1)}, bf16[320,512]{1,0:T(8,128)(2,1)S(1)}, u32[]{:S(2)}, u32[]{:S(2)}) collective-permute-start(bf16[320,512]{1,0:T(8,128)(2,1)} %get-tuple-element.46), channel_id=1, source_target_pairs={{0,1},{1,0},{2,3},{3,2},{4,5},{5,4},{6,7},{7,6},{8,9},{9,8},{10,11... | collective-permute-start | bytes 983048 | tf_op jit(solution)/shard_map/ppermute | solution.py:57
  12.5 21.7 %copy-start.8 = (bf16[1088,256]{1,0:T(8,128)(2,1)}, bf16[1088,256]{1,0:T(8,128)(2,1)S(1)}, u32[]{:S(2)}) copy-start(bf16[1088,256]{1,0:T(8,128)(2,1)S(1)} %collective-permute-done.refs_1_) | copy-start | bytes 1671172
  12.5 17.1 %collective-permute-start.3 = (bf16[1088,256]{1,0:T(8,128)(2,1)S(1)}, bf16[1088,256]{1,0:T(8,128)(2,1)S(1)}, u32[]{:S(2)}, u32[]{:S(2)}) collective-permute-start(bf16[1088,256]{1,0:T(8,128)(2,1)S(1)} %collective-permute-done.refs_1_), channel_id=1, source_target_pairs={{0,4},{1,29},{4,8},{5,1},{8,12},{9,5},{12,16},{13,9},{16,20},{17,1... | collective-permute-start | bytes 1671176 | tf_op jit(solution)/shard_map/ppermute | solution.py:626
  16.4 1.1 %copy-start.1 = (f32[320,512]{1,0:T(8,128)S(1)}, f32[320,512]{1,0:T(8,128)}, u32[]{:S(2)}) copy-start(f32[320,512]{1,0:T(8,128)} %get-tuple-element.45.keep) | copy-start | bytes 1966084
  17.6 15.7 %collective-permute-start.2 = (bf16[288,512]{1,0:T(8,128)(2,1)S(1)}, bf16[288,512]{1,0:T(8,128)(2,1)S(1)}, u32[]{:S(2)}, u32[]{:S(2)}) collective-permute-start(bf16[288,512]{1,0:T(8,128)(2,1)S(1)} %get-tuple-element.53), channel_id=1, source_target_pairs={{0,2},{2,0},{1,3},{3,1},{4,6},{6,4},{5,7},{7,5},{8,10},{10,8},{9,1... | collective-permute-start | bytes 884744 | tf_op jit(solution)/shard_map/ppermute | solution.py:57
  22.6 54.0 %collective-permute-start.7 = (bf16[256,2048]{1,0:T(8,128)(2,1)}, bf16[256,2048]{1,0:T(8,128)(2,1)S(1)}, u32[]{:S(2)}, u32[]{:S(2)}) collective-permute-start(bf16[256,2048]{1,0:T(8,128)(2,1)} %get-tuple-element.69), channel_id=1, source_target_pairs={{0,64},{32,96},{64,0},{96,32},{1,65},{33,97},{65,1},{97,33},{2,66}... | collective-permute-start | bytes 3145736 | tf_op jit(solution)/shard_map/ppermute | solution.py:640
  25.8 50.7 %collective-permute-start.8 = (bf16[256,2048]{1,0:T(8,128)(2,1)}, bf16[256,2048]{1,0:T(8,128)(2,1)}, u32[]{:S(2)}, u32[]{:S(2)}) collective-permute-start(bf16[256,2048]{1,0:T(8,128)(2,1)} %get-tuple-element.70), channel_id=1, source_target_pairs={{0,32},{32,64},{64,96},{96,0},{1,33},{33,65},{65,97},{97,1},{2,34}... | collective-permute-start | bytes 3145736 | tf_op jit(solution)/shard_map/ppermute | solution.py:640
  26.5 50.1 %collective-permute-start.9 = (bf16[256,2048]{1,0:T(8,128)(2,1)}, bf16[256,2048]{1,0:T(8,128)(2,1)}, u32[]{:S(2)}, u32[]{:S(2)}) collective-permute-start(bf16[256,2048]{1,0:T(8,128)(2,1)} %get-tuple-element.71), channel_id=1, source_target_pairs={{0,96},{32,0},{64,32},{96,64},{1,97},{33,1},{65,33},{97,65},{2,98}... | collective-permute-start | bytes 3145736 | tf_op jit(solution)/shard_map/ppermute | solution.py:640
  29.6 12.5 %copy-start.6 = (bf16[1088,256]{1,0:T(8,128)(2,1)}, bf16[1088,256]{1,0:T(8,128)(2,1)S(1)}, u32[]{:S(2)}) copy-start(bf16[1088,256]{1,0:T(8,128)(2,1)S(1)} %collective-permute-done.3.refs_2_) | copy-start | bytes 1671172
  29.7 26.4 %collective-permute-start.5 = (bf16[1088,256]{1,0:T(8,128)(2,1)S(1)}, bf16[1088,256]{1,0:T(8,128)(2,1)S(1)}, u32[]{:S(2)}, u32[]{:S(2)}) collective-permute-start(bf16[1088,256]{1,0:T(8,128)(2,1)S(1)} %collective-permute-done.3.refs_2_), channel_id=1, source_target_pairs={{0,4},{1,29},{4,8},{5,1},{8,12},{9,5},{12,16},{13,9},{16,20},{17,1... | collective-permute-start | bytes 1671176 | tf_op jit(solution)/shard_map/ppermute | solution.py:626
  34.2 7.9 %copy-start.3 = (bf16[256,512]{1,0:T(8,128)(2,1)}, bf16[256,512]{1,0:T(8,128)(2,1)S(1)}, u32[]{:S(2)}) copy-start(bf16[256,512]{1,0:T(8,128)(2,1)S(1)} %get-tuple-element.57.near) | copy-start | bytes 786436
  34.2 4.2 %collective-permute-start.4 = (bf16[256,512]{1,0:T(8,128)(2,1)S(1)}, bf16[256,512]{1,0:T(8,128)(2,1)}, u32[]{:S(2)}, u32[]{:S(2)}) collective-permute-start(bf16[256,512]{1,0:T(8,128)(2,1)S(1)} %get-tuple-element.57.near), channel_id=1, source_target_pairs={{0,1},{1,0},{2,3},{3,2},{4,5},{5,4},{6,7},{7,6},{8,9},{9,8},{10,11... | collective-permute-start | bytes 786440 | tf_op jit(solution)/shard_map/ppermute | solution.py:57
  34.3 21.7 %all-to-all-start = ((bf16[8,64,256]{2,1,0:T(8,128)(2,1)}), bf16[8,64,256]{2,1,0:T(8,128)(2,1)S(1)}, u32[]{:S(2)}, u32[]{:S(2)}) async-start(bf16[8,64,256]{2,1,0:T(8,128)(2,1)} %get-tuple-element.60.notes), calls=%async_computation | async-start | bytes 524288 | tf_op jit(solution)/shard_map/all_to_all | solution.py:656
  38.5 17.5 %collective-permute-start.6 = (bf16[544,256]{1,0:T(8,128)(2,1)S(1)}, bf16[544,256]{1,0:T(8,128)(2,1)S(1)}, u32[]{:S(2)}, u32[]{:S(2)}) collective-permute-start(bf16[544,256]{1,0:T(8,128)(2,1)S(1)} %slice.3), channel_id=1, source_target_pairs={{0,8},{1,25},{4,12},{5,29},{8,16},{9,1},{12,20},{13,5},{16,24},{17... | collective-permute-start | bytes 835592 | tf_op jit(solution)/shard_map/ppermute | solution.py:626
  56.0 0.8 copy-start.4
  56.0 0.7 copy-start.7
  56.0 0.9 copy-start.5
  57.0 33.1 %copy-start = (bf16[256,2048]{1,0:T(8,128)(2,1)S(1)}, bf16[256,2048]{1,0:T(8,128)(2,1)}, u32[]{:S(2)}) copy-start(bf16[256,2048]{1,0:T(8,128)(2,1)} %get-tuple-element.73.refs_4_) | copy-start | bytes 3145732
  66.7 12.7 %all-to-all-start.1 = ((bf16[4,272,256]{2,1,0:T(8,128)(2,1)}), bf16[4,272,256]{2,1,0:T(8,128)(2,1)S(1)}, u32[]{:S(2)}, u32[]{:S(2)}) async-start(bf16[4,272,256]{2,1,0:T(8,128)(2,1)} %far512.1), calls=%async_computation.1 | async-start | bytes 1114112 | tf_op jit(solution)/shard_map/all_to_all | solution.py:660
  79.4 0.9 copy-start.2
  80.9 8.0 %collective-permute-start.10 = (bf16[256,256]{1,0:T(8,128)(2,1)S(1)}, bf16[256,256]{1,0:T(8,128)(2,1)S(1)}, u32[]{:S(2)}, u32[]{:S(2)}) collective-permute-start(bf16[256,256]{1,0:T(8,128)(2,1)S(1)} %merge.1.refs_0_), channel_id=1, source_target_pairs={{0,64},{32,96},{64,0},{96,32},{1,65},{33,97},{65,1},{97,33},{2,66}... | collective-permute-start | bytes 393224 | tf_op jit(solution)/shard_map/ppermute | solution.py:666
  81.0 9.1 %collective-permute-start.11 = (bf16[256,256]{1,0:T(8,128)(2,1)S(1)}, bf16[256,256]{1,0:T(8,128)(2,1)S(1)}, u32[]{:S(2)}, u32[]{:S(2)}) collective-permute-start(bf16[256,256]{1,0:T(8,128)(2,1)S(1)} %merge.1.refs_0_), channel_id=1, source_target_pairs={{0,32},{32,64},{64,96},{96,0},{1,33},{33,65},{65,97},{97,1},{2,34}... | collective-permute-start | bytes 393224 | tf_op jit(solution)/shard_map/ppermute | solution.py:666
  81.8 8.3 %collective-permute-start.12 = (bf16[256,256]{1,0:T(8,128)(2,1)S(1)}, bf16[256,256]{1,0:T(8,128)(2,1)S(1)}, u32[]{:S(2)}, u32[]{:S(2)}) collective-permute-start(bf16[256,256]{1,0:T(8,128)(2,1)S(1)} %merge.1.refs_0_), channel_id=1, source_target_pairs={{0,96},{32,0},{64,32},{96,64},{1,97},{33,1},{65,33},{97,65},{2,98}... | collective-permute-start | bytes 393224 | tf_op jit(solution)/shard_map/ppermute | solution.py:666
  92.9 2.2 %collective-permute-start.13 = (bf16[256,1024]{1,0:T(8,128)(2,1)S(1)}, bf16[256,1024]{1,0:T(8,128)(2,1)S(1)}, u32[]{:S(2)}, u32[]{:S(2)}) collective-permute-start(bf16[256,1024]{1,0:T(8,128)(2,1)S(1)} %get-tuple-element.78), channel_id=1, source_target_pairs={{0,1},{1,0},{2,3},{3,2},{4,5},{5,4},{6,7},{7,6},{8,9},{9,8},{10,11... | collective-permute-start | bytes 1572872 | tf_op jit(solution)/shard_map/ppermute | solution.py:57
  95.3 5.6 %collective-permute-start.16 = (bf16[256,256]{1,0:T(8,128)(2,1)S(1)}, bf16[256,256]{1,0:T(8,128)(2,1)S(1)}, u32[]{:S(2)}, u32[]{:S(2)}) collective-permute-start(bf16[256,256]{1,0:T(8,128)(2,1)S(1)} %get-tuple-element.82), channel_id=1, source_target_pairs={{0,130},{2,0},{128,2},{130,128},{1,131},{3,1},{129,3},{131,129},{4... | collective-permute-start | bytes 393224 | tf_op jit(solution)/shard_map/ppermute | solution.py:671
  97.3 9.3 %collective-permute-start.15 = (bf16[256,256]{1,0:T(8,128)(2,1)S(1)}, bf16[256,256]{1,0:T(8,128)(2,1)S(1)}, u32[]{:S(2)}, u32[]{:S(2)}) collective-permute-start(bf16[256,256]{1,0:T(8,128)(2,1)S(1)} %get-tuple-element.81), channel_id=1, source_target_pairs={{0,2},{2,128},{128,130},{130,0},{1,3},{3,129},{129,131},{131,1},{4... | collective-permute-start | bytes 393224 | tf_op jit(solution)/shard_map/ppermute | solution.py:671
  97.4 9.1 %collective-permute-start.14 = (bf16[256,256]{1,0:T(8,128)(2,1)S(1)}, bf16[256,256]{1,0:T(8,128)(2,1)S(1)}, u32[]{:S(2)}, u32[]{:S(2)}) collective-permute-start(bf16[256,256]{1,0:T(8,128)(2,1)S(1)} %get-tuple-element.80), channel_id=1, source_target_pairs={{0,128},{2,130},{128,0},{130,2},{1,129},{3,131},{129,1},{131,3},{4... | collective-permute-start | bytes 393224 | tf_op jit(solution)/shard_map/ppermute | solution.py:671
